TPU v7x, 32 devices: a whole 2x2x4 slice. The times are simulated.
32 devices in a mesh: row: 4 (over z), col: 8 (over y, x, core).
Axes of the slice: x: 2, y: 2, z: 4, core: 2. Of those that a mesh axis runs over, the one named last changes fastest.
Arguments:
- fields: bfloat16 [512, 64, 1024], P(None, 'row', 'col'), may hold values from -6 to 6
- enc_mix: bfloat16 [8, 64, 64], replicated, may hold values from -0.5 to 0.5
- k_cycle: bfloat16 [512, 512], P('row', 'col'), may hold values from -0.09375 to 0.09375
- centre_mix: bfloat16 [8, 64, 64], P(None, 'row'), may hold values from -0.4375 to 0.4375
- dec_mix: bfloat16 [8, 64, 64], replicated, may hold values from -0.5 to 0.5
Outputs:
- decoded: bfloat16 [512, 64, 1024], P(None, 'row', 'col')
All inputs are finite; a program needn't handle non-finite values.
Results may differ from a plain program's by a relative error of at most 0.014.
Values may be sent and summed in bfloat16 or wider, within the bound.
No kernel may reach another device: no remote copies, remote signals or barrier semaphores. Data moves between devices by JAX's collectives and lax.ppermute only.
A program may use at most 128 MiB of HBM per device.

v0:
```python
import functools
import math

import jax
import jax.numpy as jnp
import numpy as np
from jax import lax
from jax.experimental import pallas as pl
from jax.experimental.pallas import tpu as pltpu
from jax.sharding import PartitionSpec as P

F32, BF16 = jnp.float32, jnp.bfloat16

COMPONENTS = ((0, 1, 4, 5), (2, 3, 6, 7))
TAPS = ((0, 1), (1, 1), (1, 0), (1, -1))


def place_of(component):
    return (component >> 1) & 1, (component & 1) + 2 * (component >> 2)


def spread_table():
    table = np.zeros((256, 256), np.float32)
    for b in range(4):
        for field in range(64):
            table[b * 64 + field, (field // 8) * 32 + b * 8 + field % 8] = 1.0
    return table


def order_table():
    table = np.zeros((512, 512), np.float32)
    for field in range(64):
        for component in range(8):
            group, b = place_of(component)
            table[field * 8 + component, group * 256 + (field // 8) * 32 + b * 8 + field % 8] = 1.0
    return table


def turn_signs(turn):
    signs = np.zeros((8, 8), np.int64)
    signs[0, 0] = 1
    signs[1, 1] = (-1) ** turn
    for frequency in range(1, 4):
        angle = 2.0 * math.pi * frequency * turn / 8.0
        cosine, sine = np.cos(angle), np.sin(angle)
        block = np.array([[cosine, -sine], [sine, cosine]])
        block[np.abs(block) < 0.1] = 0.0
        first = 2 * frequency
        signs[first : first + 2, first : first + 2] = np.sign(block)
    return signs


def turn_table(turn):
    signs = turn_signs(turn)
    table = np.zeros((2, 256, 256), np.float32)
    for group in range(2):
        for b_from in range(4):
            for b_to in range(4):
                sign = signs[COMPONENTS[group][b_to], COMPONENTS[group][b_from]]
                if sign:
                    for c in range(8):
                        for m in range(8):
                            table[group, c * 32 + b_from * 8 + m, c * 32 + b_to * 8 + m] = sign
    return table


def pool_table():
    table = np.zeros((64, 256), np.float32)
    for x in range(256):
        table[(x % 128) // 2, x] = 0.25
    return table


def dot(a, b):
    return jnp.dot(a, b, preferred_element_type=F32)


def dot_nt(a, b):
    return lax.dot_general(a, b, (((1,), (1,)), ((), ())), preferred_element_type=F32)


def mix_matrix(piece, spread, group):
    parts = [spread[b * 64 : (b + 1) * 64] for b in range(4)]
    if group == 0:
        rows = [dot(piece(0), parts[0]), dot(piece(1), parts[1])]
        u, v = 4, 5
    else:
        rows = [
            dot(piece(2), parts[0]) - dot(piece(3), parts[1]),
            dot(piece(3), parts[0]) + dot(piece(2), parts[1]),
        ]
        u, v = 6, 7
    rows += [
        dot(piece(u), parts[2]) - dot(piece(v), parts[3]),
        dot(piece(v), parts[2]) + dot(piece(u), parts[3]),
    ]
    chunks = [rows[b][c * 8 : (c + 1) * 8] for c in range(8) for b in range(4)]
    return jnp.concatenate(chunks, axis=0).astype(BF16)


def row_start(c, component):
    return ((c * 8) * 8 + component) * 16


def gather_rows(wide, y, group):
    chunks = [
        wide[pl.ds(row_start(c, COMPONENTS[group][b]) + y, 8, stride=128), :]
        for c in range(8)
        for b in range(4)
    ]
    return jnp.concatenate(chunks, axis=0)


def gates(values):
    trivial = values.reshape(8, 4, 8, values.shape[1])[:, 0]
    return jax.nn.sigmoid(trivial)


def gated(values, scale):
    split = values.reshape(8, 4, 8, values.shape[1])
    return (split * scale[:, None]).reshape(values.shape)


def encode_kernel(
    fields, weights, k_local, centre, spread, pool_t,
    encoded, pooled, pay_down, pay_up, pay_own,
    held, wide, sems, *, chunks,
):
    size = 512 // chunks
    copies = []
    for n in range(chunks):
        span = pl.ds(n * size, size)
        copies.append(pltpu.make_async_copy(fields.at[span], held.at[span], sems.at[n]))
        copies[-1].start()
    table = spread[...]
    mixes = [mix_matrix(lambda s: weights[s], table, group) for group in range(2)]
    rows_in, cols_in = k_local.shape
    own_rows = centre.shape[1]
    for j in range(rows_in // 16):
        pay_own[0:16, j * cols_in : (j + 1) * cols_in] = k_local[j * 16 : (j + 1) * 16, :]
    pay_own[16 : 16 + own_rows, :] = jnp.concatenate([centre[s] for s in range(8)], axis=1)
    for n in range(chunks):
        copies[n].wait()
        piece = held[n * size : (n + 1) * size].astype(F32)
        wide[n * size * 16 : (n + 1) * size * 16, :] = piece.reshape(size * 16, 128)

    def step(line, carry):
        result = []
        scale = None
        for group in range(2):
            x = jnp.concatenate(
                [gather_rows(wide, 2 * line, group), gather_rows(wide, 2 * line + 1, group)], axis=1
            )
            y = dot(mixes[group], x.astype(BF16))
            if group == 0:
                scale = gates(y)
            e = (x + gated(y, scale)).astype(BF16)
            encoded[line, group * 256 : (group + 1) * 256, :] = e
            result.append(e)
        mean = dot_nt(pool_t[...], jnp.concatenate(result, axis=0))
        pooled[line] = mean.astype(BF16)
        return carry

    lax.fori_loop(0, 8, step, 0)
    for target, line in ((pay_down, 7), (pay_up, 0)):
        target[0:64, :] = pooled[line]
        target[64:96, :] = pay_own[...]


def middle_kernel(*refs, rows, shape):
    rows_in, cols_in = shape
    pooled, own, above, below = refs[:4]
    others = refs[4 : 4 + rows - 3]
    order = refs[1 + rows]
    near, far, block, raw = refs[2 + rows :]
    row, col = lax.axis_index("row"), lax.axis_index("col")

    def put(source, start, index):
        for j in range(rows_in // 16):
            raw[index, j * 16 : (j + 1) * 16, :] = source[
                start : start + 16, j * cols_in : (j + 1) * cols_in
            ]

    put(own, 0, row)
    put(above, 64, lax.rem(row + rows - 1, rows))
    put(below, 64, lax.rem(row + 1, rows))
    for n, other in enumerate(others):
        put(other, 0, lax.rem(row + rows - 2 - n, rows))
    joined = jnp.concatenate([raw[r] for r in range(rows)], axis=1)
    sorted_block = dot(joined, order[...]).astype(BF16)
    block[...] = sorted_block
    top = above[0:64, :].astype(F32)
    bottom = below[0:64, :].astype(F32)
    top = jnp.where(row > 0, top, 0.0)
    bottom = jnp.where(row < rows - 1, bottom, 0.0)
    lines = [top] + [pooled[line].astype(F32) for line in range(8)] + [bottom]
    blank = jnp.zeros((6, 512), F32)
    left = jnp.concatenate([line[0:1] for line in lines] + [blank], axis=0)
    right = jnp.concatenate([line[63:64] for line in lines] + [blank], axis=0)
    even = lax.rem(col, 2) == 0
    near[0:rows_in, :] = sorted_block
    far[0:rows_in, :] = sorted_block
    near[rows_in : rows_in + 16, :] = jnp.where(even, right, left).astype(BF16)
    far[rows_in : rows_in + 16, :] = jnp.where(even, left, right).astype(BF16)


def pair_steps(cols):
    steps_even = list(range(4, cols, 2))
    steps_odd = steps_even[:-1] + [2]
    return list(zip(steps_even, steps_odd))


def final_kernel(*refs, rows, cols, shape, chunks):
    rows_in, _ = shape
    pairs = pair_steps(cols)
    refs = list(refs)
    pooled, encoded, weights, own, above, below = refs[:6]
    others = refs[6 : 6 + rows - 3]
    refs = refs[6 + rows - 3 :]
    block, near, far = refs[:3]
    near_pairs = refs[3 : 3 + len(pairs)]
    relayed = refs[3 + len(pairs)]
    relayed_pairs = refs[4 + len(pairs) : 4 + 2 * len(pairs)]
    refs = refs[4 + 2 * len(pairs) :]
    spread, turns, decoded = refs[:3]
    kt, turned, padded, left_of, right_of, middle, doubled, centre_rows, wide, out, sems = refs[3:]
    row, col = lax.axis_index("row"), lax.axis_index("col")
    even = lax.rem(col, 2) == 0
    mate = jnp.where(even, col + 1, col - 1)

    for line in range(8):
        padded[line + 1, 8:72, :] = pooled[line].astype(F32)
    padded[0, 8:72, :] = jnp.where(row > 0, above[0:64, :].astype(F32), 0.0)
    padded[9, 8:72, :] = jnp.where(row < rows - 1, below[0:64, :].astype(F32), 0.0)
    near_rim = near[rows_in : rows_in + 16, :].astype(F32)
    far_rim = far[rows_in : rows_in + 16, :].astype(F32)
    left_rim = jnp.where(even, far_rim, near_rim)
    right_rim = jnp.where(even, near_rim, far_rim)
    for line in range(10):
        padded[line, 7:8, :] = left_rim[line : line + 1]
        padded[line, 72:73, :] = right_rim[line : line + 1]

    for line in range(8):
        span = slice(line * 64, line * 64 + 64)
        for tap, (dy, dx) in enumerate(TAPS):
            ahead = padded[line + 1 + dy, 8 + dx : 72 + dx, :]
            behind = padded[line + 1 - dy, 8 - dx : 72 - dx, :]
            plus = (ahead + behind).astype(BF16)
            minus = (ahead - behind).astype(BF16)
            base = tap * 512
            left_of[span, base : base + 256] = plus[:, :256]
            left_of[span, base + 256 : base + 512] = minus[:, 256:]
            right_of[span, base : base + 256] = minus[:, :256]
            right_of[span, base + 256 : base + 512] = plus[:, 256:]

    def put(source, index):
        start = pl.multiple_of(lax.rem(index + 2 * cols, cols) * rows_in, rows_in)
        kt[pl.ds(start, rows_in), :] = source[0:rows_in, :]

    def away(index, step_even, step_odd):
        return index + jnp.where(lax.rem(index, 2) == 0, step_even, step_odd)

    put(block, col)
    put(near, mate)
    put(far, away(col, -1, 1))
    put(relayed, away(mate, -1, 1))
    for n, (step_even, step_odd) in enumerate(pairs):
        put(near_pairs[n], away(col, step_even, step_odd))
        put(relayed_pairs[n], away(mate, step_even, step_odd))

    root = math.sqrt(0.5)
    for tap in range(4):
        signs = turn_signs(tap)
        for group in range(2):
            whole = kt[:, group * 256 : (group + 1) * 256]
            result = whole.astype(F32) if tap == 0 else dot(whole, turns[tap - 1, group])
            turned[0:512, :] = result[:, 0:128]
            turned[512:1024, :] = result[:, 128:256]
            for source in range(2):
                scale = 1.0
                if tap % 2:
                    scale = (1.0, root, 0.5)[group + source]
                comps = COMPONENTS[source]
                for c in range(8):
                    read = {
                        comp: jnp.concatenate(
                            [
                                turned[pl.ds(half * 512 + c * 64 + comp, 8, stride=8), :]
                                for half in range(2)
                            ],
                            axis=1,
                        )
                        for comp in comps
                    }
                    parts = []
                    for comp in comps:
                        total = None
                        for other in comps:
                            sign = int(signs[comp, other])
                            if sign == 0:
                                continue
                            if total is None:
                                total = read[other] if sign > 0 else -read[other]
                            else:
                                total = total + read[other] if sign > 0 else total - read[other]
                        parts.append(total if scale == 1.0 else total * scale)
                    start = tap * 512 + source * 256 + c * 32
                    middle[group, start : start + 32, :] = jnp.concatenate(parts, axis=0).astype(BF16)

    own_rows = 64 // rows
    table = spread[...]

    def put_centre(source, start, index):
        place = pl.multiple_of(index * own_rows, own_rows)
        centre_rows[pl.ds(place, own_rows), :] = source[start : start + own_rows, :].astype(F32)

    put_centre(own, 16, row)
    put_centre(above, 80, lax.rem(row + rows - 1, rows))
    put_centre(below, 80, lax.rem(row + 1, rows))
    for n, other in enumerate(others):
        put_centre(other, 16, lax.rem(row + rows - 2 - n, rows))
    centre = centre_rows[...].astype(BF16)
    centres = [
        mix_matrix(lambda s: centre[:, s * 64 : (s + 1) * 64], table, group) for group in range(2)
    ]
    mixes = [mix_matrix(lambda s: weights[s], table, group) for group in range(2)]

    whole_pooled = jnp.concatenate([pooled[line] for line in range(8)], axis=0)
    totals = [
        dot(side[...], middle[group])
        + dot_nt(whole_pooled[:, group * 256 : (group + 1) * 256], centres[group])
        for group, side in enumerate((left_of, right_of))
    ]
    lane = lax.broadcasted_iota(jnp.int32, (512, 128), 1)
    first = (lane & 31) < 8
    scales = []
    for half in range(2):
        s = jnp.where(first, jax.nn.sigmoid(totals[0][:, half * 128 : half * 128 + 128]), 0.0)
        s = s + pltpu.roll(s, 8, 1)
        scales.append(s + pltpu.roll(s, 16, 1))
    scale = jnp.concatenate(scales + scales, axis=1)
    total = jnp.concatenate(totals, axis=1)
    bottleneck = (whole_pooled.astype(F32) + total * scale).astype(BF16).astype(F32)
    for line in range(8):
        padded[line, 0:64, :] = bottleneck[line * 64 : line * 64 + 64]

    def step(line, carry):
        coarse = padded[line, 0:64, :]
        for quarter in range(4):
            lanes = coarse[:, quarter * 128 : quarter * 128 + 128]
            doubled[pl.ds(quarter * 128, 64, stride=2), :] = lanes
            doubled[pl.ds(quarter * 128 + 1, 64, stride=2), :] = lanes
        fine = jnp.concatenate(
            [doubled[quarter * 128 : quarter * 128 + 128, :] for quarter in range(4)], axis=1
        ).astype(BF16)
        scale = None
        for group in range(2):
            span = slice(group * 256, (group + 1) * 256)
            low = dot_nt(mixes[group], fine[:, span])
            y = dot(mixes[group], encoded[line, span, :]) + jnp.concatenate([low, low], axis=1)
            if group == 0:
                scale = gates(y)
            d = gated(y, scale)
            for half in range(2):
                for c in range(8):
                    for b in range(4):
                        start = row_start(c, COMPONENTS[group][b]) + 2 * line + half
                        at = c * 32 + b * 8
                        wide[pl.ds(start, 8, stride=128), :] = d[
                            at : at + 8, half * 128 : half * 128 + 128
                        ]
        return carry

    lax.fori_loop(0, 8, step, 0)
    size = 512 // chunks
    copies = []
    for n in range(chunks):
        span = pl.ds(n * size, size)
        piece = wide[n * size * 16 : (n + 1) * size * 16, :].astype(BF16)
        out[n * size : (n + 1) * size] = piece.reshape(size, 16, 128)
        copies.append(pltpu.make_async_copy(out.at[span], decoded.at[span], sems.at[n]))
        copies[-1].start()
    for copy in copies:
        copy.wait()


VMEM = pl.BlockSpec(memory_space=pltpu.VMEM)
ANY = pl.BlockSpec(memory_space=pl.ANY)


def params(mebibytes):
    return pltpu.CompilerParams(vmem_limit_bytes=mebibytes * 1024 * 1024)


def per_device(fields, enc_mix, k_cycle, centre_mix, dec_mix):
    rows, cols = lax.axis_size("row"), lax.axis_size("col")
    k_local = k_cycle.T
    shape = k_local.shape
    spread = jnp.asarray(spread_table(), BF16)
    order = jnp.asarray(order_table(), BF16)
    pool_t = jnp.asarray(pool_table(), BF16)
    turns = jnp.asarray(np.stack([turn_table(t) for t in (1, 2, 3)]), BF16)
    arr = lambda *dims: jax.ShapeDtypeStruct(dims, BF16)
    chunks = 4
    encoded, pooled, pay_down, pay_up, pay_own = pl.pallas_call(
        functools.partial(encode_kernel, chunks=chunks),
        out_shape=(arr(8, 512, 256), arr(8, 64, 512), arr(96, 512), arr(96, 512), arr(32, 512)),
        in_specs=[ANY] + [VMEM] * 5,
        out_specs=(VMEM,) * 5,
        scratch_shapes=[
            pltpu.VMEM((512, 16, 128), BF16),
            pltpu.VMEM((8192, 128), F32),
            pltpu.SemaphoreType.DMA((chunks,)),
        ],
        compiler_params=params(40),
        name="encode",
    )(fields, enc_mix, k_local, centre_mix, spread, pool_t)

    def shift(array, step):
        return lax.ppermute(array, "row", [(i, (i + step) % rows) for i in range(rows)])

    above, below = shift(pay_down, 1), shift(pay_up, -1)
    others = [shift(pay_own, step) for step in range(2, rows - 1)]
    near_out, far_out, block = pl.pallas_call(
        functools.partial(middle_kernel, rows=rows, shape=shape),
        out_shape=(arr(shape[0] + 16, 512), arr(shape[0] + 16, 512), arr(shape[0], 512)),
        in_specs=[VMEM] * (2 + rows),
        out_specs=(VMEM,) * 3,
        scratch_shapes=[pltpu.VMEM((rows,) + shape, BF16)],
        compiler_params=params(16),
        name="middle",
    )(pooled, pay_own, above, below, *others, order)

    def mates(array):
        return lax.ppermute(array, "col", [(i, i ^ 1) for i in range(cols)])

    near = mates(near_out)
    far = lax.ppermute(
        far_out, "col", [(i, (i - 1 if i % 2 == 0 else i + 1) % cols) for i in range(cols)]
    )
    near_pairs = [
        lax.ppermute(
            block, "col", [((i + (even, odd)[i % 2]) % cols, i) for i in range(cols)]
        )
        for even, odd in pair_steps(cols)
    ]
    relayed = mates(far)
    relayed_pairs = [mates(array) for array in near_pairs]
    count = 6 + (rows - 3) + 4 + 2 * len(near_pairs) + 2
    return pl.pallas_call(
        functools.partial(final_kernel, rows=rows, cols=cols, shape=shape, chunks=chunks),
        out_shape=jax.ShapeDtypeStruct(fields.shape, BF16),
        in_specs=[VMEM] * count,
        out_specs=ANY,
        scratch_shapes=[
            pltpu.VMEM((512, 512), BF16),
            pltpu.VMEM((1024, 128), F32),
            pltpu.VMEM((10, 80, 512), F32),
            pltpu.VMEM((512, 2048), BF16),
            pltpu.VMEM((512, 2048), BF16),
            pltpu.VMEM((2, 2048, 256), BF16),
            pltpu.VMEM((512, 128), F32),
            pltpu.VMEM((64, 512), F32),
            pltpu.VMEM((8192, 128), F32),
            pltpu.VMEM((512, 16, 128), BF16),
            pltpu.SemaphoreType.DMA((chunks,)),
        ],
        compiler_params=params(48),
        name="final",
    )(
        pooled, encoded, dec_mix, pay_own, above, below, *others,
        block, near, far, *near_pairs, relayed, *relayed_pairs, spread, turns,
    )


def solution(mesh):
    return jax.shard_map(
        per_device,
        mesh=mesh,
        in_specs=(P(None, "row", "col"), P(), P("row", "col"), P(None, "row", None), P()),
        out_specs=P(None, "row", "col"),
        check_vma=False,
    )
```

profile of v0, /device:TPU:0, one launch (start us, length us, event | category | flops | bytes accessed | tf_op | source)
XLA Modules:
  0.0 42.3 jit_solution(6462776183033414950)
XLA Ops:
  0.0 0.0 copy-start
  0.0 1.6 %copy-done = bf16[512,16,128]{2,1,0:T(8,128)(2,1)S(1)} copy-done((bf16[512,16,128]{2,1,0:T(8,128)(2,1)S(1)}, bf16[512,16,128]{2,1,0:T(8,128)(2,1)}, u32[]{:S(2)}) %copy-start) | copy-done | bytes 2097176
  1.6 0.0 copy-start.2
  1.6 0.9 %copy-done.2 = bf16[256,256]{1,0:T(8,128)(2,1)S(1)} copy-done((bf16[256,256]{1,0:T(8,128)(2,1)S(1)}, bf16[256,256]{1,0:T(8,128)(2,1)}, u32[]{:S(2)}) %copy-start.2) | copy-done | bytes 131096
  2.5 0.0 copy-start.5
  2.5 0.9 %copy-done.5 = bf16[8,64,64]{2,1,0:T(8,128)(2,1)S(1)} copy-done((bf16[8,64,64]{2,1,0:T(8,128)(2,1)S(1)}, bf16[8,64,64]{2,1,0:T(8,128)(2,1)}, u32[]{:S(2)}) %copy-start.5) | copy-done | bytes 65560
  3.4 0.0 copy-start.7
  3.4 0.8 %copy-done.7 = bf16[8,16,64]{2,1,0:T(8,128)(2,1)S(1)} copy-done((bf16[8,16,64]{2,1,0:T(8,128)(2,1)S(1)}, bf16[8,16,64]{2,1,0:T(8,128)(2,1)}, u32[]{:S(2)}) %copy-start.7) | copy-done | bytes 16408
  4.2 0.0 copy-start.8
  4.2 0.8 %copy-done.8 = bf16[64,256]{1,0:T(8,128)(2,1)S(1)} copy-done((bf16[64,256]{1,0:T(8,128)(2,1)S(1)}, bf16[64,256]{1,0:T(8,128)(2,1)}, u32[]{:S(2)}) %copy-start.8) | copy-done | bytes 32792
  4.9 0.0 copy-start.9
  4.9 0.7 %copy-done.9 = bf16[128,64]{0,1:T(8,128)(2,1)S(1)} copy-done((bf16[128,64]{0,1:T(8,128)(2,1)S(1)}, bf16[128,64]{0,1:T(8,128)(2,1)}, u32[]{:S(2)}) %copy-start.9) | copy-done | bytes 16408
  5.6 0.0 copy-start.4
  5.6 0.0 copy-start.1
  5.6 0.0 copy-start.3
  5.6 0.0 copy-start.6
  5.6 6.0 %encode.1 = (bf16[8,512,256]{2,1,0:T(8,128)(2,1)S(1)}, bf16[8,64,512]{2,1,0:T(8,128)(2,1)S(1)}, bf16[96,512]{1,0:T(8,128)(2,1)S(1)}, bf16[96,512]{1,0:T(8,128)(2,1)S(1)}, bf16[32,512]{1,0:T(8,128)(2,1)S(1)}) custom-call(bf16[512,16,128]{2,1,0:T(8,128)(2,1)S(1)} %copy-done, bf16[8,64,64]{2,1,0:T(8,128)(2,1)S(1)} %copy-done.5, bf16[64,128]{1,0:T(8,128)(2,1)S(1)} %bitcast.1, ...), custom_call_target="tpu_custom_call" | custom-call | tf_op jit(solution)/shard_map/encode/pallas_call | solution.py:405
  11.6 3.1 %collective-permute-start = (bf16[96,512]{1,0:T(8,128)(2,1)S(1)}, bf16[96,512]{1,0:T(8,128)(2,1)S(1)}, u32[]{:S(2)}, u32[]{:S(2)}) collective-permute-start(bf16[96,512]{1,0:T(8,128)(2,1)S(1)} %get-tuple-element.16), channel_id=1, source_target_pairs={{0,8},{8,16},{16,24},{24,0},{1,9},{9,17},{17,25},{25,1},{2,10},{10... | collective-permute-start | bytes 294920 | tf_op jit(solution)/shard_map/ppermute | solution.py:420
  14.7 2.1 %collective-permute-start.1 = (bf16[96,512]{1,0:T(8,128)(2,1)S(1)}, bf16[96,512]{1,0:T(8,128)(2,1)S(1)}, u32[]{:S(2)}, u32[]{:S(2)}) collective-permute-start(bf16[96,512]{1,0:T(8,128)(2,1)S(1)} %get-tuple-element.17), channel_id=1, source_target_pairs={{0,24},{8,0},{16,8},{24,16},{1,25},{9,1},{17,9},{25,17},{2,26},{10... | collective-permute-start | bytes 294920 | tf_op jit(solution)/shard_map/ppermute | solution.py:420
  16.8 0.9 %collective-permute-start.2 = (bf16[32,512]{1,0:T(8,128)(2,1)S(1)}, bf16[32,512]{1,0:T(8,128)(2,1)S(1)}, u32[]{:S(2)}, u32[]{:S(2)}) collective-permute-start(bf16[32,512]{1,0:T(8,128)(2,1)S(1)} %get-tuple-element.15.refs_1_.refs_3_), channel_id=1, source_target_pairs={{0,16},{8,24},{16,0},{24,8},{1,17},{9,25},{17,1},{25,9},{2,18},{10... | collective-permute-start | bytes 98312 | tf_op jit(solution)/shard_map/ppermute | solution.py:420
  17.8 5.3 %collective-permute-done.2.refs_4_.refs_6_ = bf16[32,512]{1,0:T(8,128)(2,1)S(1)} collective-permute-done((bf16[32,512]{1,0:T(8,128)(2,1)S(1)}, bf16[32,512]{1,0:T(8,128)(2,1)S(1)}, u32[]{:S(2)}, u32[]{:S(2)}) %collective-permute-start.2) | collective-permute-done | bytes 32800 | tf_op jit(solution)/shard_map/ppermute | solution.py:420
  23.1 0.0 collective-permute-done.refs_2_.refs_4_
  23.1 0.0 collective-permute-done.1.refs_3_.refs_5_
  23.1 0.0 copy-done.4
  23.1 0.2 middle.1
  23.3 1.9 %collective-permute-start.4 = (bf16[80,512]{1,0:T(8,128)(2,1)S(1)}, bf16[80,512]{1,0:T(8,128)(2,1)S(1)}, u32[]{:S(2)}, u32[]{:S(2)}) collective-permute-start(bf16[80,512]{1,0:T(8,128)(2,1)S(1)} %get-tuple-element.20), channel_id=1, source_target_pairs={{0,7},{1,2},{2,1},{3,4},{4,3},{5,6},{6,5},{7,0},{8,15},{9,10},{10,... | collective-permute-start | bytes 245768 | tf_op jit(solution)/shard_map/ppermute | solution.py:438
  25.2 0.0 collective-permute-start.6
  25.2 1.2 %collective-permute-start.5 = (bf16[64,512]{1,0:T(8,128)(2,1)S(1)}, bf16[64,512]{1,0:T(8,128)(2,1)S(1)}, u32[]{:S(2)}, u32[]{:S(2)}) collective-permute-start(bf16[64,512]{1,0:T(8,128)(2,1)S(1)} %get-tuple-element.18.refs_7_), channel_id=1, source_target_pairs={{4,0},{5,1},{6,2},{7,3},{0,4},{1,5},{2,6},{3,7},{12,8},{13,9},{14,... | collective-permute-start | bytes 196616 | tf_op jit(solution)/shard_map/ppermute | solution.py:442
  26.4 0.9 %collective-permute-start.3 = (bf16[80,512]{1,0:T(8,128)(2,1)S(1)}, bf16[80,512]{1,0:T(8,128)(2,1)S(1)}, u32[]{:S(2)}, u32[]{:S(2)}) collective-permute-start(bf16[80,512]{1,0:T(8,128)(2,1)S(1)} %get-tuple-element.19), channel_id=1, source_target_pairs={{0,1},{1,0},{2,3},{3,2},{4,5},{5,4},{6,7},{7,6},{8,9},{9,8},{10,11... | collective-permute-start | bytes 245768 | tf_op jit(solution)/shard_map/ppermute | solution.py:435
  27.4 1.5 %collective-permute-done.4.refs_9_ = bf16[80,512]{1,0:T(8,128)(2,1)S(1)} collective-permute-done((bf16[80,512]{1,0:T(8,128)(2,1)S(1)}, bf16[80,512]{1,0:T(8,128)(2,1)S(1)}, u32[]{:S(2)}, u32[]{:S(2)}) %collective-permute-start.4) | collective-permute-done | bytes 81952 | tf_op jit(solution)/shard_map/ppermute | solution.py:438
  28.9 0.0 collective-permute-start.7
  28.9 1.6 %collective-permute-done.6.refs_11_ = bf16[64,512]{1,0:T(8,128)(2,1)S(1)} collective-permute-done((bf16[64,512]{1,0:T(8,128)(2,1)S(1)}, bf16[64,512]{1,0:T(8,128)(2,1)S(1)}, u32[]{:S(2)}, u32[]{:S(2)}) %collective-permute-start.6) | collective-permute-done | bytes 65568 | tf_op jit(solution)/shard_map/ppermute | solution.py:442
  30.5 0.0 collective-permute-start.9
  30.5 0.4 collective-permute-done.5.refs_10_
  30.9 0.1 collective-permute-start.8
  31.0 0.0 collective-permute-done.3.refs_8_
  31.0 0.7 %collective-permute-done.9.refs_14_ = bf16[64,512]{1,0:T(8,128)(2,1)S(1)} collective-permute-done((bf16[64,512]{1,0:T(8,128)(2,1)S(1)}, bf16[64,512]{1,0:T(8,128)(2,1)S(1)}, u32[]{:S(2)}, u32[]{:S(2)}) %collective-permute-start.9) | collective-permute-done | bytes 65568 | tf_op jit(solution)/shard_map/ppermute | solution.py:435
  31.8 0.4 collective-permute-done.8.refs_13_
  32.2 0.0 collective-permute-done.7.refs_12_
  32.2 0.0 copy-done.1
  32.2 0.0 copy-done.3
  32.2 0.0 copy-done.6
  32.2 10.1 %final.1 = bf16[512,16,128]{2,1,0:T(8,128)(2,1)} custom-call(bf16[8,64,512]{2,1,0:T(8,128)(2,1)S(1)} %get-tuple-element.13.refs_0_, bf16[8,512,256]{2,1,0:T(8,128)(2,1)S(1)} %get-tuple-element.14.refs_1_, bf16[8,64,64]{2,1,0:T(8,128)(2,1)S(1)} %copy-done.6, bf16[32,512]{1,0:T(8,128)(2,1)S(1)} %get-tuple-element.15.refs_1_.refs_3_, ...), custom_call_target="tpu_custom_call" | custom-call | tf_op jit(solution)/shard_map/final/pallas_call | solution.py:450
Async XLA Ops:
  0.0 1.6 %copy-start = (bf16[512,16,128]{2,1,0:T(8,128)(2,1)S(1)}, bf16[512,16,128]{2,1,0:T(8,128)(2,1)}, u32[]{:S(2)}) copy-start(bf16[512,16,128]{2,1,0:T(8,128)(2,1)} %fields.1) | copy-start | bytes 6291460
  1.6 0.9 %copy-start.2 = (bf16[256,256]{1,0:T(8,128)(2,1)S(1)}, bf16[256,256]{1,0:T(8,128)(2,1)}, u32[]{:S(2)}) copy-start(bf16[256,256]{1,0:T(8,128)(2,1)} %constant.8.clone.spread.refs_15_) | copy-start | bytes 393220
  2.5 0.9 %copy-start.5 = (bf16[8,64,64]{2,1,0:T(8,128)(2,1)S(1)}, bf16[8,64,64]{2,1,0:T(8,128)(2,1)}, u32[]{:S(2)}) copy-start(bf16[8,64,64]{2,1,0:T(8,128)(2,1)} %weights.1) | copy-start | bytes 196612
  3.4 0.8 %copy-start.7 = (bf16[8,16,64]{2,1,0:T(8,128)(2,1)S(1)}, bf16[8,16,64]{2,1,0:T(8,128)(2,1)}, u32[]{:S(2)}) copy-start(bf16[8,16,64]{2,1,0:T(8,128)(2,1)} %centre.1) | copy-start | bytes 49156
  4.2 0.8 %copy-start.8 = (bf16[64,256]{1,0:T(8,128)(2,1)S(1)}, bf16[64,256]{1,0:T(8,128)(2,1)}, u32[]{:S(2)}) copy-start(bf16[64,256]{1,0:T(8,128)(2,1)} %constant.10.clone.pool_t) | copy-start | bytes 98308
  4.9 0.7 %copy-start.9 = (bf16[128,64]{0,1:T(8,128)(2,1)S(1)}, bf16[128,64]{0,1:T(8,128)(2,1)}, u32[]{:S(2)}) copy-start(bf16[128,64]{0,1:T(8,128)(2,1)} %param.11) | copy-start | bytes 49156
  5.6 17.4 %copy-start.4 = (bf16[512,512]{1,0:T(8,128)(2,1)S(1)}, bf16[512,512]{1,0:T(8,128)(2,1)}, u32[]{:S(2)}) copy-start(bf16[512,512]{1,0:T(8,128)(2,1)} %constant.9.clone.refs_5_) | copy-start | bytes 1572868
  5.6 26.5 %copy-start.1 = (bf16[3,2,256,256]{3,2,1,0:T(8,128)(2,1)S(1)}, bf16[3,2,256,256]{3,2,1,0:T(8,128)(2,1)}, u32[]{:S(2)}) copy-start(bf16[3,2,256,256]{3,2,1,0:T(8,128)(2,1)} %constant.11.clone.refs_16_) | copy-start | bytes 2359300
  5.6 26.5 %copy-start.3 = (bf16[256,256]{1,0:T(8,128)(2,1)S(1)}, bf16[256,256]{1,0:T(8,128)(2,1)}, u32[]{:S(2)}) copy-start(bf16[256,256]{1,0:T(8,128)(2,1)} %constant.8.clone.spread.refs_15_) | copy-start | bytes 393220
  5.6 26.5 %copy-start.6 = (bf16[8,64,64]{2,1,0:T(8,128)(2,1)S(1)}, bf16[8,64,64]{2,1,0:T(8,128)(2,1)}, u32[]{:S(2)}) copy-start(bf16[8,64,64]{2,1,0:T(8,128)(2,1)} %refs_2_.1) | copy-start | bytes 196612
  11.6 11.4 %collective-permute-start = (bf16[96,512]{1,0:T(8,128)(2,1)S(1)}, bf16[96,512]{1,0:T(8,128)(2,1)S(1)}, u32[]{:S(2)}, u32[]{:S(2)}) collective-permute-start(bf16[96,512]{1,0:T(8,128)(2,1)S(1)} %get-tuple-element.16), channel_id=1, source_target_pairs={{0,8},{8,16},{16,24},{24,0},{1,9},{9,17},{17,25},{25,1},{2,10},{10... | collective-permute-start | bytes 294920 | tf_op jit(solution)/shard_map/ppermute | solution.py:420
  14.7 8.3 %collective-permute-start.1 = (bf16[96,512]{1,0:T(8,128)(2,1)S(1)}, bf16[96,512]{1,0:T(8,128)(2,1)S(1)}, u32[]{:S(2)}, u32[]{:S(2)}) collective-permute-start(bf16[96,512]{1,0:T(8,128)(2,1)S(1)} %get-tuple-element.17), channel_id=1, source_target_pairs={{0,24},{8,0},{16,8},{24,16},{1,25},{9,1},{17,9},{25,17},{2,26},{10... | collective-permute-start | bytes 294920 | tf_op jit(solution)/shard_map/ppermute | solution.py:420
  16.8 6.2 %collective-permute-start.2 = (bf16[32,512]{1,0:T(8,128)(2,1)S(1)}, bf16[32,512]{1,0:T(8,128)(2,1)S(1)}, u32[]{:S(2)}, u32[]{:S(2)}) collective-permute-start(bf16[32,512]{1,0:T(8,128)(2,1)S(1)} %get-tuple-element.15.refs_1_.refs_3_), channel_id=1, source_target_pairs={{0,16},{8,24},{16,0},{24,8},{1,17},{9,25},{17,1},{25,9},{2,18},{10... | collective-permute-start | bytes 98312 | tf_op jit(solution)/shard_map/ppermute | solution.py:420
  23.3 5.6 %collective-permute-start.4 = (bf16[80,512]{1,0:T(8,128)(2,1)S(1)}, bf16[80,512]{1,0:T(8,128)(2,1)S(1)}, u32[]{:S(2)}, u32[]{:S(2)}) collective-permute-start(bf16[80,512]{1,0:T(8,128)(2,1)S(1)} %get-tuple-element.20), channel_id=1, source_target_pairs={{0,7},{1,2},{2,1},{3,4},{4,3},{5,6},{6,5},{7,0},{8,15},{9,10},{10,... | collective-permute-start | bytes 245768 | tf_op jit(solution)/shard_map/ppermute | solution.py:438
  25.2 5.3 %collective-permute-start.6 = (bf16[64,512]{1,0:T(8,128)(2,1)S(1)}, bf16[64,512]{1,0:T(8,128)(2,1)S(1)}, u32[]{:S(2)}, u32[]{:S(2)}) collective-permute-start(bf16[64,512]{1,0:T(8,128)(2,1)S(1)} %get-tuple-element.18.refs_7_), channel_id=1, source_target_pairs={{6,0},{3,1},{0,2},{5,3},{2,4},{7,5},{4,6},{1,7},{14,8},{11,9},{8,1... | collective-permute-start | bytes 196616 | tf_op jit(solution)/shard_map/ppermute | solution.py:442
  25.2 5.7 %collective-permute-start.5 = (bf16[64,512]{1,0:T(8,128)(2,1)S(1)}, bf16[64,512]{1,0:T(8,128)(2,1)S(1)}, u32[]{:S(2)}, u32[]{:S(2)}) collective-permute-start(bf16[64,512]{1,0:T(8,128)(2,1)S(1)} %get-tuple-element.18.refs_7_), channel_id=1, source_target_pairs={{4,0},{5,1},{6,2},{7,3},{0,4},{1,5},{2,6},{3,7},{12,8},{13,9},{14,... | collective-permute-start | bytes 196616 | tf_op jit(solution)/shard_map/ppermute | solution.py:442
  26.4 4.6 %collective-permute-start.3 = (bf16[80,512]{1,0:T(8,128)(2,1)S(1)}, bf16[80,512]{1,0:T(8,128)(2,1)S(1)}, u32[]{:S(2)}, u32[]{:S(2)}) collective-permute-start(bf16[80,512]{1,0:T(8,128)(2,1)S(1)} %get-tuple-element.19), channel_id=1, source_target_pairs={{0,1},{1,0},{2,3},{3,2},{4,5},{5,4},{6,7},{7,6},{8,9},{9,8},{10,11... | collective-permute-start | bytes 245768 | tf_op jit(solution)/shard_map/ppermute | solution.py:435
  28.9 3.3 %collective-permute-start.7 = (bf16[80,512]{1,0:T(8,128)(2,1)S(1)}, bf16[80,512]{1,0:T(8,128)(2,1)S(1)}, u32[]{:S(2)}, u32[]{:S(2)}) collective-permute-start(bf16[80,512]{1,0:T(8,128)(2,1)S(1)} %collective-permute-done.4.refs_9_), channel_id=1, source_target_pairs={{0,1},{1,0},{2,3},{3,2},{4,5},{5,4},{6,7},{7,6},{8,9},{9,8},{10,11... | collective-permute-start | bytes 245768 | tf_op jit(solution)/shard_map/ppermute | solution.py:435
  30.5 1.3 %collective-permute-start.9 = (bf16[64,512]{1,0:T(8,128)(2,1)S(1)}, bf16[64,512]{1,0:T(8,128)(2,1)S(1)}, u32[]{:S(2)}, u32[]{:S(2)}) collective-permute-start(bf16[64,512]{1,0:T(8,128)(2,1)S(1)} %collective-permute-done.6.refs_11_), channel_id=1, source_target_pairs={{0,1},{1,0},{2,3},{3,2},{4,5},{5,4},{6,7},{7,6},{8,9},{9,8},{10,11... | collective-permute-start | bytes 196616 | tf_op jit(solution)/shard_map/ppermute | solution.py:435
  30.9 1.3 %collective-permute-start.8 = (bf16[64,512]{1,0:T(8,128)(2,1)S(1)}, bf16[64,512]{1,0:T(8,128)(2,1)S(1)}, u32[]{:S(2)}, u32[]{:S(2)}) collective-permute-start(bf16[64,512]{1,0:T(8,128)(2,1)S(1)} %collective-permute-done.5.refs_10_), channel_id=1, source_target_pairs={{0,1},{1,0},{2,3},{3,2},{4,5},{5,4},{6,7},{7,6},{8,9},{9,8},{10,11... | collective-permute-start | bytes 196616 | tf_op jit(solution)/shard_map/ppermute | solution.py:435
where the time goes:
time: 42.7 us; the launch traced here: 42.3 us
  Pallas kernels  16.3 us (38%)
  starting transfers between devices  10.3 us (24%)
  waiting for transfers between devices  10 us (23%)
  local copies, waits for them, and re-layouts  5.64 us (13%)
    pallas_call x1, Pallas kernels, per_device(): pl.pallas_call(functools.partial(final_kernel, rows=rows, cols=cols, shap...  10.1 us
    ppermute x3, starting transfers between devices, shift(): lax.ppermute(array, 'row', [(i, (i + step) % rows) for i in range(rows)])  6.11 us
    pallas_call x1, Pallas kernels, per_device(): pl.pallas_call(functools.partial(encode_kernel, chunks=chunks), out_shape...  5.98 us
    unnamed x20, local copies, waits for them, and re-layouts  5.64 us
    ppermute x3, waiting for transfers between devices, shift(): lax.ppermute(array, 'row', [(i, (i + step) % rows) for i in range(rows)])  5.31 us
    ppermute x2, waiting for transfers between devices, per_device(): lax.ppermute(block, 'col', [((i + (even, odd)[i % 2]) % cols, i) for i in...  2.01 us
    ppermute x1, starting transfers between devices, per_device(): lax.ppermute(far_out, 'col', [(i, (i - 1 if i % 2 == 0 else i + 1) % cols...  1.94 us
    ppermute x1, waiting for transfers between devices, per_device(): lax.ppermute(far_out, 'col', [(i, (i - 1 if i % 2 == 0 else i + 1) % cols...  1.54 us
  transfers between devices with their start and end apart: 10, of which 6 were waited for; matrix products, arithmetic and copies ran while one was open for 0% of the time, Pallas kernels for 0%

commit v1 on v0

v1 whole, which is shorter than its diff:
```python
import functools
import math

import jax
import jax.numpy as jnp
import numpy as np
from jax import lax
from jax.experimental import pallas as pl
from jax.experimental.pallas import tpu as pltpu
from jax.sharding import PartitionSpec as P

F32, BF16 = jnp.float32, jnp.bfloat16

COMPONENTS = ((0, 1, 4, 5), (2, 3, 6, 7))
TAPS = ((0, 1), (1, 1), (1, 0), (1, -1))


def turn_signs(turn):
    signs = np.zeros((8, 8), np.int64)
    signs[0, 0] = 1
    signs[1, 1] = (-1) ** turn
    for frequency in range(1, 4):
        angle = 2.0 * math.pi * frequency * turn / 8.0
        cosine, sine = np.cos(angle), np.sin(angle)
        block = np.array([[cosine, -sine], [sine, cosine]])
        block[np.abs(block) < 0.1] = 0.0
        first = 2 * frequency
        signs[first : first + 2, first : first + 2] = np.sign(block)
    return signs


def turn_table(turn):
    signs = turn_signs(turn)
    table = np.zeros((2, 256, 256), np.float32)
    for group in range(2):
        for b_from in range(4):
            for b_to in range(4):
                sign = signs[COMPONENTS[group][b_to], COMPONENTS[group][b_from]]
                if sign:
                    for c in range(8):
                        for m in range(8):
                            table[group, c * 32 + b_from * 8 + m, c * 32 + b_to * 8 + m] = sign
    return table


def iota(shape, dim):
    return lax.broadcasted_iota(jnp.int32, shape, dim)


def spread_table():
    r, s = iota((256, 256), 0), iota((256, 256), 1)
    target = ((r & 63) >> 3) * 32 + (r >> 6) * 8 + (r & 7)
    return jnp.where(s == target, 1.0, 0.0).astype(BF16)


def order_table():
    r, s = iota((512, 512), 0), iota((512, 512), 1)
    field, component = r >> 3, r & 7
    group, b = (component >> 1) & 1, (component & 1) + 2 * (component >> 2)
    target = group * 256 + (field >> 3) * 32 + b * 8 + (field & 7)
    return jnp.where(s == target, 1.0, 0.0).astype(BF16)


def pool_table():
    x, column = iota((64, 256), 1), iota((64, 256), 0)
    return jnp.where(((x & 127) >> 1) == column, 0.25, 0.0).astype(BF16)


def dot(a, b):
    return jnp.dot(a, b, preferred_element_type=F32)


def dot_nt(a, b):
    return lax.dot_general(a, b, (((1,), (1,)), ((), ())), preferred_element_type=F32)


def mix_matrix(piece, spread, group):
    parts = [spread[b * 64 : (b + 1) * 64] for b in range(4)]
    if group == 0:
        rows = [dot(piece(0), parts[0]), dot(piece(1), parts[1])]
        u, v = 4, 5
    else:
        rows = [
            dot(piece(2), parts[0]) - dot(piece(3), parts[1]),
            dot(piece(3), parts[0]) + dot(piece(2), parts[1]),
        ]
        u, v = 6, 7
    rows += [
        dot(piece(u), parts[2]) - dot(piece(v), parts[3]),
        dot(piece(v), parts[2]) + dot(piece(u), parts[3]),
    ]
    chunks = [rows[b][c * 8 : (c + 1) * 8] for c in range(8) for b in range(4)]
    return jnp.concatenate(chunks, axis=0).astype(BF16)


def row_start(c, component):
    return ((c * 8) * 8 + component) * 16


def gather_rows(wide, y, group):
    chunks = [
        wide[pl.ds(row_start(c, COMPONENTS[group][b]) + y, 8, stride=128), :]
        for c in range(8)
        for b in range(4)
    ]
    return jnp.concatenate(chunks, axis=0)


def gates(values):
    trivial = values.reshape(8, 4, 8, values.shape[1])[:, 0]
    return jax.nn.sigmoid(trivial)


def gated(values, scale):
    split = values.reshape(8, 4, 8, values.shape[1])
    return (split * scale[:, None]).reshape(values.shape)


def encode_line(wide, line, mixes, pool_t):
    result = []
    scale = None
    for group in range(2):
        x = jnp.concatenate(
            [gather_rows(wide, 2 * line, group), gather_rows(wide, 2 * line + 1, group)], axis=1
        )
        y = dot(mixes[group], x.astype(BF16))
        if group == 0:
            scale = gates(y)
        result.append((x + gated(y, scale)).astype(BF16))
    mean = dot_nt(pool_t, jnp.concatenate(result, axis=0))
    return result, mean.astype(BF16)


def edge_kernel(
    fields_in, weights_in, k_in, centre_in,
    wide, encoded, pooled, pay_down, pay_up, pay_own, mixes_out,
    held, weights, k_local, centre, sems, small, *, chunks,
):
    starts = []
    for n, (source, target) in enumerate(
        ((weights_in, weights), (k_in, k_local), (centre_in, centre))
    ):
        starts.append(pltpu.make_async_copy(source, target, small.at[n]))
        starts[-1].start()
    size = 512 // chunks
    copies = []
    for n in range(chunks):
        span = pl.ds(n * size, size)
        copies.append(pltpu.make_async_copy(fields_in.at[span], held.at[span], sems.at[n]))
        copies[-1].start()
    table = spread_table()
    pool_t = pool_table()
    for start in starts:
        start.wait()
    mixes = [mix_matrix(lambda s: weights[s], table, group) for group in range(2)]
    for group in range(2):
        mixes_out[group] = mixes[group]
    rows_in, cols_in = k_local.shape
    own_rows = centre.shape[1]
    for j in range(rows_in // 16):
        pay_own[0:16, j * cols_in : (j + 1) * cols_in] = k_local[j * 16 : (j + 1) * 16, :]
    pay_own[16 : 16 + own_rows, :] = jnp.concatenate([centre[s] for s in range(8)], axis=1)
    for n in range(chunks):
        copies[n].wait()
        piece = held[n * size : (n + 1) * size].astype(F32)
        wide[n * size * 16 : (n + 1) * size * 16, :] = piece.reshape(size * 16, 128)
    for n, (target, line) in enumerate(((pay_up, 0), (pay_down, 7))):
        result, mean = encode_line(wide, line, mixes, pool_t)
        encoded[n, 0:256, :] = result[0]
        encoded[n, 256:512, :] = result[1]
        pooled[n] = mean
        target[0:64, :] = mean
        target[64:96, :] = pay_own[...]


def inner_kernel(wide, edges, mixes_in, weights, pooled, halves, mixes_out):
    table = spread_table()
    pool_t = pool_table()
    mixes = [mixes_in[group] for group in range(2)]
    ends = [mix_matrix(lambda s: weights[s], table, group) for group in range(2)]
    for group in range(2):
        mixes_out[group] = ends[group]

    def step(n, carry):
        result, mean = encode_line(wide, n + 1, mixes, pool_t)
        pooled[n] = mean
        for group in range(2):
            halves[n + 1, group * 256 : (group + 1) * 256, :] = dot(ends[group], result[group])
        return carry

    lax.fori_loop(0, 6, step, 0, unroll=UNROLL)
    for n, line in enumerate((0, 7)):
        for group in range(2):
            span = slice(group * 256, (group + 1) * 256)
            halves[line, span, :] = dot(ends[group], edges[n, span, :])


def rims_kernel(*refs, rows, shape):
    rows_in, cols_in = shape
    ends, inner, own, above, below = refs[:5]
    others = refs[5 : 5 + rows - 3]
    near, far, block, raw = refs[2 + rows :]
    row, col = lax.axis_index("row"), lax.axis_index("col")

    def put(source, start, index):
        for j in range(rows_in // 16):
            raw[index, j * 16 : (j + 1) * 16, :] = source[
                start : start + 16, j * cols_in : (j + 1) * cols_in
            ]

    put(own, 0, row)
    put(above, 64, lax.rem(row + rows - 1, rows))
    put(below, 64, lax.rem(row + 1, rows))
    for n, other in enumerate(others):
        put(other, 0, lax.rem(row + rows - 2 - n, rows))
    joined = jnp.concatenate([raw[r] for r in range(rows)], axis=1)
    sorted_block = dot(joined, order_table()).astype(BF16)
    block[...] = sorted_block
    lines = all_lines(ends, inner, above, below, row, rows)
    blank = jnp.zeros((6, 512), F32)
    left = jnp.concatenate([line[0:1] for line in lines] + [blank], axis=0)
    right = jnp.concatenate([line[63:64] for line in lines] + [blank], axis=0)
    even = lax.rem(col, 2) == 0
    near[0:rows_in, :] = sorted_block
    far[0:rows_in, :] = sorted_block
    near[rows_in : rows_in + 16, :] = jnp.where(even, right, left).astype(BF16)
    far[rows_in : rows_in + 16, :] = jnp.where(even, left, right).astype(BF16)


def own_lines(ends, inner):
    return [ends[0]] + [inner[line] for line in range(6)] + [ends[1]]


def all_lines(ends, inner, above, below, row, rows):
    top = jnp.where(row > 0, above[0:64, :].astype(F32), 0.0)
    bottom = jnp.where(row < rows - 1, below[0:64, :].astype(F32), 0.0)
    return [top] + [line.astype(F32) for line in own_lines(ends, inner)] + [bottom]


def taps_kernel(*refs, rows):
    ends, inner, own, above, below = refs[:5]
    others = refs[5 : 5 + rows - 3]
    left_of, right_of, middle, padded, centre_rows = refs[2 + rows :]
    row = lax.axis_index("row")
    zero = jnp.zeros((1, 512), F32)
    for line, values in enumerate(all_lines(ends, inner, above, below, row, rows)):
        padded[line, 8:72, :] = values
        padded[line, 7:8, :] = zero
        padded[line, 72:73, :] = zero
    for line in range(8):
        span = slice(line * 64, line * 64 + 64)
        for tap, (dy, dx) in enumerate(TAPS):
            ahead = padded[line + 1 + dy, 8 + dx : 72 + dx, :]
            behind = padded[line + 1 - dy, 8 - dx : 72 - dx, :]
            plus = (ahead + behind).astype(BF16)
            minus = (ahead - behind).astype(BF16)
            base = tap * 512
            left_of[span, base : base + 256] = plus[:, :256]
            left_of[span, base + 256 : base + 512] = minus[:, 256:]
            right_of[span, base : base + 256] = minus[:, :256]
            right_of[span, base + 256 : base + 512] = plus[:, 256:]

    own_rows = 64 // rows
    table = spread_table()

    def put_centre(source, start, index):
        place = pl.multiple_of(index * own_rows, own_rows)
        centre_rows[pl.ds(place, own_rows), :] = source[start : start + own_rows, :].astype(F32)

    put_centre(own, 16, row)
    put_centre(above, 80, lax.rem(row + rows - 1, rows))
    put_centre(below, 80, lax.rem(row + 1, rows))
    for n, other in enumerate(others):
        put_centre(other, 16, lax.rem(row + rows - 2 - n, rows))
    centre = centre_rows[...].astype(BF16)
    whole = jnp.concatenate(own_lines(ends, inner), axis=0)
    for group in range(2):
        span = slice(group * 256, (group + 1) * 256)
        matrix = mix_matrix(lambda s: centre[:, s * 64 : (s + 1) * 64], table, group)
        middle[:, span] = dot_nt(whole[:, span], matrix)


def pair_steps(cols):
    steps_even = list(range(4, cols, 2))
    steps_odd = steps_even[:-1] + [2]
    return list(zip(steps_even, steps_odd))


def rim_rows(left_rim, right_rim, group):
    parts = []
    for dy, dx in TAPS:
        if dx == 0:
            parts += [jnp.zeros((16, 512), F32)]
            continue
        first = left_rim[1 - dx * dy : 9 - dx * dy]
        last = right_rim[1 + dx * dy : 9 + dx * dy]
        plus = jnp.concatenate([first, last], axis=0)
        minus = jnp.concatenate([first * float(-dx), last * float(dx)], axis=0)
        pair = (plus, minus) if group == 0 else (minus, plus)
        parts += [pair[0][:, :256], pair[1][:, 256:]]
    return jnp.concatenate(parts, axis=1).astype(BF16)


def final_kernel(*refs, rows, cols, shape, chunks):
    rows_in, _ = shape
    pairs = pair_steps(cols)
    ends, inner, halves, mixes, left_of, right_of, centre = refs[:7]
    block, near, far = refs[7:10]
    near_pairs = refs[10 : 10 + len(pairs)]
    relayed = refs[10 + len(pairs)]
    relayed_pairs = refs[11 + len(pairs) : 11 + 2 * len(pairs)]
    refs = refs[11 + 2 * len(pairs) :]
    turns, decoded = refs[:2]
    kt, turned, middle, coarse, doubled, wide, out, sems = refs[2:]
    col = lax.axis_index("col")
    even = lax.rem(col, 2) == 0
    mate = jnp.where(even, col + 1, col - 1)

    def put(source, index):
        start = pl.multiple_of(lax.rem(index + 2 * cols, cols) * rows_in, rows_in)
        kt[pl.ds(start, rows_in), :] = source[0:rows_in, :]

    def away(index, step_even, step_odd):
        return index + jnp.where(lax.rem(index, 2) == 0, step_even, step_odd)

    put(block, col)
    put(near, mate)
    put(far, away(col, -1, 1))
    put(relayed, away(mate, -1, 1))
    for n, (step_even, step_odd) in enumerate(pairs):
        put(near_pairs[n], away(col, step_even, step_odd))
        put(relayed_pairs[n], away(mate, step_even, step_odd))

    root = math.sqrt(0.5)
    for tap in range(4):
        signs = turn_signs(tap)
        for group in range(2):
            whole = kt[:, group * 256 : (group + 1) * 256]
            result = whole.astype(F32) if tap == 0 else dot(whole, turns[tap - 1, group])
            base = ((tap * 2 + group) % 2) * 1024
            turned[base : base + 512, :] = result[:, 0:128]
            turned[base + 512 : base + 1024, :] = result[:, 128:256]
            for source in range(2):
                scale = 1.0
                if tap % 2:
                    scale = (1.0, root, 0.5)[group + source]
                comps = COMPONENTS[source]
                for c in range(8):
                    read = {
                        comp: jnp.concatenate(
                            [
                                turned[pl.ds(base + half * 512 + c * 64 + comp, 8, stride=8), :]
                                for half in range(2)
                            ],
                            axis=1,
                        )
                        for comp in comps
                    }
                    parts = []
                    for comp in comps:
                        total = None
                        for other in comps:
                            sign = int(signs[comp, other])
                            if sign == 0:
                                continue
                            if total is None:
                                total = read[other] if sign > 0 else -read[other]
                            else:
                                total = total + read[other] if sign > 0 else total - read[other]
                        parts.append(total if scale == 1.0 else total * scale)
                    start = tap * 512 + source * 256 + c * 32
                    middle[group, start : start + 32, :] = jnp.concatenate(parts, axis=0).astype(BF16)

    near_rim = near[rows_in : rows_in + 16, :].astype(F32)
    far_rim = far[rows_in : rows_in + 16, :].astype(F32)
    left_rim = jnp.where(even, far_rim, near_rim)
    right_rim = jnp.where(even, near_rim, far_rim)
    totals = []
    sub = iota((8, 8, 256), 1)
    for group, side in enumerate((left_of, right_of)):
        rows_of = jnp.concatenate([side[...], rim_rows(left_rim, right_rim, group)], axis=0)
        total = dot(rows_of, middle[group])
        extra = total[512:528]
        total = total[0:512] + centre[:, group * 256 : (group + 1) * 256]
        total = total.reshape(8, 8, 8, 256)
        first = total[:, 0] + jnp.where(sub == 0, extra[0:8][:, None, :], 0.0)
        last = total[:, 7] + jnp.where(sub == 7, extra[8:16][:, None, :], 0.0)
        total = jnp.concatenate([first[:, None], total[:, 1:7], last[:, None]], axis=1)
        totals.append(total.reshape(512, 256))
    lane = iota((512, 128), 1)
    is_first = (lane & 31) < 8
    scales = []
    for half in range(2):
        s = jnp.where(is_first, jax.nn.sigmoid(totals[0][:, half * 128 : half * 128 + 128]), 0.0)
        s = s + pltpu.roll(s, 8, 1)
        scales.append(s + pltpu.roll(s, 16, 1))
    scale = jnp.concatenate(scales + scales, axis=1)
    total = jnp.concatenate(totals, axis=1)
    own = jnp.concatenate(own_lines(ends, inner), axis=0).astype(F32)
    coarse[...] = (own + total * scale).astype(BF16).astype(F32).reshape(8, 64, 512)
    matrices = [mixes[group] for group in range(2)]

    def step(line, carry):
        values = coarse[line]
        for quarter in range(4):
            lanes = values[:, quarter * 128 : quarter * 128 + 128]
            doubled[line, pl.ds(quarter * 128, 64, stride=2), :] = lanes
            doubled[line, pl.ds(quarter * 128 + 1, 64, stride=2), :] = lanes
        fine = jnp.concatenate(
            [doubled[line, quarter * 128 : quarter * 128 + 128, :] for quarter in range(4)], axis=1
        ).astype(BF16)
        scale = None
        for group in range(2):
            span = slice(group * 256, (group + 1) * 256)
            low = dot_nt(matrices[group], fine[:, span])
            y = halves[line, span, :] + jnp.concatenate([low, low], axis=1)
            if group == 0:
                scale = gates(y)
            d = gated(y, scale)
            for half in range(2):
                for c in range(8):
                    for b in range(4):
                        start = row_start(c, COMPONENTS[group][b]) + 2 * line + half
                        at = c * 32 + b * 8
                        wide[pl.ds(start, 8, stride=128), :] = d[
                            at : at + 8, half * 128 : half * 128 + 128
                        ]
        return carry

    lax.fori_loop(0, 8, step, 0, unroll=UNROLL)
    size = 512 // chunks
    copies = []
    for n in range(chunks):
        span = pl.ds(n * size, size)
        piece = wide[n * size * 16 : (n + 1) * size * 16, :].astype(BF16)
        out[n * size : (n + 1) * size] = piece.reshape(size, 16, 128)
        copies.append(pltpu.make_async_copy(out.at[span], decoded.at[span], sems.at[n]))
        copies[-1].start()
    for copy in copies:
        copy.wait()


VMEM = pl.BlockSpec(memory_space=pltpu.VMEM)
HBM = pl.BlockSpec(memory_space=pltpu.HBM)
UNROLL = 2


def call(kernel, name, ins, outs, shapes, scratch, mebibytes):
    return pl.pallas_call(
        kernel,
        out_shape=shapes,
        in_specs=ins,
        out_specs=outs,
        scratch_shapes=scratch,
        compiler_params=pltpu.CompilerParams(vmem_limit_bytes=mebibytes * 1024 * 1024),
        name=name,
    )


def arr(*dims, dtype=BF16):
    return jax.ShapeDtypeStruct(dims, dtype)


def per_device(fields, enc_mix, k_cycle, centre_mix, dec_mix):
    rows, cols = lax.axis_size("row"), lax.axis_size("col")
    k_local = k_cycle.T
    shape = k_local.shape
    turns = jnp.asarray(np.stack([turn_table(t) for t in (1, 2, 3)]), BF16)
    chunks = 4
    wide, edges, ends, pay_down, pay_up, pay_own, mixes = call(
        functools.partial(edge_kernel, chunks=chunks),
        "edges",
        [HBM] * 4,
        (VMEM,) * 7,
        (
            arr(8192, 128, dtype=F32), arr(2, 512, 256), arr(2, 64, 512),
            arr(96, 512), arr(96, 512), arr(32, 512), arr(2, 256, 256),
        ),
        [
            pltpu.VMEM((512, 16, 128), BF16),
            pltpu.VMEM(enc_mix.shape, BF16),
            pltpu.VMEM(shape, BF16),
            pltpu.VMEM(centre_mix.shape, BF16),
            pltpu.SemaphoreType.DMA((chunks,)),
            pltpu.SemaphoreType.DMA((3,)),
        ],
        24,
    )(*[pltpu.with_memory_space_constraint(x, pltpu.HBM) for x in (fields, enc_mix, k_local, centre_mix)])

    def shift(array, step):
        return lax.ppermute(array, "row", [(i, (i + step) % rows) for i in range(rows)])

    above, below = shift(pay_down, 1), shift(pay_up, -1)
    others = [shift(pay_own, step) for step in range(2, rows - 1)]
    inner, halves, out_mixes = call(
        inner_kernel,
        "inner",
        [VMEM] * 4,
        (VMEM,) * 3,
        (arr(6, 64, 512), arr(8, 512, 256, dtype=F32), arr(2, 256, 256)),
        [],
        24,
    )(wide, edges, mixes, dec_mix)
    near_out, far_out, block = call(
        functools.partial(rims_kernel, rows=rows, shape=shape),
        "rims",
        [VMEM] * (2 + rows),
        (VMEM,) * 3,
        (arr(shape[0] + 16, 512), arr(shape[0] + 16, 512), arr(shape[0], 512)),
        [pltpu.VMEM((rows,) + shape, BF16)],
        16,
    )(ends, inner, pay_own, above, below, *others)

    def mates(array):
        return lax.ppermute(array, "col", [(i, i ^ 1) for i in range(cols)])

    near = mates(near_out)
    far = lax.ppermute(
        far_out, "col", [(i, (i - 1 if i % 2 == 0 else i + 1) % cols) for i in range(cols)]
    )
    near_pairs = [
        lax.ppermute(
            block, "col", [((i + (even, odd)[i % 2]) % cols, i) for i in range(cols)]
        )
        for even, odd in pair_steps(cols)
    ]
    left_of, right_of, centre = call(
        functools.partial(taps_kernel, rows=rows),
        "taps",
        [VMEM] * (2 + rows),
        (VMEM,) * 3,
        (arr(512, 2048), arr(512, 2048), arr(512, 512, dtype=F32)),
        [pltpu.VMEM((10, 80, 512), F32), pltpu.VMEM((64, 512), F32)],
        24,
    )(ends, inner, pay_own, above, below, *others)
    relayed = mates(far)
    relayed_pairs = [mates(array) for array in near_pairs]
    return call(
        functools.partial(final_kernel, rows=rows, cols=cols, shape=shape, chunks=chunks),
        "final",
        [VMEM] * (12 + 2 * len(near_pairs)),
        HBM,
        jax.ShapeDtypeStruct(fields.shape, BF16),
        [
            pltpu.VMEM((512, 512), BF16),
            pltpu.VMEM((2048, 128), F32),
            pltpu.VMEM((2, 2048, 256), BF16),
            pltpu.VMEM((8, 64, 512), F32),
            pltpu.VMEM((8, 512, 128), F32),
            pltpu.VMEM((8192, 128), F32),
            pltpu.VMEM((512, 16, 128), BF16),
            pltpu.SemaphoreType.DMA((chunks,)),
        ],
        40,
    )(
        ends, inner, halves, out_mixes, left_of, right_of, centre,
        block, near, far, *near_pairs, relayed, *relayed_pairs, turns,
    )


def solution(mesh):
    return jax.shard_map(
        per_device,
        mesh=mesh,
        in_specs=(P(None, "row", "col"), P(), P("row", "col"), P(None, "row", None), P()),
        out_specs=P(None, "row", "col"),
        check_vma=False,
    )
```

time: 42.7 us -> 33.6 us (0.79)
  local copies, waits for them, and re-layouts: 5.64 us -> 0.01 us
  waiting for transfers between devices: 10 us -> 4.41 us
  Pallas kernels: 16.3 us -> 18.6 us
    unnamed x20 -> x4, local copies, waits for them, and re-layouts: 5.64 us -> 0.01 us
    ppermute x3, waiting for transfers between devices: 5.31 us -> 0.86 us  [shift(): lax.ppermute(array, 'row', [(i, (i + step) % rows) for i in range(rows)])]
    pallas_call x3 -> x5, Pallas kernels: 16.3 us -> 18.6 us  [the longest x1 8.07 us: per_device(): call(functools.partial(final_kernel, rows=rows, cols=cols, shape=shape, c...]
    ppermute x4, waiting for transfers between devices: 1.15 us -> 0.01 us  [mates(): return lax.ppermute(array, 'col', [(i, i ^ 1) for i in range(cols)])]
  transfers between devices with their start and end apart: 10 -> 10, of which waited for: 6 -> 4; matrix products, arithmetic and copies ran while one was open for 0% -> 0% of each run, Pallas kernels for 0% -> 21%
where the time goes in v1:
time: 33.6 us; the launch traced here: 33.4 us
  Pallas kernels  18.6 us (55%)
  starting transfers between devices  10.3 us (31%)
  waiting for transfers between devices  4.41 us (13%)
    pallas_call x1, Pallas kernels, per_device(): call(functools.partial(final_kernel, rows=rows, cols=cols, shape=shape, c...  8.07 us
    ppermute x3, starting transfers between devices, shift(): lax.ppermute(array, 'row', [(i, (i + step) % rows) for i in range(rows)])  6.12 us
    pallas_call x1, Pallas kernels, per_device(): call(inner_kernel, 'inner', [VMEM] * 4, (VMEM,) * 3, (arr(6, 64, 512), ar...  4.43 us
    pallas_call x1, Pallas kernels, per_device(): call(functools.partial(edge_kernel, chunks=chunks), 'edges', [HBM] * 4, (...  3.04 us
    pallas_call x1, Pallas kernels, per_device(): call(functools.partial(taps_kernel, rows=rows), 'taps', [VMEM] * (2 + row...  2.72 us
    ppermute x2, waiting for transfers between devices, per_device(): lax.ppermute(block, 'col', [((i + (even, odd)[i % 2]) % cols, i) for i in...  2.01 us
    ppermute x1, starting transfers between devices, per_device(): lax.ppermute(far_out, 'col', [(i, (i - 1 if i % 2 == 0 else i + 1) % cols...  1.96 us
    ppermute x1, waiting for transfers between devices, per_device(): lax.ppermute(far_out, 'col', [(i, (i - 1 if i % 2 == 0 else i + 1) % cols...  1.54 us
  transfers between devices with their start and end apart: 10, of which 4 were waited for; matrix products, arithmetic and copies ran while one was open for 0% of the time, Pallas kernels for 21%

profile of v1, /device:TPU:0, one launch (start us, length us, event | category | flops | bytes accessed | tf_op | source)
XLA Modules:
  0.0 33.4 jit_solution(9528805420484056833)
XLA Ops:
  0.0 0.0 copy-start.1
  0.0 3.0 %edges.1 = (f32[8192,128]{1,0:T(8,128)S(1)}, bf16[2,512,256]{2,1,0:T(8,128)(2,1)S(1)}, bf16[2,64,512]{2,1,0:T(8,128)(2,1)S(1)}, bf16[96,512]{1,0:T(8,128)(2,1)S(...) custom-call(bf16[512,16,128]{2,1,0:T(8,128)(2,1)} %fields_in.1, ...), custom_call_target="tpu_custom_call" | custom-call | tf_op jit(solution)/shard_map/edges/pallas_call | solution.py:470
  3.1 3.1 %collective-permute-start = (bf16[96,512]{1,0:T(8,128)(2,1)S(1)}, bf16[96,512]{1,0:T(8,128)(2,1)S(1)}, u32[]{:S(2)}, u32[]{:S(2)}) collective-permute-start(bf16[96,512]{1,0:T(8,128)(2,1)S(1)} %get-tuple-element.29), channel_id=1, source_target_pairs={{0,8},{8,16},{16,24},{24,0},{1,9},{9,17},{17,25},{25,1},{2,10},{10... | collective-permute-start | bytes 294920 | tf_op jit(solution)/shard_map/ppermute | solution.py:491
  6.1 2.1 %collective-permute-start.1 = (bf16[96,512]{1,0:T(8,128)(2,1)S(1)}, bf16[96,512]{1,0:T(8,128)(2,1)S(1)}, u32[]{:S(2)}, u32[]{:S(2)}) collective-permute-start(bf16[96,512]{1,0:T(8,128)(2,1)S(1)} %get-tuple-element.30), channel_id=1, source_target_pairs={{0,24},{8,0},{16,8},{24,16},{1,25},{9,1},{17,9},{25,17},{2,26},{10... | collective-permute-start | bytes 294920 | tf_op jit(solution)/shard_map/ppermute | solution.py:491
  8.2 0.9 %collective-permute-start.2 = (bf16[32,512]{1,0:T(8,128)(2,1)S(1)}, bf16[32,512]{1,0:T(8,128)(2,1)S(1)}, u32[]{:S(2)}, u32[]{:S(2)}) collective-permute-start(bf16[32,512]{1,0:T(8,128)(2,1)S(1)} %get-tuple-element.28.refs_2_), channel_id=1, source_target_pairs={{0,16},{8,24},{16,0},{24,8},{1,17},{9,25},{17,1},{25,9},{2,18},{10... | collective-permute-start | bytes 98312 | tf_op jit(solution)/shard_map/ppermute | solution.py:491
  9.2 0.0 copy-done.1
  9.2 0.0 copy-start
  9.2 4.4 %inner.1 = (bf16[6,64,512]{2,1,0:T(8,128)(2,1)S(1)}, f32[8,512,256]{2,1,0:T(8,128)S(1)}, bf16[2,256,256]{2,1,0:T(8,128)(2,1)S(1)}) custom-call(f32[8192,128]{1,0:T(8,128)S(1)} %get-tuple-element.22.wide, bf16[2,512,256]{2,1,0:T(8,128)(2,1)S(1)} %get-tuple-element.23.edges, bf16[2,256,256]{2,1,0:T(8,128)(2,1)S(1)} %get-tuple-element.24.mixes_in, ...), custom_call_target="tpu_custom_call" | custom-call | tf_op jit(solution)/shard_map/inner/pallas_call | solution.py:495
  13.6 0.9 %collective-permute-done.2.refs_5_ = bf16[32,512]{1,0:T(8,128)(2,1)S(1)} collective-permute-done((bf16[32,512]{1,0:T(8,128)(2,1)S(1)}, bf16[32,512]{1,0:T(8,128)(2,1)S(1)}, u32[]{:S(2)}, u32[]{:S(2)}) %collective-permute-start.2) | collective-permute-done | bytes 32800 | tf_op jit(solution)/shard_map/ppermute | solution.py:491
  14.5 0.0 collective-permute-done.refs_3_
  14.5 0.0 collective-permute-done.1.refs_4_
  14.5 0.4 %rims.1 = (bf16[80,512]{1,0:T(8,128)(2,1)S(1)}, bf16[80,512]{1,0:T(8,128)(2,1)S(1)}, bf16[64,512]{1,0:T(8,128)(2,1)S(1)}) custom-call(bf16[2,64,512]{2,1,0:T(8,128)(2,1)S(1)} %get-tuple-element.21.refs_0_, bf16[6,64,512]{2,1,0:T(8,128)(2,1)S(1)} %get-tuple-element.25.refs_1_, bf16[32,512]{1,0:T(8,128)(2,1)S(1)} %get-tuple-element.28.refs_2_, ...), custom_call_target="tpu_custom_call" | custom-call | tf_op jit(solution)/shard_map/rims/pallas_call | solution.py:504
  14.8 2.0 %collective-permute-start.4 = (bf16[80,512]{1,0:T(8,128)(2,1)S(1)}, bf16[80,512]{1,0:T(8,128)(2,1)S(1)}, u32[]{:S(2)}, u32[]{:S(2)}) collective-permute-start(bf16[80,512]{1,0:T(8,128)(2,1)S(1)} %get-tuple-element.36), channel_id=1, source_target_pairs={{0,7},{1,2},{2,1},{3,4},{4,3},{5,6},{6,5},{7,0},{8,15},{9,10},{10,... | collective-permute-start | bytes 245768 | tf_op jit(solution)/shard_map/ppermute | solution.py:518
  16.8 0.0 collective-permute-start.6
  16.8 1.2 %collective-permute-start.5 = (bf16[64,512]{1,0:T(8,128)(2,1)S(1)}, bf16[64,512]{1,0:T(8,128)(2,1)S(1)}, u32[]{:S(2)}, u32[]{:S(2)}) collective-permute-start(bf16[64,512]{1,0:T(8,128)(2,1)S(1)} %get-tuple-element.34.refs_7_), channel_id=1, source_target_pairs={{4,0},{5,1},{6,2},{7,3},{0,4},{1,5},{2,6},{3,7},{12,8},{13,9},{14,... | collective-permute-start | bytes 196616 | tf_op jit(solution)/shard_map/ppermute | solution.py:522
  18.0 0.9 %collective-permute-start.3 = (bf16[80,512]{1,0:T(8,128)(2,1)S(1)}, bf16[80,512]{1,0:T(8,128)(2,1)S(1)}, u32[]{:S(2)}, u32[]{:S(2)}) collective-permute-start(bf16[80,512]{1,0:T(8,128)(2,1)S(1)} %get-tuple-element.35), channel_id=1, source_target_pairs={{0,1},{1,0},{2,3},{3,2},{4,5},{5,4},{6,7},{7,6},{8,9},{9,8},{10,11... | collective-permute-start | bytes 245768 | tf_op jit(solution)/shard_map/ppermute | solution.py:515
  18.9 1.5 %collective-permute-done.4.refs_9_ = bf16[80,512]{1,0:T(8,128)(2,1)S(1)} collective-permute-done((bf16[80,512]{1,0:T(8,128)(2,1)S(1)}, bf16[80,512]{1,0:T(8,128)(2,1)S(1)}, u32[]{:S(2)}, u32[]{:S(2)}) %collective-permute-start.4) | collective-permute-done | bytes 81952 | tf_op jit(solution)/shard_map/ppermute | solution.py:518
  20.5 0.0 collective-permute-start.7
  20.5 1.6 %collective-permute-done.6.refs_11_ = bf16[64,512]{1,0:T(8,128)(2,1)S(1)} collective-permute-done((bf16[64,512]{1,0:T(8,128)(2,1)S(1)}, bf16[64,512]{1,0:T(8,128)(2,1)S(1)}, u32[]{:S(2)}, u32[]{:S(2)}) %collective-permute-start.6) | collective-permute-done | bytes 65568 | tf_op jit(solution)/shard_map/ppermute | solution.py:522
  22.1 0.0 collective-permute-start.9
  22.1 0.4 %collective-permute-done.5.refs_10_ = bf16[64,512]{1,0:T(8,128)(2,1)S(1)} collective-permute-done((bf16[64,512]{1,0:T(8,128)(2,1)S(1)}, bf16[64,512]{1,0:T(8,128)(2,1)S(1)}, u32[]{:S(2)}, u32[]{:S(2)}) %collective-permute-start.5) | collective-permute-done | bytes 65568 | tf_op jit(solution)/shard_map/ppermute | solution.py:522
  22.5 0.1 collective-permute-start.8
  22.6 2.7 %taps.1 = (bf16[512,2048]{1,0:T(8,128)(2,1)S(1)}, bf16[512,2048]{1,0:T(8,128)(2,1)S(1)}, f32[512,512]{1,0:T(8,128)S(1)}) custom-call(bf16[2,64,512]{2,1,0:T(8,128)(2,1)S(1)} %get-tuple-element.21.refs_0_, bf16[6,64,512]{2,1,0:T(8,128)(2,1)S(1)} %get-tuple-element.25.refs_1_, bf16[32,512]{1,0:T(8,128)(2,1)S(1)} %get-tuple-element.28.refs_2_, ...), custom_call_target="tpu_custom_call" | custom-call | tf_op jit(solution)/shard_map/taps/pallas_call | solution.py:527
  25.3 0.0 collective-permute-done.3.refs_8_
  25.3 0.0 collective-permute-done.9.refs_14_
  25.3 0.0 collective-permute-done.8.refs_13_
  25.3 0.0 collective-permute-done.7.refs_12_
  25.4 0.0 copy-done
  25.4 8.1 %final.1 = bf16[512,16,128]{2,1,0:T(8,128)(2,1)} custom-call(bf16[2,64,512]{2,1,0:T(8,128)(2,1)S(1)} %get-tuple-element.21.refs_0_, bf16[6,64,512]{2,1,0:T(8,128)(2,1)S(1)} %get-tuple-element.25.refs_1_, f32[8,512,256]{2,1,0:T(8,128)S(1)} %get-tuple-element.26.refs_2_, bf16[2,256,256]{2,1,0:T(8,128)(2,1)S(1)} %get-tuple-element.27.refs_3_, ...), custom_call_target="tpu_custom_call" | custom-call | tf_op jit(solution)/shard_map/final/pallas_call | solution.py:538
Async XLA Ops:
  0.0 9.2 %copy-start.1 = (bf16[8,64,64]{2,1,0:T(8,128)(2,1)S(1)}, bf16[8,64,64]{2,1,0:T(8,128)(2,1)}, u32[]{:S(2)}) copy-start(bf16[8,64,64]{2,1,0:T(8,128)(2,1)} %weights.1) | copy-start | bytes 196612
  3.1 11.4 %collective-permute-start = (bf16[96,512]{1,0:T(8,128)(2,1)S(1)}, bf16[96,512]{1,0:T(8,128)(2,1)S(1)}, u32[]{:S(2)}, u32[]{:S(2)}) collective-permute-start(bf16[96,512]{1,0:T(8,128)(2,1)S(1)} %get-tuple-element.29), channel_id=1, source_target_pairs={{0,8},{8,16},{16,24},{24,0},{1,9},{9,17},{17,25},{25,1},{2,10},{10... | collective-permute-start | bytes 294920 | tf_op jit(solution)/shard_map/ppermute | solution.py:491
  6.1 8.3 %collective-permute-start.1 = (bf16[96,512]{1,0:T(8,128)(2,1)S(1)}, bf16[96,512]{1,0:T(8,128)(2,1)S(1)}, u32[]{:S(2)}, u32[]{:S(2)}) collective-permute-start(bf16[96,512]{1,0:T(8,128)(2,1)S(1)} %get-tuple-element.30), channel_id=1, source_target_pairs={{0,24},{8,0},{16,8},{24,16},{1,25},{9,1},{17,9},{25,17},{2,26},{10... | collective-permute-start | bytes 294920 | tf_op jit(solution)/shard_map/ppermute | solution.py:491
  8.2 6.2 %collective-permute-start.2 = (bf16[32,512]{1,0:T(8,128)(2,1)S(1)}, bf16[32,512]{1,0:T(8,128)(2,1)S(1)}, u32[]{:S(2)}, u32[]{:S(2)}) collective-permute-start(bf16[32,512]{1,0:T(8,128)(2,1)S(1)} %get-tuple-element.28.refs_2_), channel_id=1, source_target_pairs={{0,16},{8,24},{16,0},{24,8},{1,17},{9,25},{17,1},{25,9},{2,18},{10... | collective-permute-start | bytes 98312 | tf_op jit(solution)/shard_map/ppermute | solution.py:491
  9.2 16.2 %copy-start = (bf16[3,2,256,256]{3,2,1,0:T(8,128)(2,1)S(1)}, bf16[3,2,256,256]{3,2,1,0:T(8,128)(2,1)}, u32[]{:S(2)}) copy-start(bf16[3,2,256,256]{3,2,1,0:T(8,128)(2,1)} %constant.2.clone.refs_15_) | copy-start | bytes 2359300
  14.8 5.6 %collective-permute-start.4 = (bf16[80,512]{1,0:T(8,128)(2,1)S(1)}, bf16[80,512]{1,0:T(8,128)(2,1)S(1)}, u32[]{:S(2)}, u32[]{:S(2)}) collective-permute-start(bf16[80,512]{1,0:T(8,128)(2,1)S(1)} %get-tuple-element.36), channel_id=1, source_target_pairs={{0,7},{1,2},{2,1},{3,4},{4,3},{5,6},{6,5},{7,0},{8,15},{9,10},{10,... | collective-permute-start | bytes 245768 | tf_op jit(solution)/shard_map/ppermute | solution.py:518
  16.8 5.3 %collective-permute-start.6 = (bf16[64,512]{1,0:T(8,128)(2,1)S(1)}, bf16[64,512]{1,0:T(8,128)(2,1)S(1)}, u32[]{:S(2)}, u32[]{:S(2)}) collective-permute-start(bf16[64,512]{1,0:T(8,128)(2,1)S(1)} %get-tuple-element.34.refs_7_), channel_id=1, source_target_pairs={{6,0},{3,1},{0,2},{5,3},{2,4},{7,5},{4,6},{1,7},{14,8},{11,9},{8,1... | collective-permute-start | bytes 196616 | tf_op jit(solution)/shard_map/ppermute | solution.py:522
  16.8 5.7 %collective-permute-start.5 = (bf16[64,512]{1,0:T(8,128)(2,1)S(1)}, bf16[64,512]{1,0:T(8,128)(2,1)S(1)}, u32[]{:S(2)}, u32[]{:S(2)}) collective-permute-start(bf16[64,512]{1,0:T(8,128)(2,1)S(1)} %get-tuple-element.34.refs_7_), channel_id=1, source_target_pairs={{4,0},{5,1},{6,2},{7,3},{0,4},{1,5},{2,6},{3,7},{12,8},{13,9},{14,... | collective-permute-start | bytes 196616 | tf_op jit(solution)/shard_map/ppermute | solution.py:522
  18.0 7.3 %collective-permute-start.3 = (bf16[80,512]{1,0:T(8,128)(2,1)S(1)}, bf16[80,512]{1,0:T(8,128)(2,1)S(1)}, u32[]{:S(2)}, u32[]{:S(2)}) collective-permute-start(bf16[80,512]{1,0:T(8,128)(2,1)S(1)} %get-tuple-element.35), channel_id=1, source_target_pairs={{0,1},{1,0},{2,3},{3,2},{4,5},{5,4},{6,7},{7,6},{8,9},{9,8},{10,11... | collective-permute-start | bytes 245768 | tf_op jit(solution)/shard_map/ppermute | solution.py:515
  20.5 4.9 %collective-permute-start.7 = (bf16[80,512]{1,0:T(8,128)(2,1)S(1)}, bf16[80,512]{1,0:T(8,128)(2,1)S(1)}, u32[]{:S(2)}, u32[]{:S(2)}) collective-permute-start(bf16[80,512]{1,0:T(8,128)(2,1)S(1)} %collective-permute-done.4.refs_9_), channel_id=1, source_target_pairs={{0,1},{1,0},{2,3},{3,2},{4,5},{5,4},{6,7},{7,6},{8,9},{9,8},{10,11... | collective-permute-start | bytes 245768 | tf_op jit(solution)/shard_map/ppermute | solution.py:515
  22.1 3.2 %collective-permute-start.9 = (bf16[64,512]{1,0:T(8,128)(2,1)S(1)}, bf16[64,512]{1,0:T(8,128)(2,1)S(1)}, u32[]{:S(2)}, u32[]{:S(2)}) collective-permute-start(bf16[64,512]{1,0:T(8,128)(2,1)S(1)} %collective-permute-done.6.refs_11_), channel_id=1, source_target_pairs={{0,1},{1,0},{2,3},{3,2},{4,5},{5,4},{6,7},{7,6},{8,9},{9,8},{10,11... | collective-permute-start | bytes 196616 | tf_op jit(solution)/shard_map/ppermute | solution.py:515
  22.5 2.9 %collective-permute-start.8 = (bf16[64,512]{1,0:T(8,128)(2,1)S(1)}, bf16[64,512]{1,0:T(8,128)(2,1)S(1)}, u32[]{:S(2)}, u32[]{:S(2)}) collective-permute-start(bf16[64,512]{1,0:T(8,128)(2,1)S(1)} %collective-permute-done.5.refs_10_), channel_id=1, source_target_pairs={{0,1},{1,0},{2,3},{3,2},{4,5},{5,4},{6,7},{7,6},{8,9},{9,8},{10,11... | collective-permute-start | bytes 196616 | tf_op jit(solution)/shard_map/ppermute | solution.py:515

commit v2 on v1

--- a/solution.py
+++ b/solution.py
@@ -94,12 +94,12 @@
 
 
 def row_start(c, component):
-    return ((c * 8) * 8 + component) * 16
+    return c * 8 * PITCH + component * 16
 
 
 def gather_rows(wide, y, group):
     chunks = [
-        wide[pl.ds(row_start(c, COMPONENTS[group][b]) + y, 8, stride=128), :]
+        wide[pl.ds(row_start(c, COMPONENTS[group][b]) + y, 8, stride=PITCH), :]
         for c in range(8)
         for b in range(4)
     ]
@@ -163,7 +163,10 @@
     for n in range(chunks):
         copies[n].wait()
         piece = held[n * size : (n + 1) * size].astype(F32)
-        wide[n * size * 16 : (n + 1) * size * 16, :] = piece.reshape(size * 16, 128)
+        piece = piece.reshape(size * 16, 128)
+        for m in range(size // 8):
+            at = (n * size // 8 + m) * PITCH
+            wide[at : at + 128, :] = piece[m * 128 : m * 128 + 128]
     for n, (target, line) in enumerate(((pay_up, 0), (pay_down, 7))):
         result, mean = encode_line(wide, line, mixes, pool_t)
         encoded[n, 0:256, :] = result[0]
@@ -240,20 +243,22 @@
 def taps_kernel(*refs, rows):
     ends, inner, own, above, below = refs[:5]
     others = refs[5 : 5 + rows - 3]
-    left_of, right_of, middle, padded, centre_rows = refs[2 + rows :]
+    left_of, right_of, middle, padded, shifted, centre_rows = refs[2 + rows :]
     row = lax.axis_index("row")
     zero = jnp.zeros((1, 512), F32)
     for line, values in enumerate(all_lines(ends, inner, above, below, row, rows)):
         padded[line, 8:72, :] = values
         padded[line, 7:8, :] = zero
         padded[line, 72:73, :] = zero
+        shifted[1, line] = values.astype(BF16)
+        shifted[0, line] = padded[line, 7:71, :].astype(BF16)
+        shifted[2, line] = padded[line, 9:73, :].astype(BF16)
     for line in range(8):
         span = slice(line * 64, line * 64 + 64)
         for tap, (dy, dx) in enumerate(TAPS):
-            ahead = padded[line + 1 + dy, 8 + dx : 72 + dx, :]
-            behind = padded[line + 1 - dy, 8 - dx : 72 - dx, :]
-            plus = (ahead + behind).astype(BF16)
-            minus = (ahead - behind).astype(BF16)
+            ahead = shifted[1 + dx, line + 1 + dy]
+            behind = shifted[1 - dx, line + 1 - dy]
+            plus, minus = ahead + behind, ahead - behind
             base = tap * 512
             left_of[span, base : base + 256] = plus[:, :256]
             left_of[span, base + 256 : base + 512] = minus[:, 256:]
@@ -263,15 +268,15 @@
     own_rows = 64 // rows
     table = spread_table()
 
-    def put_centre(source, start, index):
+    def put_centre(values, index):
         place = pl.multiple_of(index * own_rows, own_rows)
-        centre_rows[pl.ds(place, own_rows), :] = source[start : start + own_rows, :].astype(F32)
-
-    put_centre(own, 16, row)
-    put_centre(above, 80, lax.rem(row + rows - 1, rows))
-    put_centre(below, 80, lax.rem(row + 1, rows))
+        centre_rows[pl.ds(place, own_rows), :] = values.astype(F32)
+
+    put_centre(own[16 : 16 + own_rows, :], row)
+    put_centre(above[80 : 80 + own_rows, :], lax.rem(row + rows - 1, rows))
+    put_centre(below[80 : 80 + own_rows, :], lax.rem(row + 1, rows))
     for n, other in enumerate(others):
-        put_centre(other, 16, lax.rem(row + rows - 2 - n, rows))
+        put_centre(other[16 : 16 + own_rows, :], lax.rem(row + rows - 2 - n, rows))
     centre = centre_rows[...].astype(BF16)
     whole = jnp.concatenate(own_lines(ends, inner), axis=0)
     for group in range(2):
@@ -301,55 +306,28 @@
     return jnp.concatenate(parts, axis=1).astype(BF16)
 
 
-def final_kernel(*refs, rows, cols, shape, chunks):
-    rows_in, _ = shape
-    pairs = pair_steps(cols)
-    ends, inner, halves, mixes, left_of, right_of, centre = refs[:7]
-    block, near, far = refs[7:10]
-    near_pairs = refs[10 : 10 + len(pairs)]
-    relayed = refs[10 + len(pairs)]
-    relayed_pairs = refs[11 + len(pairs) : 11 + 2 * len(pairs)]
-    refs = refs[11 + 2 * len(pairs) :]
-    turns, decoded = refs[:2]
-    kt, turned, middle, coarse, doubled, wide, out, sems = refs[2:]
-    col = lax.axis_index("col")
-    even = lax.rem(col, 2) == 0
-    mate = jnp.where(even, col + 1, col - 1)
-
-    def put(source, index):
-        start = pl.multiple_of(lax.rem(index + 2 * cols, cols) * rows_in, rows_in)
-        kt[pl.ds(start, rows_in), :] = source[0:rows_in, :]
-
-    def away(index, step_even, step_odd):
-        return index + jnp.where(lax.rem(index, 2) == 0, step_even, step_odd)
-
-    put(block, col)
-    put(near, mate)
-    put(far, away(col, -1, 1))
-    put(relayed, away(mate, -1, 1))
-    for n, (step_even, step_odd) in enumerate(pairs):
-        put(near_pairs[n], away(col, step_even, step_odd))
-        put(relayed_pairs[n], away(mate, step_even, step_odd))
-
+def turn_blocks(blocks, places, turns, turned, middle):
     root = math.sqrt(0.5)
+    whole = jnp.concatenate(blocks, axis=0)
+    count = whole.shape[0] // 64
     for tap in range(4):
         signs = turn_signs(tap)
         for group in range(2):
-            whole = kt[:, group * 256 : (group + 1) * 256]
-            result = whole.astype(F32) if tap == 0 else dot(whole, turns[tap - 1, group])
+            side = whole[:, group * 256 : (group + 1) * 256]
+            result = side.astype(F32) if tap == 0 else dot(side, turns[tap - 1, group])
             base = ((tap * 2 + group) % 2) * 1024
-            turned[base : base + 512, :] = result[:, 0:128]
-            turned[base + 512 : base + 1024, :] = result[:, 128:256]
+            turned[base : base + count * 64, :] = result[:, 0:128]
+            turned[base + 512 : base + 512 + count * 64, :] = result[:, 128:256]
             for source in range(2):
                 scale = 1.0
                 if tap % 2:
                     scale = (1.0, root, 0.5)[group + source]
                 comps = COMPONENTS[source]
-                for c in range(8):
+                for n in range(count):
                     read = {
                         comp: jnp.concatenate(
                             [
-                                turned[pl.ds(base + half * 512 + c * 64 + comp, 8, stride=8), :]
+                                turned[pl.ds(base + half * 512 + n * 64 + comp, 8, stride=8), :]
                                 for half in range(2)
                             ],
                             axis=1,
@@ -368,8 +346,55 @@
                             else:
                                 total = total + read[other] if sign > 0 else total - read[other]
                         parts.append(total if scale == 1.0 else total * scale)
-                    start = tap * 512 + source * 256 + c * 32
-                    middle[group, start : start + 32, :] = jnp.concatenate(parts, axis=0).astype(BF16)
+                    start = pl.multiple_of(tap * 512 + source * 256 + places[n] * 32, 32)
+                    middle[group, pl.ds(start, 32), :] = jnp.concatenate(parts, axis=0).astype(BF16)
+
+
+def away(index, step_even, step_odd, cols):
+    index = index + jnp.where(lax.rem(index, 2) == 0, step_even, step_odd)
+    return lax.rem(index + 2 * cols, cols)
+
+
+def block_places(col, cols):
+    even = lax.rem(col, 2) == 0
+    mate = jnp.where(even, col + 1, col - 1)
+    steps = [(-1, 1)] + pair_steps(cols)
+    first = [col, mate] + [away(col, a, b, cols) for a, b in steps]
+    return first, [away(mate, a, b, cols) for a, b in steps]
+
+
+def early_kernel(*refs, cols, rows_in):
+    blocks = refs[: 2 + cols // 2 - 1]
+    turns, middle, turned = refs[2 + cols // 2 - 1 :]
+    places, _ = block_places(lax.axis_index("col"), cols)
+    turn_blocks([block[0:rows_in, :] for block in blocks], places, turns, turned, middle)
+
+
+def final_kernel(*refs, cols, shape, chunks, split):
+    rows_in, _ = shape
+    relays = cols // 2 - 1
+    ends, inner, halves, mixes, left_of, right_of, centre = refs[:7]
+    near, far = refs[7:9]
+    refs = refs[9:]
+    col = lax.axis_index("col")
+    even = lax.rem(col, 2) == 0
+    first, second = block_places(col, cols)
+    if split:
+        relayed, turns = refs[:relays], refs[relays]
+        decoded, middle, turned, coarse, doubled, wide, out, sems = refs[relays + 2 :]
+        late = [block[0:rows_in, :] for block in relayed]
+        places = second
+    else:
+        held, relayed, turns = refs[: relays], refs[relays : 2 * relays], refs[2 * relays]
+        decoded, kt, middle, turned, coarse, doubled, wide, out, sems = refs[2 * relays + 1 :]
+        for block, index in zip((held[0], near, far) + held[1:] + relayed, first + second):
+            start = pl.multiple_of(index * rows_in, rows_in)
+            kt[pl.ds(start, rows_in), :] = block[0:rows_in, :]
+        late = [kt[...]]
+        places = list(range(8))
+
+    pending = list(late)
+    turn_blocks(pending, places, turns, turned, middle)
 
     near_rim = near[rows_in : rows_in + 16, :].astype(F32)
     far_rim = far[rows_in : rows_in + 16, :].astype(F32)
@@ -422,7 +447,7 @@
                     for b in range(4):
                         start = row_start(c, COMPONENTS[group][b]) + 2 * line + half
                         at = c * 32 + b * 8
-                        wide[pl.ds(start, 8, stride=128), :] = d[
+                        wide[pl.ds(start, 8, stride=PITCH), :] = d[
                             at : at + 8, half * 128 : half * 128 + 128
                         ]
         return carry
@@ -432,8 +457,10 @@
     copies = []
     for n in range(chunks):
         span = pl.ds(n * size, size)
-        piece = wide[n * size * 16 : (n + 1) * size * 16, :].astype(BF16)
-        out[n * size : (n + 1) * size] = piece.reshape(size, 16, 128)
+        for m in range(size // 8):
+            at = (n * size // 8 + m) * PITCH
+            piece = wide[at : at + 128, :].astype(BF16)
+            out[n * size + m * 8 : n * size + m * 8 + 8] = piece.reshape(8, 16, 128)
         copies.append(pltpu.make_async_copy(out.at[span], decoded.at[span], sems.at[n]))
         copies[-1].start()
     for copy in copies:
@@ -442,10 +469,11 @@
 
 VMEM = pl.BlockSpec(memory_space=pltpu.VMEM)
 HBM = pl.BlockSpec(memory_space=pltpu.HBM)
-UNROLL = 2
-
-
-def call(kernel, name, ins, outs, shapes, scratch, mebibytes):
+UNROLL = True
+PITCH = 136
+
+
+def call(kernel, name, ins, outs, shapes, scratch, mebibytes, aliases={}):
     return pl.pallas_call(
         kernel,
         out_shape=shapes,
@@ -454,6 +482,7 @@
         scratch_shapes=scratch,
         compiler_params=pltpu.CompilerParams(vmem_limit_bytes=mebibytes * 1024 * 1024),
         name=name,
+        input_output_aliases=aliases,
     )
 
 
@@ -465,6 +494,10 @@
     rows, cols = lax.axis_size("row"), lax.axis_size("col")
     k_local = k_cycle.T
     shape = k_local.shape
+
+    def shift(array, step):
+        return lax.ppermute(array, "row", [(i, (i + step) % rows) for i in range(rows)])
+
     turns = jnp.asarray(np.stack([turn_table(t) for t in (1, 2, 3)]), BF16)
     chunks = 4
     wide, edges, ends, pay_down, pay_up, pay_own, mixes = call(
@@ -473,7 +506,7 @@
         [HBM] * 4,
         (VMEM,) * 7,
         (
-            arr(8192, 128, dtype=F32), arr(2, 512, 256), arr(2, 64, 512),
+            arr(64 * PITCH, 128, dtype=F32), arr(2, 512, 256), arr(2, 64, 512),
             arr(96, 512), arr(96, 512), arr(32, 512), arr(2, 256, 256),
         ),
         [
@@ -486,9 +519,6 @@
         ],
         24,
     )(*[pltpu.with_memory_space_constraint(x, pltpu.HBM) for x in (fields, enc_mix, k_local, centre_mix)])
-
-    def shift(array, step):
-        return lax.ppermute(array, "row", [(i, (i + step) % rows) for i in range(rows)])
 
     above, below = shift(pay_down, 1), shift(pay_up, -1)
     others = [shift(pay_own, step) for step in range(2, rows - 1)]
@@ -530,32 +560,47 @@
         [VMEM] * (2 + rows),
         (VMEM,) * 3,
         (arr(512, 2048), arr(512, 2048), arr(512, 512, dtype=F32)),
-        [pltpu.VMEM((10, 80, 512), F32), pltpu.VMEM((64, 512), F32)],
+        [
+            pltpu.VMEM((10, 80, 512), F32),
+            pltpu.VMEM((3, 10, 64, 512), BF16),
+            pltpu.VMEM((64, 512), F32),
+        ],
         24,
     )(ends, inner, pay_own, above, below, *others)
-    relayed = mates(far)
-    relayed_pairs = [mates(array) for array in near_pairs]
+    near, far, near_pairs, left_of, right_of, centre = lax.optimization_barrier(
+        (near, far, near_pairs, left_of, right_of, centre)
+    )
+    relayed = [mates(array) for array in [far] + near_pairs]
+    split = shape[0] == 64
+    scratch = [
+        pltpu.VMEM((2048, 128), F32),
+        pltpu.VMEM((8, 64, 512), F32),
+        pltpu.VMEM((8, 512, 128), F32),
+        pltpu.VMEM((64 * PITCH, 128), F32),
+        pltpu.VMEM((512, 16, 128), BF16),
+        pltpu.SemaphoreType.DMA((chunks,)),
+    ]
+    kernel = functools.partial(final_kernel, cols=cols, shape=shape, chunks=chunks, split=split)
+    operands = [ends, inner, halves, out_mixes, left_of, right_of, centre, near, far]
+    result = jax.ShapeDtypeStruct(fields.shape, BF16)
+    if not split:
+        operands += [block] + near_pairs + relayed + [turns]
+        scratch = [pltpu.VMEM((512, 512), BF16), pltpu.VMEM((2, 2048, 256), BF16)] + scratch
+        return call(kernel, "final", [VMEM] * len(operands), HBM, result, scratch, 40)(*operands)
+    middle = call(
+        functools.partial(early_kernel, cols=cols, rows_in=shape[0]),
+        "early",
+        [VMEM] * (4 + len(near_pairs)),
+        VMEM,
+        arr(2, 2048, 256),
+        [pltpu.VMEM((2048, 128), F32)],
+        24,
+    )(block, near, far, *near_pairs, turns)
+    operands += relayed + [turns, middle]
     return call(
-        functools.partial(final_kernel, rows=rows, cols=cols, shape=shape, chunks=chunks),
-        "final",
-        [VMEM] * (12 + 2 * len(near_pairs)),
-        HBM,
-        jax.ShapeDtypeStruct(fields.shape, BF16),
-        [
-            pltpu.VMEM((512, 512), BF16),
-            pltpu.VMEM((2048, 128), F32),
-            pltpu.VMEM((2, 2048, 256), BF16),
-            pltpu.VMEM((8, 64, 512), F32),
-            pltpu.VMEM((8, 512, 128), F32),
-            pltpu.VMEM((8192, 128), F32),
-            pltpu.VMEM((512, 16, 128), BF16),
-            pltpu.SemaphoreType.DMA((chunks,)),
-        ],
-        40,
-    )(
-        ends, inner, halves, out_mixes, left_of, right_of, centre,
-        block, near, far, *near_pairs, relayed, *relayed_pairs, turns,
-    )
+        kernel, "final", [VMEM] * len(operands), (HBM, VMEM), (result, arr(2, 2048, 256)),
+        scratch, 40, aliases={len(operands) - 1: 1},
+    )(*operands)[0]
 
 
 def solution(mesh):

time: 33.6 us -> 29 us (0.86)
  Pallas kernels: 18.6 us -> 12.7 us
  waiting for transfers between devices: 4.41 us -> 5.56 us
    pallas_call x1 -> x2, Pallas kernels: 8.07 us -> 5.52 us  [the longest x1 4.74 us: per_device(): call(kernel, 'final', [VMEM] * len(operands), (HBM, VMEM), (result, arr(2...]
    pallas_call x1, Pallas kernels: 4.43 us -> 2.62 us  [per_device(): call(inner_kernel, 'inner', [VMEM] * 4, (VMEM,) * 3, (arr(6, 64, 512), ar...]
    ppermute x3, waiting for transfers between devices: 0.86 us -> 2.66 us  [shift(): lax.ppermute(array, 'row', [(i, (i + step) % rows) for i in range(rows)])]
    ppermute x1, waiting for transfers between devices: 1.54 us -> 0.01 us  [per_device(): lax.ppermute(far_out, 'col', [(i, (i - 1 if i % 2 == 0 else i + 1) % cols...]
    pallas_call x1, Pallas kernels: 2.72 us -> 1.56 us  [per_device(): call(functools.partial(taps_kernel, rows=rows), 'taps', [VMEM] * (2 + row...]
    ppermute x1, starting transfers between devices: 1.96 us -> 2.55 us  [per_device(): lax.ppermute(far_out, 'col', [(i, (i - 1 if i % 2 == 0 else i + 1) % cols...]
    ppermute x2, waiting for transfers between devices: 2.01 us -> 2.51 us  [per_device(): lax.ppermute(block, 'col', [((i + (even, odd)[i % 2]) % cols, i) for i in...]
    ppermute x4, waiting for transfers between devices: 0.01 us -> 0.4 us  [mates(): return lax.ppermute(array, 'col', [(i, i ^ 1) for i in range(cols)])]
  transfers between devices with their start and end apart: 10 -> 10, of which waited for: 4 -> 3; matrix products, arithmetic and copies ran while one was open for 0% -> 0% of each run, Pallas kernels for 21% -> 17%
where the time goes in v2:
time: 29 us; the launch traced here: 28.9 us
  Pallas kernels  12.7 us (44%)
  starting transfers between devices  10.5 us (36%)
  waiting for transfers between devices  5.56 us (19%)
    ppermute x3, starting transfers between devices, shift(): lax.ppermute(array, 'row', [(i, (i + step) % rows) for i in range(rows)])  6.11 us
    pallas_call x1, Pallas kernels, per_device(): call(kernel, 'final', [VMEM] * len(operands), (HBM, VMEM), (result, arr(2...  4.74 us
    pallas_call x1, Pallas kernels, per_device(): call(functools.partial(edge_kernel, chunks=chunks), 'edges', [HBM] * 4, (...  2.67 us
    ppermute x3, waiting for transfers between devices, shift(): lax.ppermute(array, 'row', [(i, (i + step) % rows) for i in range(rows)])  2.66 us
    pallas_call x1, Pallas kernels, per_device(): call(inner_kernel, 'inner', [VMEM] * 4, (VMEM,) * 3, (arr(6, 64, 512), ar...  2.62 us
    ppermute x1, starting transfers between devices, per_device(): lax.ppermute(far_out, 'col', [(i, (i - 1 if i % 2 == 0 else i + 1) % cols...  2.55 us
    ppermute x2, waiting for transfers between devices, per_device(): lax.ppermute(block, 'col', [((i + (even, odd)[i % 2]) % cols, i) for i in...  2.51 us
    pallas_call x1, Pallas kernels, per_device(): call(functools.partial(taps_kernel, rows=rows), 'taps', [VMEM] * (2 + row...  1.56 us
  transfers between devices with their start and end apart: 10, of which 3 were waited for; matrix products, arithmetic and copies ran while one was open for 0% of the time, Pallas kernels for 17%

profile of v2, /device:TPU:0, one launch (start us, length us, event | category | flops | bytes accessed | tf_op | source)
XLA Modules:
  0.0 28.9 jit_solution(2851955439652604998)
XLA Ops:
  0.0 0.0 copy-start.1
  0.0 2.7 %edges.1 = (f32[8704,128]{1,0:T(8,128)S(1)}, bf16[2,512,256]{2,1,0:T(8,128)(2,1)S(1)}, bf16[2,64,512]{2,1,0:T(8,128)(2,1)S(1)}, bf16[96,512]{1,0:T(8,128)(2,1)S(...) custom-call(bf16[512,16,128]{2,1,0:T(8,128)(2,1)} %fields_in.1, ...), custom_call_target="tpu_custom_call" | custom-call | tf_op jit(solution)/shard_map/edges/pallas_call | solution.py:503
  2.7 3.1 %collective-permute-start = (bf16[96,512]{1,0:T(8,128)(2,1)S(1)}, bf16[96,512]{1,0:T(8,128)(2,1)S(1)}, u32[]{:S(2)}, u32[]{:S(2)}) collective-permute-start(bf16[96,512]{1,0:T(8,128)(2,1)S(1)} %get-tuple-element.37), channel_id=1, source_target_pairs={{0,8},{8,16},{16,24},{24,0},{1,9},{9,17},{17,25},{25,1},{2,10},{10... | collective-permute-start | bytes 294920 | tf_op jit(solution)/shard_map/ppermute | solution.py:499
  5.8 2.1 %collective-permute-start.1 = (bf16[96,512]{1,0:T(8,128)(2,1)S(1)}, bf16[96,512]{1,0:T(8,128)(2,1)S(1)}, u32[]{:S(2)}, u32[]{:S(2)}) collective-permute-start(bf16[96,512]{1,0:T(8,128)(2,1)S(1)} %get-tuple-element.38), channel_id=1, source_target_pairs={{0,24},{8,0},{16,8},{24,16},{1,25},{9,1},{17,9},{25,17},{2,26},{10... | collective-permute-start | bytes 294920 | tf_op jit(solution)/shard_map/ppermute | solution.py:499
  7.8 0.9 %collective-permute-start.2 = (bf16[32,512]{1,0:T(8,128)(2,1)S(1)}, bf16[32,512]{1,0:T(8,128)(2,1)S(1)}, u32[]{:S(2)}, u32[]{:S(2)}) collective-permute-start(bf16[32,512]{1,0:T(8,128)(2,1)S(1)} %get-tuple-element.36.refs_2_), channel_id=1, source_target_pairs={{0,16},{8,24},{16,0},{24,8},{1,17},{9,25},{17,1},{25,9},{2,18},{10... | collective-permute-start | bytes 98312 | tf_op jit(solution)/shard_map/ppermute | solution.py:499
  8.8 0.0 copy-done.1
  8.8 2.6 %inner.1 = (bf16[6,64,512]{2,1,0:T(8,128)(2,1)S(1)}, f32[8,512,256]{2,1,0:T(8,128)S(1)}, bf16[2,256,256]{2,1,0:T(8,128)(2,1)S(1)}) custom-call(f32[8704,128]{1,0:T(8,128)S(1)} %get-tuple-element.30.wide, bf16[2,512,256]{2,1,0:T(8,128)(2,1)S(1)} %get-tuple-element.31.edges, bf16[2,256,256]{2,1,0:T(8,128)(2,1)S(1)} %get-tuple-element.32.mixes_in, ...), custom_call_target="tpu_custom_call" | custom-call | tf_op jit(solution)/shard_map/inner/pallas_call | solution.py:525
  11.4 0.0 copy-start
  11.4 2.7 %collective-permute-done.2.refs_5_ = bf16[32,512]{1,0:T(8,128)(2,1)S(1)} collective-permute-done((bf16[32,512]{1,0:T(8,128)(2,1)S(1)}, bf16[32,512]{1,0:T(8,128)(2,1)S(1)}, u32[]{:S(2)}, u32[]{:S(2)}) %collective-permute-start.2) | collective-permute-done | bytes 32800 | tf_op jit(solution)/shard_map/ppermute | solution.py:499
  14.1 0.0 collective-permute-done.refs_3_
  14.1 0.0 collective-permute-done.1.refs_4_
  14.1 0.4 %rims.1 = (bf16[80,512]{1,0:T(8,128)(2,1)S(1)}, bf16[80,512]{1,0:T(8,128)(2,1)S(1)}, bf16[64,512]{1,0:T(8,128)(2,1)S(1)}) custom-call(bf16[2,64,512]{2,1,0:T(8,128)(2,1)S(1)} %get-tuple-element.29.refs_0_, bf16[6,64,512]{2,1,0:T(8,128)(2,1)S(1)} %get-tuple-element.33.refs_1_, bf16[32,512]{1,0:T(8,128)(2,1)S(1)} %get-tuple-element.36.refs_2_, ...), custom_call_target="tpu_custom_call" | custom-call | tf_op jit(solution)/shard_map/rims/pallas_call | solution.py:534
  14.5 0.1 collective-permute-start.3
  14.5 2.5 %collective-permute-start.4 = (bf16[80,512]{1,0:T(8,128)(2,1)S(1)}, bf16[80,512]{1,0:T(8,128)(2,1)S(1)}, u32[]{:S(2)}, u32[]{:S(2)}) collective-permute-start(bf16[80,512]{1,0:T(8,128)(2,1)S(1)} %get-tuple-element.40), channel_id=1, source_target_pairs={{0,7},{1,2},{2,1},{3,4},{4,3},{5,6},{6,5},{7,0},{8,15},{9,10},{10,... | collective-permute-start | bytes 245768 | tf_op jit(solution)/shard_map/ppermute | solution.py:548
  17.1 0.0 collective-permute-start.6
  17.1 1.1 %collective-permute-start.5 = (bf16[64,512]{1,0:T(8,128)(2,1)S(1)}, bf16[64,512]{1,0:T(8,128)(2,1)S(1)}, u32[]{:S(2)}, u32[]{:S(2)}) collective-permute-start(bf16[64,512]{1,0:T(8,128)(2,1)S(1)} %get-tuple-element.41.refs_0_), channel_id=1, source_target_pairs={{4,0},{5,1},{6,2},{7,3},{0,4},{1,5},{2,6},{3,7},{12,8},{13,9},{14,... | collective-permute-start | bytes 196616 | tf_op jit(solution)/shard_map/ppermute | solution.py:552
  18.2 1.6 %taps.1 = (bf16[512,2048]{1,0:T(8,128)(2,1)S(1)}, bf16[512,2048]{1,0:T(8,128)(2,1)S(1)}, f32[512,512]{1,0:T(8,128)S(1)}) custom-call(bf16[2,64,512]{2,1,0:T(8,128)(2,1)S(1)} %get-tuple-element.29.refs_0_, bf16[6,64,512]{2,1,0:T(8,128)(2,1)S(1)} %get-tuple-element.33.refs_1_, bf16[32,512]{1,0:T(8,128)(2,1)S(1)} %get-tuple-element.36.refs_2_, ...), custom_call_target="tpu_custom_call" | custom-call | tf_op jit(solution)/shard_map/taps/pallas_call | solution.py:557
  19.8 2.5 %collective-permute-done.6.refs_4_ = bf16[64,512]{1,0:T(8,128)(2,1)S(1)} collective-permute-done((bf16[64,512]{1,0:T(8,128)(2,1)S(1)}, bf16[64,512]{1,0:T(8,128)(2,1)S(1)}, u32[]{:S(2)}, u32[]{:S(2)}) %collective-permute-start.6) | collective-permute-done | bytes 65568 | tf_op jit(solution)/shard_map/ppermute | solution.py:552
  22.3 0.0 collective-permute-done.5.refs_3_
  22.3 0.0 collective-permute-done.3.refs_1_.refs_7_
  22.3 0.0 collective-permute-done.4.refs_2_.refs_8_
  22.3 0.1 collective-permute-start.7
  22.4 0.5 %collective-permute-start.8 = (bf16[64,512]{1,0:T(8,128)(2,1)S(1)}, bf16[64,512]{1,0:T(8,128)(2,1)S(1)}, u32[]{:S(2)}, u32[]{:S(2)}) collective-permute-start(bf16[64,512]{1,0:T(8,128)(2,1)S(1)} %collective-permute-done.5.refs_3_), channel_id=1, source_target_pairs={{0,1},{1,0},{2,3},{3,2},{4,5},{5,4},{6,7},{7,6},{8,9},{9,8},{10,11... | collective-permute-start | bytes 196616 | tf_op jit(solution)/shard_map/ppermute | solution.py:545
  22.8 0.1 collective-permute-start.9
  22.9 0.0 copy-done
  22.9 0.8 %early.1.refs_13_ = bf16[2,2048,256]{2,1,0:T(8,128)(2,1)S(1)} custom-call(bf16[64,512]{1,0:T(8,128)(2,1)S(1)} %get-tuple-element.41.refs_0_, bf16[80,512]{1,0:T(8,128)(2,1)S(1)} %collective-permute-done.3.refs_1_.refs_7_, bf16[80,512]{1,0:T(8,128)(2,1)S(1)} %collective-permute-done.4.refs_2_.refs_8_, bf16[64,512]{1,0:T(8,128)(2,1)S(1)} %collective-permute-done.5.refs_3_, ...), custom_call_target="tpu_custom_call" | custom-call | tf_op jit(solution)/shard_map/early/pallas_call | solution.py:590
  23.7 0.0 collective-permute-done.8.refs_10_
  23.8 0.4 %collective-permute-done.9.refs_11_ = bf16[64,512]{1,0:T(8,128)(2,1)S(1)} collective-permute-done((bf16[64,512]{1,0:T(8,128)(2,1)S(1)}, bf16[64,512]{1,0:T(8,128)(2,1)S(1)}, u32[]{:S(2)}, u32[]{:S(2)}) %collective-permute-start.9) | collective-permute-done | bytes 65568 | tf_op jit(solution)/shard_map/ppermute | solution.py:545
  24.1 0.0 collective-permute-done.7.refs_9_
  24.1 4.7 %final.1 = (bf16[512,16,128]{2,1,0:T(8,128)(2,1)}, bf16[2,2048,256]{2,1,0:T(8,128)(2,1)S(1)}) custom-call(bf16[2,64,512]{2,1,0:T(8,128)(2,1)S(1)} %get-tuple-element.29.refs_0_, bf16[6,64,512]{2,1,0:T(8,128)(2,1)S(1)} %get-tuple-element.33.refs_1_, f32[8,512,256]{2,1,0:T(8,128)S(1)} %get-tuple-element.34.refs_2_, ...), custom_call_target="tpu_custom_call", output_to_operand_aliasing={{1}: (13, {})} | custom-call | tf_op jit(solution)/shard_map/final/pallas_call | solution.py:600
Async XLA Ops:
  0.0 8.8 %copy-start.1 = (bf16[8,64,64]{2,1,0:T(8,128)(2,1)S(1)}, bf16[8,64,64]{2,1,0:T(8,128)(2,1)}, u32[]{:S(2)}) copy-start(bf16[8,64,64]{2,1,0:T(8,128)(2,1)} %weights.1) | copy-start | bytes 196612
  2.7 11.4 %collective-permute-start = (bf16[96,512]{1,0:T(8,128)(2,1)S(1)}, bf16[96,512]{1,0:T(8,128)(2,1)S(1)}, u32[]{:S(2)}, u32[]{:S(2)}) collective-permute-start(bf16[96,512]{1,0:T(8,128)(2,1)S(1)} %get-tuple-element.37), channel_id=1, source_target_pairs={{0,8},{8,16},{16,24},{24,0},{1,9},{9,17},{17,25},{25,1},{2,10},{10... | collective-permute-start | bytes 294920 | tf_op jit(solution)/shard_map/ppermute | solution.py:499
  5.8 8.3 %collective-permute-start.1 = (bf16[96,512]{1,0:T(8,128)(2,1)S(1)}, bf16[96,512]{1,0:T(8,128)(2,1)S(1)}, u32[]{:S(2)}, u32[]{:S(2)}) collective-permute-start(bf16[96,512]{1,0:T(8,128)(2,1)S(1)} %get-tuple-element.38), channel_id=1, source_target_pairs={{0,24},{8,0},{16,8},{24,16},{1,25},{9,1},{17,9},{25,17},{2,26},{10... | collective-permute-start | bytes 294920 | tf_op jit(solution)/shard_map/ppermute | solution.py:499
  7.8 6.2 %collective-permute-start.2 = (bf16[32,512]{1,0:T(8,128)(2,1)S(1)}, bf16[32,512]{1,0:T(8,128)(2,1)S(1)}, u32[]{:S(2)}, u32[]{:S(2)}) collective-permute-start(bf16[32,512]{1,0:T(8,128)(2,1)S(1)} %get-tuple-element.36.refs_2_), channel_id=1, source_target_pairs={{0,16},{8,24},{16,0},{24,8},{1,17},{9,25},{17,1},{25,9},{2,18},{10... | collective-permute-start | bytes 98312 | tf_op jit(solution)/shard_map/ppermute | solution.py:499
  11.4 11.5 %copy-start = (bf16[3,2,256,256]{3,2,1,0:T(8,128)(2,1)S(1)}, bf16[3,2,256,256]{3,2,1,0:T(8,128)(2,1)}, u32[]{:S(2)}) copy-start(bf16[3,2,256,256]{3,2,1,0:T(8,128)(2,1)} %constant.2.clone.refs_5_.refs_12_) | copy-start | bytes 2359300
  14.5 7.8 %collective-permute-start.3 = (bf16[80,512]{1,0:T(8,128)(2,1)S(1)}, bf16[80,512]{1,0:T(8,128)(2,1)S(1)}, u32[]{:S(2)}, u32[]{:S(2)}) collective-permute-start(bf16[80,512]{1,0:T(8,128)(2,1)S(1)} %get-tuple-element.39), channel_id=1, source_target_pairs={{0,1},{1,0},{2,3},{3,2},{4,5},{5,4},{6,7},{7,6},{8,9},{9,8},{10,11... | collective-permute-start | bytes 245768 | tf_op jit(solution)/shard_map/ppermute | solution.py:545
  14.5 7.7 %collective-permute-start.4 = (bf16[80,512]{1,0:T(8,128)(2,1)S(1)}, bf16[80,512]{1,0:T(8,128)(2,1)S(1)}, u32[]{:S(2)}, u32[]{:S(2)}) collective-permute-start(bf16[80,512]{1,0:T(8,128)(2,1)S(1)} %get-tuple-element.40), channel_id=1, source_target_pairs={{0,7},{1,2},{2,1},{3,4},{4,3},{5,6},{6,5},{7,0},{8,15},{9,10},{10,... | collective-permute-start | bytes 245768 | tf_op jit(solution)/shard_map/ppermute | solution.py:548
  17.1 5.2 %collective-permute-start.6 = (bf16[64,512]{1,0:T(8,128)(2,1)S(1)}, bf16[64,512]{1,0:T(8,128)(2,1)S(1)}, u32[]{:S(2)}, u32[]{:S(2)}) collective-permute-start(bf16[64,512]{1,0:T(8,128)(2,1)S(1)} %get-tuple-element.41.refs_0_), channel_id=1, source_target_pairs={{6,0},{3,1},{0,2},{5,3},{2,4},{7,5},{4,6},{1,7},{14,8},{11,9},{8,1... | collective-permute-start | bytes 196616 | tf_op jit(solution)/shard_map/ppermute | solution.py:552
  17.1 5.2 %collective-permute-start.5 = (bf16[64,512]{1,0:T(8,128)(2,1)S(1)}, bf16[64,512]{1,0:T(8,128)(2,1)S(1)}, u32[]{:S(2)}, u32[]{:S(2)}) collective-permute-start(bf16[64,512]{1,0:T(8,128)(2,1)S(1)} %get-tuple-element.41.refs_0_), channel_id=1, source_target_pairs={{4,0},{5,1},{6,2},{7,3},{0,4},{1,5},{2,6},{3,7},{12,8},{13,9},{14,... | collective-permute-start | bytes 196616 | tf_op jit(solution)/shard_map/ppermute | solution.py:552
  22.3 1.8 %collective-permute-start.7 = (bf16[80,512]{1,0:T(8,128)(2,1)S(1)}, bf16[80,512]{1,0:T(8,128)(2,1)S(1)}, u32[]{:S(2)}, u32[]{:S(2)}) collective-permute-start(bf16[80,512]{1,0:T(8,128)(2,1)S(1)} %collective-permute-done.4.refs_2_.refs_8_), channel_id=1, source_target_pairs={{0,1},{1,0},{2,3},{3,2},{4,5},{5,4},{6,7},{7,6},{8,9},{9,8},{10,11... | collective-permute-start | bytes 245768 | tf_op jit(solution)/shard_map/ppermute | solution.py:545
  22.4 1.4 %collective-permute-start.8 = (bf16[64,512]{1,0:T(8,128)(2,1)S(1)}, bf16[64,512]{1,0:T(8,128)(2,1)S(1)}, u32[]{:S(2)}, u32[]{:S(2)}) collective-permute-start(bf16[64,512]{1,0:T(8,128)(2,1)S(1)} %collective-permute-done.5.refs_3_), channel_id=1, source_target_pairs={{0,1},{1,0},{2,3},{3,2},{4,5},{5,4},{6,7},{7,6},{8,9},{9,8},{10,11... | collective-permute-start | bytes 196616 | tf_op jit(solution)/shard_map/ppermute | solution.py:545
  22.8 1.3 %collective-permute-start.9 = (bf16[64,512]{1,0:T(8,128)(2,1)S(1)}, bf16[64,512]{1,0:T(8,128)(2,1)S(1)}, u32[]{:S(2)}, u32[]{:S(2)}) collective-permute-start(bf16[64,512]{1,0:T(8,128)(2,1)S(1)} %collective-permute-done.6.refs_4_), channel_id=1, source_target_pairs={{0,1},{1,0},{2,3},{3,2},{4,5},{5,4},{6,7},{7,6},{8,9},{9,8},{10,11... | collective-permute-start | bytes 196616 | tf_op jit(solution)/shard_map/ppermute | solution.py:545

commit v3 on v2

--- a/solution.py
+++ b/solution.py
@@ -107,12 +107,12 @@
 
 
 def gates(values):
-    trivial = values.reshape(8, 4, 8, values.shape[1])[:, 0]
+    trivial = values.reshape(-1, 4, 8, values.shape[1])[:, 0]
     return jax.nn.sigmoid(trivial)
 
 
 def gated(values, scale):
-    split = values.reshape(8, 4, 8, values.shape[1])
+    split = values.reshape(-1, 4, 8, values.shape[1])
     return (split * scale[:, None]).reshape(values.shape)
 
 
@@ -159,7 +159,10 @@
     own_rows = centre.shape[1]
     for j in range(rows_in // 16):
         pay_own[0:16, j * cols_in : (j + 1) * cols_in] = k_local[j * 16 : (j + 1) * 16, :]
-    pay_own[16 : 16 + own_rows, :] = jnp.concatenate([centre[s] for s in range(8)], axis=1)
+    first = 4 * lax.rem(lax.axis_index("col"), 2)
+    part = jnp.concatenate([centre[first + s].astype(F32) for s in range(4)], axis=1)
+    for j in range(own_rows // 8):
+        pay_own[16:24, j * 256 : (j + 1) * 256] = part[j * 8 : (j + 1) * 8].astype(BF16)
     for n in range(chunks):
         copies[n].wait()
         piece = held[n * size : (n + 1) * size].astype(F32)
@@ -173,7 +176,7 @@
         encoded[n, 256:512, :] = result[1]
         pooled[n] = mean
         target[0:64, :] = mean
-        target[64:96, :] = pay_own[...]
+        target[64:88, :] = pay_own[...]
 
 
 def inner_kernel(wide, edges, mixes_in, weights, pooled, halves, mixes_out):
@@ -202,14 +205,20 @@
     rows_in, cols_in = shape
     ends, inner, own, above, below = refs[:5]
     others = refs[5 : 5 + rows - 3]
-    near, far, block, raw = refs[2 + rows :]
+    near, far, block, half, raw, parts = refs[2 + rows :]
     row, col = lax.axis_index("row"), lax.axis_index("col")
+
+    own_rows = 64 // rows
 
     def put(source, start, index):
         for j in range(rows_in // 16):
             raw[index, j * 16 : (j + 1) * 16, :] = source[
                 start : start + 16, j * cols_in : (j + 1) * cols_in
             ]
+        part = source[start + 16 : start + 24, :].astype(F32)
+        for j in range(own_rows // 8):
+            place = pl.multiple_of(index * own_rows + j * 8, 8)
+            parts[pl.ds(place, 8), :] = part[:, j * 256 : (j + 1) * 256]
 
     put(own, 0, row)
     put(above, 64, lax.rem(row + rows - 1, rows))
@@ -226,6 +235,8 @@
     even = lax.rem(col, 2) == 0
     near[0:rows_in, :] = sorted_block
     far[0:rows_in, :] = sorted_block
+    half[...] = jnp.concatenate([parts[0:32, :], parts[32:64, :]], axis=1).astype(BF16)
+    near[rows_in + 16 : rows_in + 48, :] = half[...]
     near[rows_in : rows_in + 16, :] = jnp.where(even, right, left).astype(BF16)
     far[rows_in : rows_in + 16, :] = jnp.where(even, left, right).astype(BF16)
 
@@ -241,9 +252,7 @@
 
 
 def taps_kernel(*refs, rows):
-    ends, inner, own, above, below = refs[:5]
-    others = refs[5 : 5 + rows - 3]
-    left_of, right_of, middle, padded, shifted, centre_rows = refs[2 + rows :]
+    ends, inner, above, below, left_of, right_of, padded, shifted = refs
     row = lax.axis_index("row")
     zero = jnp.zeros((1, 512), F32)
     for line, values in enumerate(all_lines(ends, inner, above, below, row, rows)):
@@ -264,25 +273,6 @@
             left_of[span, base + 256 : base + 512] = minus[:, 256:]
             right_of[span, base : base + 256] = minus[:, :256]
             right_of[span, base + 256 : base + 512] = plus[:, 256:]
-
-    own_rows = 64 // rows
-    table = spread_table()
-
-    def put_centre(values, index):
-        place = pl.multiple_of(index * own_rows, own_rows)
-        centre_rows[pl.ds(place, own_rows), :] = values.astype(F32)
-
-    put_centre(own[16 : 16 + own_rows, :], row)
-    put_centre(above[80 : 80 + own_rows, :], lax.rem(row + rows - 1, rows))
-    put_centre(below[80 : 80 + own_rows, :], lax.rem(row + 1, rows))
-    for n, other in enumerate(others):
-        put_centre(other[16 : 16 + own_rows, :], lax.rem(row + rows - 2 - n, rows))
-    centre = centre_rows[...].astype(BF16)
-    whole = jnp.concatenate(own_lines(ends, inner), axis=0)
-    for group in range(2):
-        span = slice(group * 256, (group + 1) * 256)
-        matrix = mix_matrix(lambda s: centre[:, s * 64 : (s + 1) * 64], table, group)
-        middle[:, span] = dot_nt(whole[:, span], matrix)
 
 
 def pair_steps(cols):
@@ -363,6 +353,29 @@
     return first, [away(mate, a, b, cols) for a, b in steps]
 
 
+def centre_kernel(ends, inner, half, near, centre, *, rows_in):
+    even = lax.rem(lax.axis_index("col"), 2) == 0
+    one = half[...].astype(F32)
+    two = near[rows_in + 16 : rows_in + 48, :].astype(F32)
+    halves = [
+        jnp.where(even, one, two).astype(BF16),
+        jnp.where(even, two, one).astype(BF16),
+    ]
+
+    def piece(s):
+        at = (s % 4) * 64
+        source = halves[s // 4]
+        return jnp.concatenate(
+            [source[:, at : at + 64], source[:, 256 + at : 320 + at]], axis=0
+        )
+
+    table = spread_table()
+    whole = jnp.concatenate(own_lines(ends, inner), axis=0)
+    for group in range(2):
+        span = slice(group * 256, (group + 1) * 256)
+        centre[:, span] = dot_nt(whole[:, span], mix_matrix(piece, table, group))
+
+
 def early_kernel(*refs, cols, rows_in):
     blocks = refs[: 2 + cols // 2 - 1]
     turns, middle, turned = refs[2 + cols // 2 - 1 :]
@@ -381,12 +394,12 @@
     first, second = block_places(col, cols)
     if split:
         relayed, turns = refs[:relays], refs[relays]
-        decoded, middle, turned, coarse, doubled, wide, out, sems = refs[relays + 2 :]
+        decoded, middle, turned, lows, wide, out, sems = refs[relays + 2 :]
         late = [block[0:rows_in, :] for block in relayed]
         places = second
     else:
         held, relayed, turns = refs[: relays], refs[relays : 2 * relays], refs[2 * relays]
-        decoded, kt, middle, turned, coarse, doubled, wide, out, sems = refs[2 * relays + 1 :]
+        decoded, kt, middle, turned, lows, wide, out, sems = refs[2 * relays + 1 :]
         for block, index in zip((held[0], near, far) + held[1:] + relayed, first + second):
             start = pl.multiple_of(index * rows_in, rows_in)
             kt[pl.ds(start, rows_in), :] = block[0:rows_in, :]
@@ -422,45 +435,42 @@
     scale = jnp.concatenate(scales + scales, axis=1)
     total = jnp.concatenate(totals, axis=1)
     own = jnp.concatenate(own_lines(ends, inner), axis=0).astype(F32)
-    coarse[...] = (own + total * scale).astype(BF16).astype(F32).reshape(8, 64, 512)
-    matrices = [mixes[group] for group in range(2)]
-
-    def step(line, carry):
-        values = coarse[line]
-        for quarter in range(4):
-            lanes = values[:, quarter * 128 : quarter * 128 + 128]
-            doubled[line, pl.ds(quarter * 128, 64, stride=2), :] = lanes
-            doubled[line, pl.ds(quarter * 128 + 1, 64, stride=2), :] = lanes
-        fine = jnp.concatenate(
-            [doubled[line, quarter * 128 : quarter * 128 + 128, :] for quarter in range(4)], axis=1
-        ).astype(BF16)
-        scale = None
-        for group in range(2):
-            span = slice(group * 256, (group + 1) * 256)
-            low = dot_nt(matrices[group], fine[:, span])
-            y = halves[line, span, :] + jnp.concatenate([low, low], axis=1)
-            if group == 0:
-                scale = gates(y)
-            d = gated(y, scale)
-            for half in range(2):
-                for c in range(8):
-                    for b in range(4):
-                        start = row_start(c, COMPONENTS[group][b]) + 2 * line + half
-                        at = c * 32 + b * 8
-                        wide[pl.ds(start, 8, stride=PITCH), :] = d[
-                            at : at + 8, half * 128 : half * 128 + 128
-                        ]
-        return carry
-
-    lax.fori_loop(0, 8, step, 0, unroll=UNROLL)
+    bottleneck = (own + total * scale).astype(BF16)
+    for group in range(2):
+        span = slice(group * 256, (group + 1) * 256)
+        for part in range(2):
+            lows[part, span, :] = dot_nt(
+                mixes[group], bottleneck[part * 256 : (part + 1) * 256, span]
+            )
     size = 512 // chunks
+    per = 8 // chunks
     copies = []
     for n in range(chunks):
-        span = pl.ds(n * size, size)
+        for line in range(8):
+            scale = None
+            for group in range(2):
+                at = group * 256 + n * per * 32
+                index = (iota((per * 32, 128), 1) >> 1) + (line % 2) * 64
+                column = ((line % 4) // 2) * 128
+                low = lows[line // 4, at : at + per * 32, column : column + 128]
+                low = jnp.take_along_axis(low, index, axis=1)
+                y = halves[line, at : at + per * 32, :] + jnp.concatenate([low, low], axis=1)
+                if group == 0:
+                    scale = gates(y)
+                d = gated(y, scale)
+                for half in range(2):
+                    for c in range(per):
+                        for b in range(4):
+                            start = row_start(n * per + c, COMPONENTS[group][b]) + 2 * line + half
+                            at = c * 32 + b * 8
+                            wide[pl.ds(start, 8, stride=PITCH), :] = d[
+                                at : at + 8, half * 128 : half * 128 + 128
+                            ]
         for m in range(size // 8):
             at = (n * size // 8 + m) * PITCH
             piece = wide[at : at + 128, :].astype(BF16)
             out[n * size + m * 8 : n * size + m * 8 + 8] = piece.reshape(8, 16, 128)
+        span = pl.ds(n * size, size)
         copies.append(pltpu.make_async_copy(out.at[span], decoded.at[span], sems.at[n]))
         copies[-1].start()
     for copy in copies:
@@ -507,7 +517,7 @@
         (VMEM,) * 7,
         (
             arr(64 * PITCH, 128, dtype=F32), arr(2, 512, 256), arr(2, 64, 512),
-            arr(96, 512), arr(96, 512), arr(32, 512), arr(2, 256, 256),
+            arr(88, 512), arr(88, 512), arr(24, 512), arr(2, 256, 256),
         ),
         [
             pltpu.VMEM((512, 16, 128), BF16),
@@ -531,13 +541,13 @@
         [],
         24,
     )(wide, edges, mixes, dec_mix)
-    near_out, far_out, block = call(
+    near_out, far_out, block, half = call(
         functools.partial(rims_kernel, rows=rows, shape=shape),
         "rims",
         [VMEM] * (2 + rows),
-        (VMEM,) * 3,
-        (arr(shape[0] + 16, 512), arr(shape[0] + 16, 512), arr(shape[0], 512)),
-        [pltpu.VMEM((rows,) + shape, BF16)],
+        (VMEM,) * 4,
+        (arr(shape[0] + 48, 512), arr(shape[0] + 16, 512), arr(shape[0], 512), arr(32, 512)),
+        [pltpu.VMEM((rows,) + shape, BF16), pltpu.VMEM((64, 256), F32)],
         16,
     )(ends, inner, pay_own, above, below, *others)
 
@@ -554,19 +564,24 @@
         )
         for even, odd in pair_steps(cols)
     ]
-    left_of, right_of, centre = call(
+    left_of, right_of = call(
         functools.partial(taps_kernel, rows=rows),
         "taps",
-        [VMEM] * (2 + rows),
-        (VMEM,) * 3,
-        (arr(512, 2048), arr(512, 2048), arr(512, 512, dtype=F32)),
-        [
-            pltpu.VMEM((10, 80, 512), F32),
-            pltpu.VMEM((3, 10, 64, 512), BF16),
-            pltpu.VMEM((64, 512), F32),
-        ],
+        [VMEM] * 4,
+        (VMEM,) * 2,
+        (arr(512, 2048), arr(512, 2048)),
+        [pltpu.VMEM((10, 80, 512), F32), pltpu.VMEM((3, 10, 64, 512), BF16)],
         24,
-    )(ends, inner, pay_own, above, below, *others)
+    )(ends, inner, above, below)
+    centre = call(
+        functools.partial(centre_kernel, rows_in=shape[0]),
+        "centre",
+        [VMEM] * 4,
+        VMEM,
+        arr(512, 512, dtype=F32),
+        [],
+        16,
+    )(ends, inner, half, near)
     near, far, near_pairs, left_of, right_of, centre = lax.optimization_barrier(
         (near, far, near_pairs, left_of, right_of, centre)
     )
@@ -574,8 +589,7 @@
     split = shape[0] == 64
     scratch = [
         pltpu.VMEM((2048, 128), F32),
-        pltpu.VMEM((8, 64, 512), F32),
-        pltpu.VMEM((8, 512, 128), F32),
+        pltpu.VMEM((2, 512, 256), F32),
         pltpu.VMEM((64 * PITCH, 128), F32),
         pltpu.VMEM((512, 16, 128), BF16),
         pltpu.SemaphoreType.DMA((chunks,)),

time: 29 us -> 28 us (0.966)
  waiting for transfers between devices: 5.56 us -> 4.78 us
    ppermute x3, waiting for transfers between devices: 2.66 us -> 1.95 us  [shift(): lax.ppermute(array, 'row', [(i, (i + step) % rows) for i in range(rows)])]
    pallas_call x1, Pallas kernels: 4.74 us -> 4.45 us  [per_device(): call(kernel, 'final', [VMEM] * len(operands), (HBM, VMEM), (result, arr(2...]
    pallas_call x1 -> x2, Pallas kernels: 1.56 us -> 1.64 us  [the longest x1 0.88 us: per_device(): call(functools.partial(centre_kernel, rows_in=shape[0]), 'centre', [VMEM]...]
  transfers between devices with their start and end apart: 10 -> 10, of which waited for: 3 -> 3; matrix products, arithmetic and copies ran while one was open for 0% -> 0% of each run, Pallas kernels for 17% -> 18%
where the time goes in v3:
time: 28 us; the launch traced here: 27.8 us
  Pallas kernels  12.5 us (45%)
  starting transfers between devices  10.4 us (37%)
  waiting for transfers between devices  4.78 us (17%)
    ppermute x3, starting transfers between devices, shift(): lax.ppermute(array, 'row', [(i, (i + step) % rows) for i in range(rows)])  6.12 us
    pallas_call x1, Pallas kernels, per_device(): call(kernel, 'final', [VMEM] * len(operands), (HBM, VMEM), (result, arr(2...  4.45 us
    pallas_call x1, Pallas kernels, per_device(): call(functools.partial(edge_kernel, chunks=chunks), 'edges', [HBM] * 4, (...  2.68 us
    pallas_call x1, Pallas kernels, per_device(): call(inner_kernel, 'inner', [VMEM] * 4, (VMEM,) * 3, (arr(6, 64, 512), ar...  2.61 us
    ppermute x1, starting transfers between devices, per_device(): lax.ppermute(far_out, 'col', [(i, (i - 1 if i % 2 == 0 else i + 1) % cols...  2.56 us
    ppermute x2, waiting for transfers between devices, per_device(): lax.ppermute(block, 'col', [((i + (even, odd)[i % 2]) % cols, i) for i in...  2.42 us
    ppermute x3, waiting for transfers between devices, shift(): lax.ppermute(array, 'row', [(i, (i + step) % rows) for i in range(rows)])  1.95 us
    ppermute x2, starting transfers between devices, per_device(): lax.ppermute(block, 'col', [((i + (even, odd)[i % 2]) % cols, i) for i in...  1.09 us
  transfers between devices with their start and end apart: 10, of which 3 were waited for; matrix products, arithmetic and copies ran while one was open for 0% of the time, Pallas kernels for 18%

profile of v3, /device:TPU:0, one launch (start us, length us, event | category | flops | bytes accessed | tf_op | source)
XLA Modules:
  0.0 27.8 jit_solution(17400279460159588438)
XLA Ops:
  0.0 0.0 copy-start.1
  0.0 2.7 %edges.1 = (f32[8704,128]{1,0:T(8,128)S(1)}, bf16[2,512,256]{2,1,0:T(8,128)(2,1)S(1)}, bf16[2,64,512]{2,1,0:T(8,128)(2,1)S(1)}, bf16[88,512]{1,0:T(8,128)(2,1)S(...) custom-call(bf16[512,16,128]{2,1,0:T(8,128)(2,1)} %fields_in.1, ...), custom_call_target="tpu_custom_call" | custom-call | tf_op jit(solution)/shard_map/edges/pallas_call | solution.py:513
  2.7 3.1 %collective-permute-start = (bf16[88,512]{1,0:T(8,128)(2,1)S(1)}, bf16[88,512]{1,0:T(8,128)(2,1)S(1)}, u32[]{:S(2)}, u32[]{:S(2)}) collective-permute-start(bf16[88,512]{1,0:T(8,128)(2,1)S(1)} %get-tuple-element.37), channel_id=1, source_target_pairs={{0,8},{8,16},{16,24},{24,0},{1,9},{9,17},{17,25},{25,1},{2,10},{10... | collective-permute-start | bytes 270344 | tf_op jit(solution)/shard_map/ppermute | solution.py:509
  5.8 2.1 %collective-permute-start.1 = (bf16[88,512]{1,0:T(8,128)(2,1)S(1)}, bf16[88,512]{1,0:T(8,128)(2,1)S(1)}, u32[]{:S(2)}, u32[]{:S(2)}) collective-permute-start(bf16[88,512]{1,0:T(8,128)(2,1)S(1)} %get-tuple-element.38), channel_id=1, source_target_pairs={{0,24},{8,0},{16,8},{24,16},{1,25},{9,1},{17,9},{25,17},{2,26},{10... | collective-permute-start | bytes 270344 | tf_op jit(solution)/shard_map/ppermute | solution.py:509
  7.9 1.0 %collective-permute-start.2 = (bf16[24,512]{1,0:T(8,128)(2,1)S(1)}, bf16[24,512]{1,0:T(8,128)(2,1)S(1)}, u32[]{:S(2)}, u32[]{:S(2)}) collective-permute-start(bf16[24,512]{1,0:T(8,128)(2,1)S(1)} %get-tuple-element.36.refs_2_), channel_id=1, source_target_pairs={{0,16},{8,24},{16,0},{24,8},{1,17},{9,25},{17,1},{25,9},{2,18},{10... | collective-permute-start | bytes 73736 | tf_op jit(solution)/shard_map/ppermute | solution.py:509
  8.8 0.0 copy-done.1
  8.8 2.6 %inner.1 = (bf16[6,64,512]{2,1,0:T(8,128)(2,1)S(1)}, f32[8,512,256]{2,1,0:T(8,128)S(1)}, bf16[2,256,256]{2,1,0:T(8,128)(2,1)S(1)}) custom-call(f32[8704,128]{1,0:T(8,128)S(1)} %get-tuple-element.30.wide, bf16[2,512,256]{2,1,0:T(8,128)(2,1)S(1)} %get-tuple-element.31.edges, bf16[2,256,256]{2,1,0:T(8,128)(2,1)S(1)} %get-tuple-element.32.mixes_in, ...), custom_call_target="tpu_custom_call" | custom-call | tf_op jit(solution)/shard_map/inner/pallas_call | solution.py:535
  11.4 0.0 copy-start
  11.4 1.9 %collective-permute-done.2.refs_5_ = bf16[24,512]{1,0:T(8,128)(2,1)S(1)} collective-permute-done((bf16[24,512]{1,0:T(8,128)(2,1)S(1)}, bf16[24,512]{1,0:T(8,128)(2,1)S(1)}, u32[]{:S(2)}, u32[]{:S(2)}) %collective-permute-start.2) | collective-permute-done | bytes 24608 | tf_op jit(solution)/shard_map/ppermute | solution.py:509
  13.4 0.0 collective-permute-done.refs_3_.refs_2_
  13.4 0.0 collective-permute-done.1.refs_4_.refs_3_
  13.4 0.4 %rims.1 = (bf16[112,512]{1,0:T(8,128)(2,1)S(1)}, bf16[80,512]{1,0:T(8,128)(2,1)S(1)}, bf16[64,512]{1,0:T(8,128)(2,1)S(1)}, bf16[32,512]{1,0:T(8,128)(2,1)S(1)}) custom-call(bf16[2,64,512]{2,1,0:T(8,128)(2,1)S(1)} %get-tuple-element.29.refs_0_.ends, bf16[6,64,512]{2,1,0:T(8,128)(2,1)S(1)} %get-tuple-element.33.refs_1_.inner, ...), custom_call_target="tpu_custom_call" | custom-call | tf_op jit(solution)/shard_map/rims/pallas_call | solution.py:544
  13.8 0.1 collective-permute-start.3
  13.9 2.6 %collective-permute-start.4 = (bf16[80,512]{1,0:T(8,128)(2,1)S(1)}, bf16[80,512]{1,0:T(8,128)(2,1)S(1)}, u32[]{:S(2)}, u32[]{:S(2)}) collective-permute-start(bf16[80,512]{1,0:T(8,128)(2,1)S(1)} %get-tuple-element.40), channel_id=1, source_target_pairs={{0,7},{1,2},{2,1},{3,4},{4,3},{5,6},{6,5},{7,0},{8,15},{9,10},{10,... | collective-permute-start | bytes 245768 | tf_op jit(solution)/shard_map/ppermute | solution.py:558
  16.4 0.0 collective-permute-start.6
  16.4 1.1 %collective-permute-start.5 = (bf16[64,512]{1,0:T(8,128)(2,1)S(1)}, bf16[64,512]{1,0:T(8,128)(2,1)S(1)}, u32[]{:S(2)}, u32[]{:S(2)}) collective-permute-start(bf16[64,512]{1,0:T(8,128)(2,1)S(1)} %get-tuple-element.41.refs_0_), channel_id=1, source_target_pairs={{4,0},{5,1},{6,2},{7,3},{0,4},{1,5},{2,6},{3,7},{12,8},{13,9},{14,... | collective-permute-start | bytes 196616 | tf_op jit(solution)/shard_map/ppermute | solution.py:562
  17.5 0.8 %taps.1 = (bf16[512,2048]{1,0:T(8,128)(2,1)S(1)}, bf16[512,2048]{1,0:T(8,128)(2,1)S(1)}) custom-call(bf16[2,64,512]{2,1,0:T(8,128)(2,1)S(1)} %get-tuple-element.29.refs_0_.ends, bf16[6,64,512]{2,1,0:T(8,128)(2,1)S(1)} %get-tuple-element.33.refs_1_.inner, bf16[88,512]{1,0:T(8,128)(2,1)S(1)} %collective-permute-done.refs_3_.refs_2_, ...), custom_call_target="tpu_custom_call" | custom-call | tf_op jit(solution)/shard_map/taps/pallas_call | solution.py:567
  18.3 0.0 collective-permute-done.3.near.refs_1_.refs_7_
  18.3 0.9 %centre.1.refs_6_ = f32[512,512]{1,0:T(8,128)S(1)} custom-call(bf16[2,64,512]{2,1,0:T(8,128)(2,1)S(1)} %get-tuple-element.29.refs_0_.ends, bf16[6,64,512]{2,1,0:T(8,128)(2,1)S(1)} %get-tuple-element.33.refs_1_.inner, bf16[32,512]{1,0:T(8,128)(2,1)S(1)} %get-tuple-element.44.half, bf16[112,512]{1,0:T(8,128)(2,1)S(1)} %collective-permute-done.3.near.refs_1_.refs_7_), custom_call_target="tpu_custom_call" | custom-call | tf_op jit(solution)/shard_map/centre/pallas_call | solution.py:576
  19.2 2.4 %collective-permute-done.6.refs_4_ = bf16[64,512]{1,0:T(8,128)(2,1)S(1)} collective-permute-done((bf16[64,512]{1,0:T(8,128)(2,1)S(1)}, bf16[64,512]{1,0:T(8,128)(2,1)S(1)}, u32[]{:S(2)}, u32[]{:S(2)}) %collective-permute-start.6) | collective-permute-done | bytes 65568 | tf_op jit(solution)/shard_map/ppermute | solution.py:562
  21.6 0.0 collective-permute-done.5.refs_3_
  21.6 0.0 collective-permute-done.4.refs_2_.refs_8_
  21.6 0.0 collective-permute-start.7
  21.6 0.5 %collective-permute-start.8 = (bf16[64,512]{1,0:T(8,128)(2,1)S(1)}, bf16[64,512]{1,0:T(8,128)(2,1)S(1)}, u32[]{:S(2)}, u32[]{:S(2)}) collective-permute-start(bf16[64,512]{1,0:T(8,128)(2,1)S(1)} %collective-permute-done.5.refs_3_), channel_id=1, source_target_pairs={{0,1},{1,0},{2,3},{3,2},{4,5},{5,4},{6,7},{7,6},{8,9},{9,8},{10,11... | collective-permute-start | bytes 196616 | tf_op jit(solution)/shard_map/ppermute | solution.py:555
  22.1 0.1 collective-permute-start.9
  22.2 0.0 copy-done
  22.2 0.8 %early.1.refs_13_ = bf16[2,2048,256]{2,1,0:T(8,128)(2,1)S(1)} custom-call(bf16[64,512]{1,0:T(8,128)(2,1)S(1)} %get-tuple-element.41.refs_0_, bf16[112,512]{1,0:T(8,128)(2,1)S(1)} %collective-permute-done.3.near.refs_1_.refs_7_, bf16[80,512]{1,0:T(8,128)(2,1)S(1)} %collective-permute-done.4.refs_2_.refs_8_, ...), custom_call_target="tpu_custom_call" | custom-call | tf_op jit(solution)/shard_map/early/pallas_call | solution.py:604
  23.0 0.0 collective-permute-done.8.refs_10_
  23.0 0.4 %collective-permute-done.9.refs_11_ = bf16[64,512]{1,0:T(8,128)(2,1)S(1)} collective-permute-done((bf16[64,512]{1,0:T(8,128)(2,1)S(1)}, bf16[64,512]{1,0:T(8,128)(2,1)S(1)}, u32[]{:S(2)}, u32[]{:S(2)}) %collective-permute-start.9) | collective-permute-done | bytes 65568 | tf_op jit(solution)/shard_map/ppermute | solution.py:555
  23.4 0.0 collective-permute-done.7.refs_9_
  23.4 4.5 %final.1 = (bf16[512,16,128]{2,1,0:T(8,128)(2,1)}, bf16[2,2048,256]{2,1,0:T(8,128)(2,1)S(1)}) custom-call(bf16[2,64,512]{2,1,0:T(8,128)(2,1)S(1)} %get-tuple-element.29.refs_0_.ends, bf16[6,64,512]{2,1,0:T(8,128)(2,1)S(1)} %get-tuple-element.33.refs_1_.inner, f32[8,512,256]{2,1,0:T(8,128)S(1)} %get-tuple-element.34.refs_2_, ...), custom_call_target="tpu_custom_call", output_to_operand_aliasing={{1}: (13, {})} | custom-call | tf_op jit(solution)/shard_map/final/pallas_call | solution.py:614
Async XLA Ops:
  0.0 8.8 %copy-start.1 = (bf16[8,64,64]{2,1,0:T(8,128)(2,1)S(1)}, bf16[8,64,64]{2,1,0:T(8,128)(2,1)}, u32[]{:S(2)}) copy-start(bf16[8,64,64]{2,1,0:T(8,128)(2,1)} %weights.1) | copy-start | bytes 196612
  2.7 10.7 %collective-permute-start = (bf16[88,512]{1,0:T(8,128)(2,1)S(1)}, bf16[88,512]{1,0:T(8,128)(2,1)S(1)}, u32[]{:S(2)}, u32[]{:S(2)}) collective-permute-start(bf16[88,512]{1,0:T(8,128)(2,1)S(1)} %get-tuple-element.37), channel_id=1, source_target_pairs={{0,8},{8,16},{16,24},{24,0},{1,9},{9,17},{17,25},{25,1},{2,10},{10... | collective-permute-start | bytes 270344 | tf_op jit(solution)/shard_map/ppermute | solution.py:509
  5.8 7.6 %collective-permute-start.1 = (bf16[88,512]{1,0:T(8,128)(2,1)S(1)}, bf16[88,512]{1,0:T(8,128)(2,1)S(1)}, u32[]{:S(2)}, u32[]{:S(2)}) collective-permute-start(bf16[88,512]{1,0:T(8,128)(2,1)S(1)} %get-tuple-element.38), channel_id=1, source_target_pairs={{0,24},{8,0},{16,8},{24,16},{1,25},{9,1},{17,9},{25,17},{2,26},{10... | collective-permute-start | bytes 270344 | tf_op jit(solution)/shard_map/ppermute | solution.py:509
  7.9 5.5 %collective-permute-start.2 = (bf16[24,512]{1,0:T(8,128)(2,1)S(1)}, bf16[24,512]{1,0:T(8,128)(2,1)S(1)}, u32[]{:S(2)}, u32[]{:S(2)}) collective-permute-start(bf16[24,512]{1,0:T(8,128)(2,1)S(1)} %get-tuple-element.36.refs_2_), channel_id=1, source_target_pairs={{0,16},{8,24},{16,0},{24,8},{1,17},{9,25},{17,1},{25,9},{2,18},{10... | collective-permute-start | bytes 73736 | tf_op jit(solution)/shard_map/ppermute | solution.py:509
  11.4 10.7 %copy-start = (bf16[3,2,256,256]{3,2,1,0:T(8,128)(2,1)S(1)}, bf16[3,2,256,256]{3,2,1,0:T(8,128)(2,1)}, u32[]{:S(2)}) copy-start(bf16[3,2,256,256]{3,2,1,0:T(8,128)(2,1)} %constant.2.clone.refs_5_.refs_12_) | copy-start | bytes 2359300
  13.8 4.5 %collective-permute-start.3 = (bf16[112,512]{1,0:T(8,128)(2,1)S(1)}, bf16[112,512]{1,0:T(8,128)(2,1)S(1)}, u32[]{:S(2)}, u32[]{:S(2)}) collective-permute-start(bf16[112,512]{1,0:T(8,128)(2,1)S(1)} %get-tuple-element.39), channel_id=1, source_target_pairs={{0,1},{1,0},{2,3},{3,2},{4,5},{5,4},{6,7},{7,6},{8,9},{9,8},{10,11... | collective-permute-start | bytes 344072 | tf_op jit(solution)/shard_map/ppermute | solution.py:555
  13.9 7.7 %collective-permute-start.4 = (bf16[80,512]{1,0:T(8,128)(2,1)S(1)}, bf16[80,512]{1,0:T(8,128)(2,1)S(1)}, u32[]{:S(2)}, u32[]{:S(2)}) collective-permute-start(bf16[80,512]{1,0:T(8,128)(2,1)S(1)} %get-tuple-element.40), channel_id=1, source_target_pairs={{0,7},{1,2},{2,1},{3,4},{4,3},{5,6},{6,5},{7,0},{8,15},{9,10},{10,... | collective-permute-start | bytes 245768 | tf_op jit(solution)/shard_map/ppermute | solution.py:558
  16.4 5.2 %collective-permute-start.6 = (bf16[64,512]{1,0:T(8,128)(2,1)S(1)}, bf16[64,512]{1,0:T(8,128)(2,1)S(1)}, u32[]{:S(2)}, u32[]{:S(2)}) collective-permute-start(bf16[64,512]{1,0:T(8,128)(2,1)S(1)} %get-tuple-element.41.refs_0_), channel_id=1, source_target_pairs={{6,0},{3,1},{0,2},{5,3},{2,4},{7,5},{4,6},{1,7},{14,8},{11,9},{8,1... | collective-permute-start | bytes 196616 | tf_op jit(solution)/shard_map/ppermute | solution.py:562
  16.4 5.2 %collective-permute-start.5 = (bf16[64,512]{1,0:T(8,128)(2,1)S(1)}, bf16[64,512]{1,0:T(8,128)(2,1)S(1)}, u32[]{:S(2)}, u32[]{:S(2)}) collective-permute-start(bf16[64,512]{1,0:T(8,128)(2,1)S(1)} %get-tuple-element.41.refs_0_), channel_id=1, source_target_pairs={{4,0},{5,1},{6,2},{7,3},{0,4},{1,5},{2,6},{3,7},{12,8},{13,9},{14,... | collective-permute-start | bytes 196616 | tf_op jit(solution)/shard_map/ppermute | solution.py:562
  21.6 1.8 %collective-permute-start.7 = (bf16[80,512]{1,0:T(8,128)(2,1)S(1)}, bf16[80,512]{1,0:T(8,128)(2,1)S(1)}, u32[]{:S(2)}, u32[]{:S(2)}) collective-permute-start(bf16[80,512]{1,0:T(8,128)(2,1)S(1)} %collective-permute-done.4.refs_2_.refs_8_), channel_id=1, source_target_pairs={{0,1},{1,0},{2,3},{3,2},{4,5},{5,4},{6,7},{7,6},{8,9},{9,8},{10,11... | collective-permute-start | bytes 245768 | tf_op jit(solution)/shard_map/ppermute | solution.py:555
  21.6 1.4 %collective-permute-start.8 = (bf16[64,512]{1,0:T(8,128)(2,1)S(1)}, bf16[64,512]{1,0:T(8,128)(2,1)S(1)}, u32[]{:S(2)}, u32[]{:S(2)}) collective-permute-start(bf16[64,512]{1,0:T(8,128)(2,1)S(1)} %collective-permute-done.5.refs_3_), channel_id=1, source_target_pairs={{0,1},{1,0},{2,3},{3,2},{4,5},{5,4},{6,7},{7,6},{8,9},{9,8},{10,11... | collective-permute-start | bytes 196616 | tf_op jit(solution)/shard_map/ppermute | solution.py:555
  22.1 1.3 %collective-permute-start.9 = (bf16[64,512]{1,0:T(8,128)(2,1)S(1)}, bf16[64,512]{1,0:T(8,128)(2,1)S(1)}, u32[]{:S(2)}, u32[]{:S(2)}) collective-permute-start(bf16[64,512]{1,0:T(8,128)(2,1)S(1)} %collective-permute-done.6.refs_4_), channel_id=1, source_target_pairs={{0,1},{1,0},{2,3},{3,2},{4,5},{5,4},{6,7},{7,6},{8,9},{9,8},{10,11... | collective-permute-start | bytes 196616 | tf_op jit(solution)/shard_map/ppermute | solution.py:555

commit v4 on v3

--- a/solution.py
+++ b/solution.py
@@ -147,7 +147,7 @@
     for n in range(chunks):
         span = pl.ds(n * size, size)
         copies.append(pltpu.make_async_copy(fields_in.at[span], held.at[span], sems.at[n]))
-        copies[-1].start()
+        copies[-1].start(priority=n % 2)
     table = spread_table()
     pool_t = pool_table()
     for start in starts:
@@ -582,10 +582,10 @@
         [],
         16,
     )(ends, inner, half, near)
-    near, far, near_pairs, left_of, right_of, centre = lax.optimization_barrier(
-        (near, far, near_pairs, left_of, right_of, centre)
-    )
-    relayed = [mates(array) for array in [far] + near_pairs]
+    def relay(array):
+        return mates(lax.optimization_barrier((array, left_of, right_of, centre))[0])
+
+    relayed = [relay(array) for array in [far] + near_pairs]
     split = shape[0] == 64
     scratch = [
         pltpu.VMEM((2048, 128), F32),

time: 28 us -> 27.4 us (0.979)
  waiting for transfers between devices: 4.78 us -> 3.98 us
  starting transfers between devices: 10.4 us -> 10.8 us
    ppermute x2, waiting for transfers between devices: 2.42 us -> 1.91 us  [per_device(): lax.ppermute(block, 'col', [((i + (even, odd)[i % 2]) % cols, i) for i in...]
    ppermute x4, starting transfers between devices: 0.65 us -> 1.06 us  [mates(): return lax.ppermute(array, 'col', [(i, i ^ 1) for i in range(cols)])]
    ppermute x4, waiting for transfers between devices: 0.4 us -> 0.11 us  [mates(): return lax.ppermute(array, 'col', [(i, i ^ 1) for i in range(cols)])]
where the time goes in v4:
time: 27.4 us; the launch traced here: 27.3 us
  Pallas kernels  12.4 us (45%)
  starting transfers between devices  10.8 us (39%)
  waiting for transfers between devices  3.98 us (15%)
    ppermute x3, starting transfers between devices, shift(): lax.ppermute(array, 'row', [(i, (i + step) % rows) for i in range(rows)])  6.12 us
    pallas_call x1, Pallas kernels, per_device(): call(kernel, 'final', [VMEM] * len(operands), (HBM, VMEM), (result, arr(2...  4.45 us
    pallas_call x1, Pallas kernels, per_device(): call(inner_kernel, 'inner', [VMEM] * 4, (VMEM,) * 3, (arr(6, 64, 512), ar...  2.62 us
    ppermute x1, starting transfers between devices, per_device(): lax.ppermute(far_out, 'col', [(i, (i - 1 if i % 2 == 0 else i + 1) % cols...  2.54 us
    pallas_call x1, Pallas kernels, per_device(): call(functools.partial(edge_kernel, chunks=chunks), 'edges', [HBM] * 4, (...  2.52 us
    ppermute x3, waiting for transfers between devices, shift(): lax.ppermute(array, 'row', [(i, (i + step) % rows) for i in range(rows)])  1.96 us
    ppermute x2, waiting for transfers between devices, per_device(): lax.ppermute(block, 'col', [((i + (even, odd)[i % 2]) % cols, i) for i in...  1.91 us
    ppermute x2, starting transfers between devices, per_device(): lax.ppermute(block, 'col', [((i + (even, odd)[i % 2]) % cols, i) for i in...  1.11 us
  transfers between devices with their start and end apart: 10, of which 3 were waited for; matrix products, arithmetic and copies ran while one was open for 0% of the time, Pallas kernels for 18%

profile of v4, /device:TPU:0, one launch (start us, length us, event | category | flops | bytes accessed | tf_op | source)
XLA Modules:
  0.0 27.3 jit_solution(13265936732693369106)
XLA Ops:
  0.0 0.0 copy-start.1
  0.0 2.5 %edges.1 = (f32[8704,128]{1,0:T(8,128)S(1)}, bf16[2,512,256]{2,1,0:T(8,128)(2,1)S(1)}, bf16[2,64,512]{2,1,0:T(8,128)(2,1)S(1)}, bf16[88,512]{1,0:T(8,128)(2,1)S(...) custom-call(bf16[512,16,128]{2,1,0:T(8,128)(2,1)} %fields_in.1, ...), custom_call_target="tpu_custom_call" | custom-call | tf_op jit(solution)/shard_map/edges/pallas_call | solution.py:513
  2.5 3.1 %collective-permute-start = (bf16[88,512]{1,0:T(8,128)(2,1)S(1)}, bf16[88,512]{1,0:T(8,128)(2,1)S(1)}, u32[]{:S(2)}, u32[]{:S(2)}) collective-permute-start(bf16[88,512]{1,0:T(8,128)(2,1)S(1)} %get-tuple-element.32), channel_id=1, source_target_pairs={{0,8},{8,16},{16,24},{24,0},{1,9},{9,17},{17,25},{25,1},{2,10},{10... | collective-permute-start | bytes 270344 | tf_op jit(solution)/shard_map/ppermute | solution.py:509
  5.6 2.1 %collective-permute-start.1 = (bf16[88,512]{1,0:T(8,128)(2,1)S(1)}, bf16[88,512]{1,0:T(8,128)(2,1)S(1)}, u32[]{:S(2)}, u32[]{:S(2)}) collective-permute-start(bf16[88,512]{1,0:T(8,128)(2,1)S(1)} %get-tuple-element.33), channel_id=1, source_target_pairs={{0,24},{8,0},{16,8},{24,16},{1,25},{9,1},{17,9},{25,17},{2,26},{10... | collective-permute-start | bytes 270344 | tf_op jit(solution)/shard_map/ppermute | solution.py:509
  7.7 0.9 %collective-permute-start.2 = (bf16[24,512]{1,0:T(8,128)(2,1)S(1)}, bf16[24,512]{1,0:T(8,128)(2,1)S(1)}, u32[]{:S(2)}, u32[]{:S(2)}) collective-permute-start(bf16[24,512]{1,0:T(8,128)(2,1)S(1)} %get-tuple-element.36.refs_2_), channel_id=1, source_target_pairs={{0,16},{8,24},{16,0},{24,8},{1,17},{9,25},{17,1},{25,9},{2,18},{10... | collective-permute-start | bytes 73736 | tf_op jit(solution)/shard_map/ppermute | solution.py:509
  8.6 0.0 copy-done.1
  8.7 2.6 %inner.1 = (bf16[6,64,512]{2,1,0:T(8,128)(2,1)S(1)}, f32[8,512,256]{2,1,0:T(8,128)S(1)}, bf16[2,256,256]{2,1,0:T(8,128)(2,1)S(1)}) custom-call(f32[8704,128]{1,0:T(8,128)S(1)} %get-tuple-element.26.wide, bf16[2,512,256]{2,1,0:T(8,128)(2,1)S(1)} %get-tuple-element.27.edges, bf16[2,256,256]{2,1,0:T(8,128)(2,1)S(1)} %get-tuple-element.28.mixes_in, ...), custom_call_target="tpu_custom_call" | custom-call | tf_op jit(solution)/shard_map/inner/pallas_call | solution.py:535
  11.3 0.0 copy-start
  11.3 2.0 %collective-permute-done.2.refs_5_ = bf16[24,512]{1,0:T(8,128)(2,1)S(1)} collective-permute-done((bf16[24,512]{1,0:T(8,128)(2,1)S(1)}, bf16[24,512]{1,0:T(8,128)(2,1)S(1)}, u32[]{:S(2)}, u32[]{:S(2)}) %collective-permute-start.2) | collective-permute-done | bytes 24608 | tf_op jit(solution)/shard_map/ppermute | solution.py:509
  13.2 0.0 collective-permute-done.refs_2_.refs_3_
  13.2 0.0 collective-permute-done.1.refs_3_.refs_4_
  13.3 0.4 %rims.1 = (bf16[112,512]{1,0:T(8,128)(2,1)S(1)}, bf16[80,512]{1,0:T(8,128)(2,1)S(1)}, bf16[64,512]{1,0:T(8,128)(2,1)S(1)}, bf16[32,512]{1,0:T(8,128)(2,1)S(1)}) custom-call(bf16[2,64,512]{2,1,0:T(8,128)(2,1)S(1)} %get-tuple-element.25.refs_0_.ends, bf16[6,64,512]{2,1,0:T(8,128)(2,1)S(1)} %get-tuple-element.29.refs_1_.inner, ...), custom_call_target="tpu_custom_call" | custom-call | tf_op jit(solution)/shard_map/rims/pallas_call | solution.py:544
  13.6 0.1 collective-permute-start.3
  13.7 2.5 %collective-permute-start.4 = (bf16[80,512]{1,0:T(8,128)(2,1)S(1)}, bf16[80,512]{1,0:T(8,128)(2,1)S(1)}, u32[]{:S(2)}, u32[]{:S(2)}) collective-permute-start(bf16[80,512]{1,0:T(8,128)(2,1)S(1)} %get-tuple-element.39), channel_id=1, source_target_pairs={{0,7},{1,2},{2,1},{3,4},{4,3},{5,6},{6,5},{7,0},{8,15},{9,10},{10,... | collective-permute-start | bytes 245768 | tf_op jit(solution)/shard_map/ppermute | solution.py:558
  16.2 0.0 collective-permute-start.8
  16.3 1.1 %collective-permute-start.6 = (bf16[64,512]{1,0:T(8,128)(2,1)S(1)}, bf16[64,512]{1,0:T(8,128)(2,1)S(1)}, u32[]{:S(2)}, u32[]{:S(2)}) collective-permute-start(bf16[64,512]{1,0:T(8,128)(2,1)S(1)} %get-tuple-element.41.refs_0_), channel_id=1, source_target_pairs={{4,0},{5,1},{6,2},{7,3},{0,4},{1,5},{2,6},{3,7},{12,8},{13,9},{14,... | collective-permute-start | bytes 196616 | tf_op jit(solution)/shard_map/ppermute | solution.py:562
  17.4 0.8 %taps.1 = (bf16[512,2048]{1,0:T(8,128)(2,1)S(1)}, bf16[512,2048]{1,0:T(8,128)(2,1)S(1)}) custom-call(bf16[2,64,512]{2,1,0:T(8,128)(2,1)S(1)} %get-tuple-element.25.refs_0_.ends, bf16[6,64,512]{2,1,0:T(8,128)(2,1)S(1)} %get-tuple-element.29.refs_1_.inner, bf16[88,512]{1,0:T(8,128)(2,1)S(1)} %collective-permute-done.refs_2_.refs_3_, ...), custom_call_target="tpu_custom_call" | custom-call | tf_op jit(solution)/shard_map/taps/pallas_call | solution.py:567
  18.1 0.0 collective-permute-done.3.near.refs_1_.refs_7_
  18.1 0.9 %centre.1.refs_6_ = f32[512,512]{1,0:T(8,128)S(1)} custom-call(bf16[2,64,512]{2,1,0:T(8,128)(2,1)S(1)} %get-tuple-element.25.refs_0_.ends, bf16[6,64,512]{2,1,0:T(8,128)(2,1)S(1)} %get-tuple-element.29.refs_1_.inner, bf16[32,512]{1,0:T(8,128)(2,1)S(1)} %get-tuple-element.37.half, bf16[112,512]{1,0:T(8,128)(2,1)S(1)} %collective-permute-done.3.near.refs_1_.refs_7_), custom_call_target="tpu_custom_call" | custom-call | tf_op jit(solution)/shard_map/centre/pallas_call | solution.py:576
  19.0 0.0 collective-permute-done.4.refs_2_.refs_8_
  19.0 0.5 %collective-permute-start.5 = (bf16[80,512]{1,0:T(8,128)(2,1)S(1)}, bf16[80,512]{1,0:T(8,128)(2,1)S(1)}, u32[]{:S(2)}, u32[]{:S(2)}) collective-permute-start(bf16[80,512]{1,0:T(8,128)(2,1)S(1)} %collective-permute-done.4.refs_2_.refs_8_), channel_id=1, source_target_pairs={{0,1},{1,0},{2,3},{3,2},{4,5},{5,4},{6,7},{7,6},{8,9},{9,8},{10,11... | collective-permute-start | bytes 245768 | tf_op jit(solution)/shard_map/ppermute | solution.py:555
  19.5 1.9 %collective-permute-done.8.refs_4_ = bf16[64,512]{1,0:T(8,128)(2,1)S(1)} collective-permute-done((bf16[64,512]{1,0:T(8,128)(2,1)S(1)}, bf16[64,512]{1,0:T(8,128)(2,1)S(1)}, u32[]{:S(2)}, u32[]{:S(2)}) %collective-permute-start.8) | collective-permute-done | bytes 65568 | tf_op jit(solution)/shard_map/ppermute | solution.py:562
  21.4 0.0 collective-permute-done.6.refs_3_
  21.4 0.0 collective-permute-start.7
  21.4 0.5 %collective-permute-start.9 = (bf16[64,512]{1,0:T(8,128)(2,1)S(1)}, bf16[64,512]{1,0:T(8,128)(2,1)S(1)}, u32[]{:S(2)}, u32[]{:S(2)}) collective-permute-start(bf16[64,512]{1,0:T(8,128)(2,1)S(1)} %collective-permute-done.8.refs_4_), channel_id=1, source_target_pairs={{0,1},{1,0},{2,3},{3,2},{4,5},{5,4},{6,7},{7,6},{8,9},{9,8},{10,11... | collective-permute-start | bytes 196616 | tf_op jit(solution)/shard_map/ppermute | solution.py:555
  21.9 0.0 copy-done
  21.9 0.8 %early.1.refs_13_ = bf16[2,2048,256]{2,1,0:T(8,128)(2,1)S(1)} custom-call(bf16[64,512]{1,0:T(8,128)(2,1)S(1)} %get-tuple-element.41.refs_0_, bf16[112,512]{1,0:T(8,128)(2,1)S(1)} %collective-permute-done.3.near.refs_1_.refs_7_, bf16[80,512]{1,0:T(8,128)(2,1)S(1)} %collective-permute-done.4.refs_2_.refs_8_, ...), custom_call_target="tpu_custom_call" | custom-call | tf_op jit(solution)/shard_map/early/pallas_call | solution.py:604
  22.7 0.0 collective-permute-done.7.refs_10_
  22.7 0.1 collective-permute-done.9.refs_11_
  22.8 0.0 collective-permute-done.5.refs_9_
  22.8 4.5 %final.1 = (bf16[512,16,128]{2,1,0:T(8,128)(2,1)}, bf16[2,2048,256]{2,1,0:T(8,128)(2,1)S(1)}) custom-call(bf16[2,64,512]{2,1,0:T(8,128)(2,1)S(1)} %get-tuple-element.25.refs_0_.ends, bf16[6,64,512]{2,1,0:T(8,128)(2,1)S(1)} %get-tuple-element.29.refs_1_.inner, f32[8,512,256]{2,1,0:T(8,128)S(1)} %get-tuple-element.30.refs_2_, ...), custom_call_target="tpu_custom_call", output_to_operand_aliasing={{1}: (13, {})} | custom-call | tf_op jit(solution)/shard_map/final/pallas_call | solution.py:614
Async XLA Ops:
  0.0 8.7 %copy-start.1 = (bf16[8,64,64]{2,1,0:T(8,128)(2,1)S(1)}, bf16[8,64,64]{2,1,0:T(8,128)(2,1)}, u32[]{:S(2)}) copy-start(bf16[8,64,64]{2,1,0:T(8,128)(2,1)} %weights.1) | copy-start | bytes 196612
  2.5 10.7 %collective-permute-start = (bf16[88,512]{1,0:T(8,128)(2,1)S(1)}, bf16[88,512]{1,0:T(8,128)(2,1)S(1)}, u32[]{:S(2)}, u32[]{:S(2)}) collective-permute-start(bf16[88,512]{1,0:T(8,128)(2,1)S(1)} %get-tuple-element.32), channel_id=1, source_target_pairs={{0,8},{8,16},{16,24},{24,0},{1,9},{9,17},{17,25},{25,1},{2,10},{10... | collective-permute-start | bytes 270344 | tf_op jit(solution)/shard_map/ppermute | solution.py:509
  5.6 7.6 %collective-permute-start.1 = (bf16[88,512]{1,0:T(8,128)(2,1)S(1)}, bf16[88,512]{1,0:T(8,128)(2,1)S(1)}, u32[]{:S(2)}, u32[]{:S(2)}) collective-permute-start(bf16[88,512]{1,0:T(8,128)(2,1)S(1)} %get-tuple-element.33), channel_id=1, source_target_pairs={{0,24},{8,0},{16,8},{24,16},{1,25},{9,1},{17,9},{25,17},{2,26},{10... | collective-permute-start | bytes 270344 | tf_op jit(solution)/shard_map/ppermute | solution.py:509
  7.7 5.5 %collective-permute-start.2 = (bf16[24,512]{1,0:T(8,128)(2,1)S(1)}, bf16[24,512]{1,0:T(8,128)(2,1)S(1)}, u32[]{:S(2)}, u32[]{:S(2)}) collective-permute-start(bf16[24,512]{1,0:T(8,128)(2,1)S(1)} %get-tuple-element.36.refs_2_), channel_id=1, source_target_pairs={{0,16},{8,24},{16,0},{24,8},{1,17},{9,25},{17,1},{25,9},{2,18},{10... | collective-permute-start | bytes 73736 | tf_op jit(solution)/shard_map/ppermute | solution.py:509
  11.3 10.7 %copy-start = (bf16[3,2,256,256]{3,2,1,0:T(8,128)(2,1)S(1)}, bf16[3,2,256,256]{3,2,1,0:T(8,128)(2,1)}, u32[]{:S(2)}) copy-start(bf16[3,2,256,256]{3,2,1,0:T(8,128)(2,1)} %constant.2.clone.refs_5_.refs_12_) | copy-start | bytes 2359300
  13.6 4.5 %collective-permute-start.3 = (bf16[112,512]{1,0:T(8,128)(2,1)S(1)}, bf16[112,512]{1,0:T(8,128)(2,1)S(1)}, u32[]{:S(2)}, u32[]{:S(2)}) collective-permute-start(bf16[112,512]{1,0:T(8,128)(2,1)S(1)} %get-tuple-element.38), channel_id=1, source_target_pairs={{0,1},{1,0},{2,3},{3,2},{4,5},{5,4},{6,7},{7,6},{8,9},{9,8},{10,11... | collective-permute-start | bytes 344072 | tf_op jit(solution)/shard_map/ppermute | solution.py:555
  13.7 5.3 %collective-permute-start.4 = (bf16[80,512]{1,0:T(8,128)(2,1)S(1)}, bf16[80,512]{1,0:T(8,128)(2,1)S(1)}, u32[]{:S(2)}, u32[]{:S(2)}) collective-permute-start(bf16[80,512]{1,0:T(8,128)(2,1)S(1)} %get-tuple-element.39), channel_id=1, source_target_pairs={{0,7},{1,2},{2,1},{3,4},{4,3},{5,6},{6,5},{7,0},{8,15},{9,10},{10,... | collective-permute-start | bytes 245768 | tf_op jit(solution)/shard_map/ppermute | solution.py:558
  16.2 5.2 %collective-permute-start.8 = (bf16[64,512]{1,0:T(8,128)(2,1)S(1)}, bf16[64,512]{1,0:T(8,128)(2,1)S(1)}, u32[]{:S(2)}, u32[]{:S(2)}) collective-permute-start(bf16[64,512]{1,0:T(8,128)(2,1)S(1)} %get-tuple-element.41.refs_0_), channel_id=1, source_target_pairs={{6,0},{3,1},{0,2},{5,3},{2,4},{7,5},{4,6},{1,7},{14,8},{11,9},{8,1... | collective-permute-start | bytes 196616 | tf_op jit(solution)/shard_map/ppermute | solution.py:562
  16.3 5.2 %collective-permute-start.6 = (bf16[64,512]{1,0:T(8,128)(2,1)S(1)}, bf16[64,512]{1,0:T(8,128)(2,1)S(1)}, u32[]{:S(2)}, u32[]{:S(2)}) collective-permute-start(bf16[64,512]{1,0:T(8,128)(2,1)S(1)} %get-tuple-element.41.refs_0_), channel_id=1, source_target_pairs={{4,0},{5,1},{6,2},{7,3},{0,4},{1,5},{2,6},{3,7},{12,8},{13,9},{14,... | collective-permute-start | bytes 196616 | tf_op jit(solution)/shard_map/ppermute | solution.py:562
  19.0 3.8 %collective-permute-start.5 = (bf16[80,512]{1,0:T(8,128)(2,1)S(1)}, bf16[80,512]{1,0:T(8,128)(2,1)S(1)}, u32[]{:S(2)}, u32[]{:S(2)}) collective-permute-start(bf16[80,512]{1,0:T(8,128)(2,1)S(1)} %collective-permute-done.4.refs_2_.refs_8_), channel_id=1, source_target_pairs={{0,1},{1,0},{2,3},{3,2},{4,5},{5,4},{6,7},{7,6},{8,9},{9,8},{10,11... | collective-permute-start | bytes 245768 | tf_op jit(solution)/shard_map/ppermute | solution.py:555
  21.4 1.3 %collective-permute-start.7 = (bf16[64,512]{1,0:T(8,128)(2,1)S(1)}, bf16[64,512]{1,0:T(8,128)(2,1)S(1)}, u32[]{:S(2)}, u32[]{:S(2)}) collective-permute-start(bf16[64,512]{1,0:T(8,128)(2,1)S(1)} %collective-permute-done.6.refs_3_), channel_id=1, source_target_pairs={{0,1},{1,0},{2,3},{3,2},{4,5},{5,4},{6,7},{7,6},{8,9},{9,8},{10,11... | collective-permute-start | bytes 196616 | tf_op jit(solution)/shard_map/ppermute | solution.py:555
  21.4 1.4 %collective-permute-start.9 = (bf16[64,512]{1,0:T(8,128)(2,1)S(1)}, bf16[64,512]{1,0:T(8,128)(2,1)S(1)}, u32[]{:S(2)}, u32[]{:S(2)}) collective-permute-start(bf16[64,512]{1,0:T(8,128)(2,1)S(1)} %collective-permute-done.8.refs_4_), channel_id=1, source_target_pairs={{0,1},{1,0},{2,3},{3,2},{4,5},{5,4},{6,7},{7,6},{8,9},{9,8},{10,11... | collective-permute-start | bytes 196616 | tf_op jit(solution)/shard_map/ppermute | solution.py:555

commit v5 on v4

--- a/solution.py
+++ b/solution.py
@@ -179,7 +179,8 @@
         target[64:88, :] = pay_own[...]
 
 
-def inner_kernel(wide, edges, mixes_in, weights, pooled, halves, mixes_out):
+def inner_kernel(wide, edges, mixes_in, weights, pooled, halves, mixes_out, order):
+    order[...] = order_table()
     table = spread_table()
     pool_t = pool_table()
     mixes = [mixes_in[group] for group in range(2)]
@@ -205,7 +206,8 @@
     rows_in, cols_in = shape
     ends, inner, own, above, below = refs[:5]
     others = refs[5 : 5 + rows - 3]
-    near, far, block, half, raw, parts = refs[2 + rows :]
+    order = refs[2 + rows]
+    near, far, block, half, raw, parts = refs[3 + rows :]
     row, col = lax.axis_index("row"), lax.axis_index("col")
 
     own_rows = 64 // rows
@@ -226,7 +228,7 @@
     for n, other in enumerate(others):
         put(other, 0, lax.rem(row + rows - 2 - n, rows))
     joined = jnp.concatenate([raw[r] for r in range(rows)], axis=1)
-    sorted_block = dot(joined, order_table()).astype(BF16)
+    sorted_block = dot(joined, order[...]).astype(BF16)
     block[...] = sorted_block
     lines = all_lines(ends, inner, above, below, row, rows)
     blank = jnp.zeros((6, 512), F32)
@@ -472,7 +474,7 @@
             out[n * size + m * 8 : n * size + m * 8 + 8] = piece.reshape(8, 16, 128)
         span = pl.ds(n * size, size)
         copies.append(pltpu.make_async_copy(out.at[span], decoded.at[span], sems.at[n]))
-        copies[-1].start()
+        copies[-1].start(priority=n % 2)
     for copy in copies:
         copy.wait()
 
@@ -532,24 +534,24 @@
 
     above, below = shift(pay_down, 1), shift(pay_up, -1)
     others = [shift(pay_own, step) for step in range(2, rows - 1)]
-    inner, halves, out_mixes = call(
+    inner, halves, out_mixes, order = call(
         inner_kernel,
         "inner",
         [VMEM] * 4,
-        (VMEM,) * 3,
-        (arr(6, 64, 512), arr(8, 512, 256, dtype=F32), arr(2, 256, 256)),
+        (VMEM,) * 4,
+        (arr(6, 64, 512), arr(8, 512, 256, dtype=F32), arr(2, 256, 256), arr(512, 512)),
         [],
         24,
     )(wide, edges, mixes, dec_mix)
     near_out, far_out, block, half = call(
         functools.partial(rims_kernel, rows=rows, shape=shape),
         "rims",
-        [VMEM] * (2 + rows),
+        [VMEM] * (3 + rows),
         (VMEM,) * 4,
         (arr(shape[0] + 48, 512), arr(shape[0] + 16, 512), arr(shape[0], 512), arr(32, 512)),
         [pltpu.VMEM((rows,) + shape, BF16), pltpu.VMEM((64, 256), F32)],
         16,
-    )(ends, inner, pay_own, above, below, *others)
+    )(ends, inner, pay_own, above, below, *others, order)
 
     def mates(array):
         return lax.ppermute(array, "col", [(i, i ^ 1) for i in range(cols)])

time: 27.4 us -> 27.3 us (level)
  transfers between devices with their start and end apart: 10 -> 10, of which waited for: 3 -> 3; matrix products, arithmetic and copies ran while one was open for 0% -> 0% of each run, Pallas kernels for 18% -> 19%
where the time goes in v5:
time: 27.3 us; the launch traced here: 27.1 us
  Pallas kernels  12.4 us (45%)
  starting transfers between devices  10.8 us (40%)
  waiting for transfers between devices  3.77 us (14%)
    ppermute x3, starting transfers between devices, shift(): lax.ppermute(array, 'row', [(i, (i + step) % rows) for i in range(rows)])  6.12 us
    pallas_call x1, Pallas kernels, per_device(): call(kernel, 'final', [VMEM] * len(operands), (HBM, VMEM), (result, arr(2...  4.45 us
    pallas_call x1, Pallas kernels, per_device(): call(inner_kernel, 'inner', [VMEM] * 4, (VMEM,) * 4, (arr(6, 64, 512), ar...  2.84 us
    ppermute x1, starting transfers between devices, per_device(): lax.ppermute(far_out, 'col', [(i, (i - 1 if i % 2 == 0 else i + 1) % cols...  2.54 us
    pallas_call x1, Pallas kernels, per_device(): call(functools.partial(edge_kernel, chunks=chunks), 'edges', [HBM] * 4, (...  2.52 us
    ppermute x2, waiting for transfers between devices, per_device(): lax.ppermute(block, 'col', [((i + (even, odd)[i % 2]) % cols, i) for i in...  1.91 us
    ppermute x3, waiting for transfers between devices, shift(): lax.ppermute(array, 'row', [(i, (i + step) % rows) for i in range(rows)])  1.74 us
    ppermute x2, starting transfers between devices, per_device(): lax.ppermute(block, 'col', [((i + (even, odd)[i % 2]) % cols, i) for i in...  1.1 us
  transfers between devices with their start and end apart: 10, of which 3 were waited for; matrix products, arithmetic and copies ran while one was open for 0% of the time, Pallas kernels for 19%

profile of v5, /device:TPU:0, one launch (start us, length us, event | category | flops | bytes accessed | tf_op | source)
XLA Modules:
  0.0 27.1 jit_solution(5766379971832956422)
XLA Ops:
  0.0 0.0 copy-start.1
  0.0 2.5 %edges.1 = (f32[8704,128]{1,0:T(8,128)S(1)}, bf16[2,512,256]{2,1,0:T(8,128)(2,1)S(1)}, bf16[2,64,512]{2,1,0:T(8,128)(2,1)S(1)}, bf16[88,512]{1,0:T(8,128)(2,1)S(...) custom-call(bf16[512,16,128]{2,1,0:T(8,128)(2,1)} %fields_in.1, ...), custom_call_target="tpu_custom_call" | custom-call | tf_op jit(solution)/shard_map/edges/pallas_call | solution.py:515
  2.5 3.1 %collective-permute-start = (bf16[88,512]{1,0:T(8,128)(2,1)S(1)}, bf16[88,512]{1,0:T(8,128)(2,1)S(1)}, u32[]{:S(2)}, u32[]{:S(2)}) collective-permute-start(bf16[88,512]{1,0:T(8,128)(2,1)S(1)} %get-tuple-element.33), channel_id=1, source_target_pairs={{0,8},{8,16},{16,24},{24,0},{1,9},{9,17},{17,25},{25,1},{2,10},{10... | collective-permute-start | bytes 270344 | tf_op jit(solution)/shard_map/ppermute | solution.py:511
  5.6 2.1 %collective-permute-start.1 = (bf16[88,512]{1,0:T(8,128)(2,1)S(1)}, bf16[88,512]{1,0:T(8,128)(2,1)S(1)}, u32[]{:S(2)}, u32[]{:S(2)}) collective-permute-start(bf16[88,512]{1,0:T(8,128)(2,1)S(1)} %get-tuple-element.34), channel_id=1, source_target_pairs={{0,24},{8,0},{16,8},{24,16},{1,25},{9,1},{17,9},{25,17},{2,26},{10... | collective-permute-start | bytes 270344 | tf_op jit(solution)/shard_map/ppermute | solution.py:511
  7.7 0.9 %collective-permute-start.2 = (bf16[24,512]{1,0:T(8,128)(2,1)S(1)}, bf16[24,512]{1,0:T(8,128)(2,1)S(1)}, u32[]{:S(2)}, u32[]{:S(2)}) collective-permute-start(bf16[24,512]{1,0:T(8,128)(2,1)S(1)} %get-tuple-element.37.refs_2_), channel_id=1, source_target_pairs={{0,16},{8,24},{16,0},{24,8},{1,17},{9,25},{17,1},{25,9},{2,18},{10... | collective-permute-start | bytes 73736 | tf_op jit(solution)/shard_map/ppermute | solution.py:511
  8.6 0.0 copy-done.1
  8.7 2.8 %inner.1 = (bf16[6,64,512]{2,1,0:T(8,128)(2,1)S(1)}, f32[8,512,256]{2,1,0:T(8,128)S(1)}, bf16[2,256,256]{2,1,0:T(8,128)(2,1)S(1)}, bf16[512,512]{1,0:T(8,128)(2,1)S(1)}) custom-call(f32[8704,128]{1,0:T(8,128)S(1)} %get-tuple-element.27.wide, bf16[2,512,256]{2,1,0:T(8,128)(2,1)S(1)} %get-tuple-element.28.edges, ...), custom_call_target="tpu_custom_call" | custom-call | tf_op jit(solution)/shard_map/inner/pallas_call | solution.py:537
  11.5 0.0 copy-start
  11.5 1.7 %collective-permute-done.2.refs_5_ = bf16[24,512]{1,0:T(8,128)(2,1)S(1)} collective-permute-done((bf16[24,512]{1,0:T(8,128)(2,1)S(1)}, bf16[24,512]{1,0:T(8,128)(2,1)S(1)}, u32[]{:S(2)}, u32[]{:S(2)}) %collective-permute-start.2) | collective-permute-done | bytes 24608 | tf_op jit(solution)/shard_map/ppermute | solution.py:511
  13.2 0.0 collective-permute-done.refs_2_.refs_3_
  13.2 0.0 collective-permute-done.1.refs_3_.refs_4_
  13.3 0.2 rims.1
  13.5 0.1 collective-permute-start.3
  13.6 2.5 %collective-permute-start.4 = (bf16[80,512]{1,0:T(8,128)(2,1)S(1)}, bf16[80,512]{1,0:T(8,128)(2,1)S(1)}, u32[]{:S(2)}, u32[]{:S(2)}) collective-permute-start(bf16[80,512]{1,0:T(8,128)(2,1)S(1)} %get-tuple-element.41), channel_id=1, source_target_pairs={{0,7},{1,2},{2,1},{3,4},{4,3},{5,6},{6,5},{7,0},{8,15},{9,10},{10,... | collective-permute-start | bytes 245768 | tf_op jit(solution)/shard_map/ppermute | solution.py:560
  16.1 0.0 collective-permute-start.8
  16.1 1.1 %collective-permute-start.6 = (bf16[64,512]{1,0:T(8,128)(2,1)S(1)}, bf16[64,512]{1,0:T(8,128)(2,1)S(1)}, u32[]{:S(2)}, u32[]{:S(2)}) collective-permute-start(bf16[64,512]{1,0:T(8,128)(2,1)S(1)} %get-tuple-element.43.refs_0_), channel_id=1, source_target_pairs={{4,0},{5,1},{6,2},{7,3},{0,4},{1,5},{2,6},{3,7},{12,8},{13,9},{14,... | collective-permute-start | bytes 196616 | tf_op jit(solution)/shard_map/ppermute | solution.py:564
  17.2 0.8 %taps.1 = (bf16[512,2048]{1,0:T(8,128)(2,1)S(1)}, bf16[512,2048]{1,0:T(8,128)(2,1)S(1)}) custom-call(bf16[2,64,512]{2,1,0:T(8,128)(2,1)S(1)} %get-tuple-element.26.refs_0_.ends, bf16[6,64,512]{2,1,0:T(8,128)(2,1)S(1)} %get-tuple-element.30.refs_1_.inner, bf16[88,512]{1,0:T(8,128)(2,1)S(1)} %collective-permute-done.refs_2_.refs_3_, ...), custom_call_target="tpu_custom_call" | custom-call | tf_op jit(solution)/shard_map/taps/pallas_call | solution.py:569
  18.0 0.0 collective-permute-done.3.near.refs_1_.refs_7_
  18.0 0.9 %centre.1.refs_6_ = f32[512,512]{1,0:T(8,128)S(1)} custom-call(bf16[2,64,512]{2,1,0:T(8,128)(2,1)S(1)} %get-tuple-element.26.refs_0_.ends, bf16[6,64,512]{2,1,0:T(8,128)(2,1)S(1)} %get-tuple-element.30.refs_1_.inner, bf16[32,512]{1,0:T(8,128)(2,1)S(1)} %get-tuple-element.39.half, bf16[112,512]{1,0:T(8,128)(2,1)S(1)} %collective-permute-done.3.near.refs_1_.refs_7_), custom_call_target="tpu_custom_call" | custom-call | tf_op jit(solution)/shard_map/centre/pallas_call | solution.py:578
  18.9 0.0 collective-permute-done.4.refs_2_.refs_8_
  18.9 0.5 %collective-permute-start.5 = (bf16[80,512]{1,0:T(8,128)(2,1)S(1)}, bf16[80,512]{1,0:T(8,128)(2,1)S(1)}, u32[]{:S(2)}, u32[]{:S(2)}) collective-permute-start(bf16[80,512]{1,0:T(8,128)(2,1)S(1)} %collective-permute-done.4.refs_2_.refs_8_), channel_id=1, source_target_pairs={{0,1},{1,0},{2,3},{3,2},{4,5},{5,4},{6,7},{7,6},{8,9},{9,8},{10,11... | collective-permute-start | bytes 245768 | tf_op jit(solution)/shard_map/ppermute | solution.py:557
  19.4 1.9 %collective-permute-done.8.refs_4_ = bf16[64,512]{1,0:T(8,128)(2,1)S(1)} collective-permute-done((bf16[64,512]{1,0:T(8,128)(2,1)S(1)}, bf16[64,512]{1,0:T(8,128)(2,1)S(1)}, u32[]{:S(2)}, u32[]{:S(2)}) %collective-permute-start.8) | collective-permute-done | bytes 65568 | tf_op jit(solution)/shard_map/ppermute | solution.py:564
  21.3 0.0 collective-permute-done.6.refs_3_
  21.3 0.0 collective-permute-start.7
  21.3 0.5 %collective-permute-start.9 = (bf16[64,512]{1,0:T(8,128)(2,1)S(1)}, bf16[64,512]{1,0:T(8,128)(2,1)S(1)}, u32[]{:S(2)}, u32[]{:S(2)}) collective-permute-start(bf16[64,512]{1,0:T(8,128)(2,1)S(1)} %collective-permute-done.8.refs_4_), channel_id=1, source_target_pairs={{0,1},{1,0},{2,3},{3,2},{4,5},{5,4},{6,7},{7,6},{8,9},{9,8},{10,11... | collective-permute-start | bytes 196616 | tf_op jit(solution)/shard_map/ppermute | solution.py:557
  21.8 0.0 copy-done
  21.8 0.8 %early.1.refs_13_ = bf16[2,2048,256]{2,1,0:T(8,128)(2,1)S(1)} custom-call(bf16[64,512]{1,0:T(8,128)(2,1)S(1)} %get-tuple-element.43.refs_0_, bf16[112,512]{1,0:T(8,128)(2,1)S(1)} %collective-permute-done.3.near.refs_1_.refs_7_, bf16[80,512]{1,0:T(8,128)(2,1)S(1)} %collective-permute-done.4.refs_2_.refs_8_, ...), custom_call_target="tpu_custom_call" | custom-call | tf_op jit(solution)/shard_map/early/pallas_call | solution.py:606
  22.6 0.0 collective-permute-done.7.refs_10_
  22.6 0.1 collective-permute-done.9.refs_11_
  22.7 0.0 collective-permute-done.5.refs_9_
  22.7 4.4 %final.1 = (bf16[512,16,128]{2,1,0:T(8,128)(2,1)}, bf16[2,2048,256]{2,1,0:T(8,128)(2,1)S(1)}) custom-call(bf16[2,64,512]{2,1,0:T(8,128)(2,1)S(1)} %get-tuple-element.26.refs_0_.ends, bf16[6,64,512]{2,1,0:T(8,128)(2,1)S(1)} %get-tuple-element.30.refs_1_.inner, f32[8,512,256]{2,1,0:T(8,128)S(1)} %get-tuple-element.31.refs_2_, ...), custom_call_target="tpu_custom_call", output_to_operand_aliasing={{1}: (13, {})} | custom-call | tf_op jit(solution)/shard_map/final/pallas_call | solution.py:616
Async XLA Ops:
  0.0 8.7 %copy-start.1 = (bf16[8,64,64]{2,1,0:T(8,128)(2,1)S(1)}, bf16[8,64,64]{2,1,0:T(8,128)(2,1)}, u32[]{:S(2)}) copy-start(bf16[8,64,64]{2,1,0:T(8,128)(2,1)} %weights.1) | copy-start | bytes 196612
  2.5 10.7 %collective-permute-start = (bf16[88,512]{1,0:T(8,128)(2,1)S(1)}, bf16[88,512]{1,0:T(8,128)(2,1)S(1)}, u32[]{:S(2)}, u32[]{:S(2)}) collective-permute-start(bf16[88,512]{1,0:T(8,128)(2,1)S(1)} %get-tuple-element.33), channel_id=1, source_target_pairs={{0,8},{8,16},{16,24},{24,0},{1,9},{9,17},{17,25},{25,1},{2,10},{10... | collective-permute-start | bytes 270344 | tf_op jit(solution)/shard_map/ppermute | solution.py:511
  5.6 7.6 %collective-permute-start.1 = (bf16[88,512]{1,0:T(8,128)(2,1)S(1)}, bf16[88,512]{1,0:T(8,128)(2,1)S(1)}, u32[]{:S(2)}, u32[]{:S(2)}) collective-permute-start(bf16[88,512]{1,0:T(8,128)(2,1)S(1)} %get-tuple-element.34), channel_id=1, source_target_pairs={{0,24},{8,0},{16,8},{24,16},{1,25},{9,1},{17,9},{25,17},{2,26},{10... | collective-permute-start | bytes 270344 | tf_op jit(solution)/shard_map/ppermute | solution.py:511
  7.7 5.5 %collective-permute-start.2 = (bf16[24,512]{1,0:T(8,128)(2,1)S(1)}, bf16[24,512]{1,0:T(8,128)(2,1)S(1)}, u32[]{:S(2)}, u32[]{:S(2)}) collective-permute-start(bf16[24,512]{1,0:T(8,128)(2,1)S(1)} %get-tuple-element.37.refs_2_), channel_id=1, source_target_pairs={{0,16},{8,24},{16,0},{24,8},{1,17},{9,25},{17,1},{25,9},{2,18},{10... | collective-permute-start | bytes 73736 | tf_op jit(solution)/shard_map/ppermute | solution.py:511
  11.5 10.3 %copy-start = (bf16[3,2,256,256]{3,2,1,0:T(8,128)(2,1)S(1)}, bf16[3,2,256,256]{3,2,1,0:T(8,128)(2,1)}, u32[]{:S(2)}) copy-start(bf16[3,2,256,256]{3,2,1,0:T(8,128)(2,1)} %constant.2.clone.refs_5_.refs_12_) | copy-start | bytes 2359300
  13.5 4.5 %collective-permute-start.3 = (bf16[112,512]{1,0:T(8,128)(2,1)S(1)}, bf16[112,512]{1,0:T(8,128)(2,1)S(1)}, u32[]{:S(2)}, u32[]{:S(2)}) collective-permute-start(bf16[112,512]{1,0:T(8,128)(2,1)S(1)} %get-tuple-element.40), channel_id=1, source_target_pairs={{0,1},{1,0},{2,3},{3,2},{4,5},{5,4},{6,7},{7,6},{8,9},{9,8},{10,11... | collective-permute-start | bytes 344072 | tf_op jit(solution)/shard_map/ppermute | solution.py:557
  13.6 5.3 %collective-permute-start.4 = (bf16[80,512]{1,0:T(8,128)(2,1)S(1)}, bf16[80,512]{1,0:T(8,128)(2,1)S(1)}, u32[]{:S(2)}, u32[]{:S(2)}) collective-permute-start(bf16[80,512]{1,0:T(8,128)(2,1)S(1)} %get-tuple-element.41), channel_id=1, source_target_pairs={{0,7},{1,2},{2,1},{3,4},{4,3},{5,6},{6,5},{7,0},{8,15},{9,10},{10,... | collective-permute-start | bytes 245768 | tf_op jit(solution)/shard_map/ppermute | solution.py:560
  16.1 5.2 %collective-permute-start.8 = (bf16[64,512]{1,0:T(8,128)(2,1)S(1)}, bf16[64,512]{1,0:T(8,128)(2,1)S(1)}, u32[]{:S(2)}, u32[]{:S(2)}) collective-permute-start(bf16[64,512]{1,0:T(8,128)(2,1)S(1)} %get-tuple-element.43.refs_0_), channel_id=1, source_target_pairs={{6,0},{3,1},{0,2},{5,3},{2,4},{7,5},{4,6},{1,7},{14,8},{11,9},{8,1... | collective-permute-start | bytes 196616 | tf_op jit(solution)/shard_map/ppermute | solution.py:564
  16.1 5.2 %collective-permute-start.6 = (bf16[64,512]{1,0:T(8,128)(2,1)S(1)}, bf16[64,512]{1,0:T(8,128)(2,1)S(1)}, u32[]{:S(2)}, u32[]{:S(2)}) collective-permute-start(bf16[64,512]{1,0:T(8,128)(2,1)S(1)} %get-tuple-element.43.refs_0_), channel_id=1, source_target_pairs={{4,0},{5,1},{6,2},{7,3},{0,4},{1,5},{2,6},{3,7},{12,8},{13,9},{14,... | collective-permute-start | bytes 196616 | tf_op jit(solution)/shard_map/ppermute | solution.py:564
  18.9 3.8 %collective-permute-start.5 = (bf16[80,512]{1,0:T(8,128)(2,1)S(1)}, bf16[80,512]{1,0:T(8,128)(2,1)S(1)}, u32[]{:S(2)}, u32[]{:S(2)}) collective-permute-start(bf16[80,512]{1,0:T(8,128)(2,1)S(1)} %collective-permute-done.4.refs_2_.refs_8_), channel_id=1, source_target_pairs={{0,1},{1,0},{2,3},{3,2},{4,5},{5,4},{6,7},{7,6},{8,9},{9,8},{10,11... | collective-permute-start | bytes 245768 | tf_op jit(solution)/shard_map/ppermute | solution.py:557
  21.3 1.3 %collective-permute-start.7 = (bf16[64,512]{1,0:T(8,128)(2,1)S(1)}, bf16[64,512]{1,0:T(8,128)(2,1)S(1)}, u32[]{:S(2)}, u32[]{:S(2)}) collective-permute-start(bf16[64,512]{1,0:T(8,128)(2,1)S(1)} %collective-permute-done.6.refs_3_), channel_id=1, source_target_pairs={{0,1},{1,0},{2,3},{3,2},{4,5},{5,4},{6,7},{7,6},{8,9},{9,8},{10,11... | collective-permute-start | bytes 196616 | tf_op jit(solution)/shard_map/ppermute | solution.py:557
  21.3 1.4 %collective-permute-start.9 = (bf16[64,512]{1,0:T(8,128)(2,1)S(1)}, bf16[64,512]{1,0:T(8,128)(2,1)S(1)}, u32[]{:S(2)}, u32[]{:S(2)}) collective-permute-start(bf16[64,512]{1,0:T(8,128)(2,1)S(1)} %collective-permute-done.8.refs_4_), channel_id=1, source_target_pairs={{0,1},{1,0},{2,3},{3,2},{4,5},{5,4},{6,7},{7,6},{8,9},{9,8},{10,11... | collective-permute-start | bytes 196616 | tf_op jit(solution)/shard_map/ppermute | solution.py:557

commit v6 on v5

--- a/solution.py
+++ b/solution.py
@@ -379,9 +379,10 @@
 
 
 def early_kernel(*refs, cols, rows_in):
-    blocks = refs[: 2 + cols // 2 - 1]
-    turns, middle, turned = refs[2 + cols // 2 - 1 :]
-    places, _ = block_places(lax.axis_index("col"), cols)
+    blocks = refs[: 2 + cols // 2]
+    turns, middle, turned = refs[2 + cols // 2 :]
+    first, second = block_places(lax.axis_index("col"), cols)
+    places = first + second[:1]
     turn_blocks([block[0:rows_in, :] for block in blocks], places, turns, turned, middle)
 
 
@@ -397,8 +398,8 @@
     if split:
         relayed, turns = refs[:relays], refs[relays]
         decoded, middle, turned, lows, wide, out, sems = refs[relays + 2 :]
-        late = [block[0:rows_in, :] for block in relayed]
-        places = second
+        late = [block[0:rows_in, :] for block in relayed[1:]]
+        places = second[1:]
     else:
         held, relayed, turns = refs[: relays], refs[relays : 2 * relays], refs[2 * relays]
         decoded, kt, middle, turned, lows, wide, out, sems = refs[2 * relays + 1 :]
@@ -606,12 +607,12 @@
     middle = call(
         functools.partial(early_kernel, cols=cols, rows_in=shape[0]),
         "early",
-        [VMEM] * (4 + len(near_pairs)),
+        [VMEM] * (5 + len(near_pairs)),
         VMEM,
         arr(2, 2048, 256),
         [pltpu.VMEM((2048, 128), F32)],
         24,
-    )(block, near, far, *near_pairs, turns)
+    )(block, near, far, *near_pairs, relayed[0], turns)
     operands += relayed + [turns, middle]
     return call(
         kernel, "final", [VMEM] * len(operands), (HBM, VMEM), (result, arr(2, 2048, 256)),

time: 27.3 us -> 27.2 us (level)
  transfers between devices with their start and end apart: 10 -> 10, of which waited for: 3 -> 2; matrix products, arithmetic and copies ran while one was open for 0% -> 0% of each run, Pallas kernels for 19% -> 20%
where the time goes in v6:
time: 27.2 us; the launch traced here: 27.1 us
  Pallas kernels  12.5 us (46%)
  starting transfers between devices  10.8 us (40%)
  waiting for transfers between devices  3.66 us (13%)
    ppermute x3, starting transfers between devices, shift(): lax.ppermute(array, 'row', [(i, (i + step) % rows) for i in range(rows)])  6.12 us
    pallas_call x1, Pallas kernels, per_device(): call(kernel, 'final', [VMEM] * len(operands), (HBM, VMEM), (result, arr(2...  4.3 us
    pallas_call x1, Pallas kernels, per_device(): call(inner_kernel, 'inner', [VMEM] * 4, (VMEM,) * 4, (arr(6, 64, 512), ar...  2.84 us
    ppermute x1, starting transfers between devices, per_device(): lax.ppermute(far_out, 'col', [(i, (i - 1 if i % 2 == 0 else i + 1) % cols...  2.54 us
    pallas_call x1, Pallas kernels, per_device(): call(functools.partial(edge_kernel, chunks=chunks), 'edges', [HBM] * 4, (...  2.52 us
    ppermute x2, waiting for transfers between devices, per_device(): lax.ppermute(block, 'col', [((i + (even, odd)[i % 2]) % cols, i) for i in...  1.91 us
    ppermute x3, waiting for transfers between devices, shift(): lax.ppermute(array, 'row', [(i, (i + step) % rows) for i in range(rows)])  1.74 us
    ppermute x2, starting transfers between devices, per_device(): lax.ppermute(block, 'col', [((i + (even, odd)[i % 2]) % cols, i) for i in...  1.1 us
  transfers between devices with their start and end apart: 10, of which 2 were waited for; matrix products, arithmetic and copies ran while one was open for 0% of the time, Pallas kernels for 20%

profile of v6, /device:TPU:0, one launch (start us, length us, event | category | flops | bytes accessed | tf_op | source)
XLA Modules:
  0.0 27.1 jit_solution(6355736037412601742)
XLA Ops:
  0.0 0.0 copy-start.1
  0.0 2.5 %edges.1 = (f32[8704,128]{1,0:T(8,128)S(1)}, bf16[2,512,256]{2,1,0:T(8,128)(2,1)S(1)}, bf16[2,64,512]{2,1,0:T(8,128)(2,1)S(1)}, bf16[88,512]{1,0:T(8,128)(2,1)S(...) custom-call(bf16[512,16,128]{2,1,0:T(8,128)(2,1)} %fields_in.1, ...), custom_call_target="tpu_custom_call" | custom-call | tf_op jit(solution)/shard_map/edges/pallas_call | solution.py:516
  2.5 3.1 %collective-permute-start = (bf16[88,512]{1,0:T(8,128)(2,1)S(1)}, bf16[88,512]{1,0:T(8,128)(2,1)S(1)}, u32[]{:S(2)}, u32[]{:S(2)}) collective-permute-start(bf16[88,512]{1,0:T(8,128)(2,1)S(1)} %get-tuple-element.33), channel_id=1, source_target_pairs={{0,8},{8,16},{16,24},{24,0},{1,9},{9,17},{17,25},{25,1},{2,10},{10... | collective-permute-start | bytes 270344 | tf_op jit(solution)/shard_map/ppermute | solution.py:512
  5.6 2.1 %collective-permute-start.1 = (bf16[88,512]{1,0:T(8,128)(2,1)S(1)}, bf16[88,512]{1,0:T(8,128)(2,1)S(1)}, u32[]{:S(2)}, u32[]{:S(2)}) collective-permute-start(bf16[88,512]{1,0:T(8,128)(2,1)S(1)} %get-tuple-element.34), channel_id=1, source_target_pairs={{0,24},{8,0},{16,8},{24,16},{1,25},{9,1},{17,9},{25,17},{2,26},{10... | collective-permute-start | bytes 270344 | tf_op jit(solution)/shard_map/ppermute | solution.py:512
  7.7 0.9 %collective-permute-start.2 = (bf16[24,512]{1,0:T(8,128)(2,1)S(1)}, bf16[24,512]{1,0:T(8,128)(2,1)S(1)}, u32[]{:S(2)}, u32[]{:S(2)}) collective-permute-start(bf16[24,512]{1,0:T(8,128)(2,1)S(1)} %get-tuple-element.37.refs_2_), channel_id=1, source_target_pairs={{0,16},{8,24},{16,0},{24,8},{1,17},{9,25},{17,1},{25,9},{2,18},{10... | collective-permute-start | bytes 73736 | tf_op jit(solution)/shard_map/ppermute | solution.py:512
  8.6 0.0 copy-done.1
  8.7 2.8 %inner.1 = (bf16[6,64,512]{2,1,0:T(8,128)(2,1)S(1)}, f32[8,512,256]{2,1,0:T(8,128)S(1)}, bf16[2,256,256]{2,1,0:T(8,128)(2,1)S(1)}, bf16[512,512]{1,0:T(8,128)(2,1)S(1)}) custom-call(f32[8704,128]{1,0:T(8,128)S(1)} %get-tuple-element.27.wide, bf16[2,512,256]{2,1,0:T(8,128)(2,1)S(1)} %get-tuple-element.28.edges, ...), custom_call_target="tpu_custom_call" | custom-call | tf_op jit(solution)/shard_map/inner/pallas_call | solution.py:538
  11.5 0.0 copy-start
  11.5 1.7 %collective-permute-done.2.refs_5_ = bf16[24,512]{1,0:T(8,128)(2,1)S(1)} collective-permute-done((bf16[24,512]{1,0:T(8,128)(2,1)S(1)}, bf16[24,512]{1,0:T(8,128)(2,1)S(1)}, u32[]{:S(2)}, u32[]{:S(2)}) %collective-permute-start.2) | collective-permute-done | bytes 24608 | tf_op jit(solution)/shard_map/ppermute | solution.py:512
  13.2 0.0 collective-permute-done.refs_2_.refs_3_
  13.2 0.0 collective-permute-done.1.refs_3_.refs_4_
  13.3 0.2 rims.1
  13.5 0.1 collective-permute-start.3
  13.6 2.5 %collective-permute-start.4 = (bf16[80,512]{1,0:T(8,128)(2,1)S(1)}, bf16[80,512]{1,0:T(8,128)(2,1)S(1)}, u32[]{:S(2)}, u32[]{:S(2)}) collective-permute-start(bf16[80,512]{1,0:T(8,128)(2,1)S(1)} %get-tuple-element.41), channel_id=1, source_target_pairs={{0,7},{1,2},{2,1},{3,4},{4,3},{5,6},{6,5},{7,0},{8,15},{9,10},{10,... | collective-permute-start | bytes 245768 | tf_op jit(solution)/shard_map/ppermute | solution.py:561
  16.1 0.0 collective-permute-start.8
  16.1 1.1 %collective-permute-start.6 = (bf16[64,512]{1,0:T(8,128)(2,1)S(1)}, bf16[64,512]{1,0:T(8,128)(2,1)S(1)}, u32[]{:S(2)}, u32[]{:S(2)}) collective-permute-start(bf16[64,512]{1,0:T(8,128)(2,1)S(1)} %get-tuple-element.43.refs_0_), channel_id=1, source_target_pairs={{4,0},{5,1},{6,2},{7,3},{0,4},{1,5},{2,6},{3,7},{12,8},{13,9},{14,... | collective-permute-start | bytes 196616 | tf_op jit(solution)/shard_map/ppermute | solution.py:565
  17.2 0.8 %taps.1 = (bf16[512,2048]{1,0:T(8,128)(2,1)S(1)}, bf16[512,2048]{1,0:T(8,128)(2,1)S(1)}) custom-call(bf16[2,64,512]{2,1,0:T(8,128)(2,1)S(1)} %get-tuple-element.26.refs_0_.ends, bf16[6,64,512]{2,1,0:T(8,128)(2,1)S(1)} %get-tuple-element.30.refs_1_.inner, bf16[88,512]{1,0:T(8,128)(2,1)S(1)} %collective-permute-done.refs_2_.refs_3_, ...), custom_call_target="tpu_custom_call" | custom-call | tf_op jit(solution)/shard_map/taps/pallas_call | solution.py:570
  18.0 0.0 collective-permute-done.3.near.refs_1_.refs_7_
  18.0 0.9 %centre.1.refs_6_ = f32[512,512]{1,0:T(8,128)S(1)} custom-call(bf16[2,64,512]{2,1,0:T(8,128)(2,1)S(1)} %get-tuple-element.26.refs_0_.ends, bf16[6,64,512]{2,1,0:T(8,128)(2,1)S(1)} %get-tuple-element.30.refs_1_.inner, bf16[32,512]{1,0:T(8,128)(2,1)S(1)} %get-tuple-element.39.half, bf16[112,512]{1,0:T(8,128)(2,1)S(1)} %collective-permute-done.3.near.refs_1_.refs_7_), custom_call_target="tpu_custom_call" | custom-call | tf_op jit(solution)/shard_map/centre/pallas_call | solution.py:579
  18.9 0.0 collective-permute-done.4.refs_2_.refs_8_
  18.9 0.5 %collective-permute-start.5 = (bf16[80,512]{1,0:T(8,128)(2,1)S(1)}, bf16[80,512]{1,0:T(8,128)(2,1)S(1)}, u32[]{:S(2)}, u32[]{:S(2)}) collective-permute-start(bf16[80,512]{1,0:T(8,128)(2,1)S(1)} %collective-permute-done.4.refs_2_.refs_8_), channel_id=1, source_target_pairs={{0,1},{1,0},{2,3},{3,2},{4,5},{5,4},{6,7},{7,6},{8,9},{9,8},{10,11... | collective-permute-start | bytes 245768 | tf_op jit(solution)/shard_map/ppermute | solution.py:558
  19.4 1.9 %collective-permute-done.8.refs_4_ = bf16[64,512]{1,0:T(8,128)(2,1)S(1)} collective-permute-done((bf16[64,512]{1,0:T(8,128)(2,1)S(1)}, bf16[64,512]{1,0:T(8,128)(2,1)S(1)}, u32[]{:S(2)}, u32[]{:S(2)}) %collective-permute-start.8) | collective-permute-done | bytes 65568 | tf_op jit(solution)/shard_map/ppermute | solution.py:565
  21.3 0.0 collective-permute-done.6.refs_3_
  21.3 0.0 collective-permute-start.7
  21.3 0.5 %collective-permute-start.9 = (bf16[64,512]{1,0:T(8,128)(2,1)S(1)}, bf16[64,512]{1,0:T(8,128)(2,1)S(1)}, u32[]{:S(2)}, u32[]{:S(2)}) collective-permute-start(bf16[64,512]{1,0:T(8,128)(2,1)S(1)} %collective-permute-done.8.refs_4_), channel_id=1, source_target_pairs={{0,1},{1,0},{2,3},{3,2},{4,5},{5,4},{6,7},{7,6},{8,9},{9,8},{10,11... | collective-permute-start | bytes 196616 | tf_op jit(solution)/shard_map/ppermute | solution.py:558
  21.8 0.0 collective-permute-done.5.refs_5_.refs_9_
  21.8 0.0 copy-done
  21.8 0.9 %early.1.refs_13_ = bf16[2,2048,256]{2,1,0:T(8,128)(2,1)S(1)} custom-call(bf16[64,512]{1,0:T(8,128)(2,1)S(1)} %get-tuple-element.43.refs_0_, bf16[112,512]{1,0:T(8,128)(2,1)S(1)} %collective-permute-done.3.near.refs_1_.refs_7_, bf16[80,512]{1,0:T(8,128)(2,1)S(1)} %collective-permute-done.4.refs_2_.refs_8_, ...), custom_call_target="tpu_custom_call" | custom-call | tf_op jit(solution)/shard_map/early/pallas_call | solution.py:607
  22.7 0.0 collective-permute-done.7.refs_10_
  22.8 0.0 collective-permute-done.9.refs_11_
  22.8 4.3 %final.1 = (bf16[512,16,128]{2,1,0:T(8,128)(2,1)}, bf16[2,2048,256]{2,1,0:T(8,128)(2,1)S(1)}) custom-call(bf16[2,64,512]{2,1,0:T(8,128)(2,1)S(1)} %get-tuple-element.26.refs_0_.ends, bf16[6,64,512]{2,1,0:T(8,128)(2,1)S(1)} %get-tuple-element.30.refs_1_.inner, f32[8,512,256]{2,1,0:T(8,128)S(1)} %get-tuple-element.31.refs_2_, ...), custom_call_target="tpu_custom_call", output_to_operand_aliasing={{1}: (13, {})} | custom-call | tf_op jit(solution)/shard_map/final/pallas_call | solution.py:617
Async XLA Ops:
  0.0 8.7 %copy-start.1 = (bf16[8,64,64]{2,1,0:T(8,128)(2,1)S(1)}, bf16[8,64,64]{2,1,0:T(8,128)(2,1)}, u32[]{:S(2)}) copy-start(bf16[8,64,64]{2,1,0:T(8,128)(2,1)} %weights.1) | copy-start | bytes 196612
  2.5 10.7 %collective-permute-start = (bf16[88,512]{1,0:T(8,128)(2,1)S(1)}, bf16[88,512]{1,0:T(8,128)(2,1)S(1)}, u32[]{:S(2)}, u32[]{:S(2)}) collective-permute-start(bf16[88,512]{1,0:T(8,128)(2,1)S(1)} %get-tuple-element.33), channel_id=1, source_target_pairs={{0,8},{8,16},{16,24},{24,0},{1,9},{9,17},{17,25},{25,1},{2,10},{10... | collective-permute-start | bytes 270344 | tf_op jit(solution)/shard_map/ppermute | solution.py:512
  5.6 7.6 %collective-permute-start.1 = (bf16[88,512]{1,0:T(8,128)(2,1)S(1)}, bf16[88,512]{1,0:T(8,128)(2,1)S(1)}, u32[]{:S(2)}, u32[]{:S(2)}) collective-permute-start(bf16[88,512]{1,0:T(8,128)(2,1)S(1)} %get-tuple-element.34), channel_id=1, source_target_pairs={{0,24},{8,0},{16,8},{24,16},{1,25},{9,1},{17,9},{25,17},{2,26},{10... | collective-permute-start | bytes 270344 | tf_op jit(solution)/shard_map/ppermute | solution.py:512
  7.7 5.5 %collective-permute-start.2 = (bf16[24,512]{1,0:T(8,128)(2,1)S(1)}, bf16[24,512]{1,0:T(8,128)(2,1)S(1)}, u32[]{:S(2)}, u32[]{:S(2)}) collective-permute-start(bf16[24,512]{1,0:T(8,128)(2,1)S(1)} %get-tuple-element.37.refs_2_), channel_id=1, source_target_pairs={{0,16},{8,24},{16,0},{24,8},{1,17},{9,25},{17,1},{25,9},{2,18},{10... | collective-permute-start | bytes 73736 | tf_op jit(solution)/shard_map/ppermute | solution.py:512
  11.5 10.3 %copy-start = (bf16[3,2,256,256]{3,2,1,0:T(8,128)(2,1)S(1)}, bf16[3,2,256,256]{3,2,1,0:T(8,128)(2,1)}, u32[]{:S(2)}) copy-start(bf16[3,2,256,256]{3,2,1,0:T(8,128)(2,1)} %constant.2.clone.refs_6_.refs_12_) | copy-start | bytes 2359300
  13.5 4.5 %collective-permute-start.3 = (bf16[112,512]{1,0:T(8,128)(2,1)S(1)}, bf16[112,512]{1,0:T(8,128)(2,1)S(1)}, u32[]{:S(2)}, u32[]{:S(2)}) collective-permute-start(bf16[112,512]{1,0:T(8,128)(2,1)S(1)} %get-tuple-element.40), channel_id=1, source_target_pairs={{0,1},{1,0},{2,3},{3,2},{4,5},{5,4},{6,7},{7,6},{8,9},{9,8},{10,11... | collective-permute-start | bytes 344072 | tf_op jit(solution)/shard_map/ppermute | solution.py:558
  13.6 5.3 %collective-permute-start.4 = (bf16[80,512]{1,0:T(8,128)(2,1)S(1)}, bf16[80,512]{1,0:T(8,128)(2,1)S(1)}, u32[]{:S(2)}, u32[]{:S(2)}) collective-permute-start(bf16[80,512]{1,0:T(8,128)(2,1)S(1)} %get-tuple-element.41), channel_id=1, source_target_pairs={{0,7},{1,2},{2,1},{3,4},{4,3},{5,6},{6,5},{7,0},{8,15},{9,10},{10,... | collective-permute-start | bytes 245768 | tf_op jit(solution)/shard_map/ppermute | solution.py:561
  16.1 5.2 %collective-permute-start.8 = (bf16[64,512]{1,0:T(8,128)(2,1)S(1)}, bf16[64,512]{1,0:T(8,128)(2,1)S(1)}, u32[]{:S(2)}, u32[]{:S(2)}) collective-permute-start(bf16[64,512]{1,0:T(8,128)(2,1)S(1)} %get-tuple-element.43.refs_0_), channel_id=1, source_target_pairs={{6,0},{3,1},{0,2},{5,3},{2,4},{7,5},{4,6},{1,7},{14,8},{11,9},{8,1... | collective-permute-start | bytes 196616 | tf_op jit(solution)/shard_map/ppermute | solution.py:565
  16.1 5.2 %collective-permute-start.6 = (bf16[64,512]{1,0:T(8,128)(2,1)S(1)}, bf16[64,512]{1,0:T(8,128)(2,1)S(1)}, u32[]{:S(2)}, u32[]{:S(2)}) collective-permute-start(bf16[64,512]{1,0:T(8,128)(2,1)S(1)} %get-tuple-element.43.refs_0_), channel_id=1, source_target_pairs={{4,0},{5,1},{6,2},{7,3},{0,4},{1,5},{2,6},{3,7},{12,8},{13,9},{14,... | collective-permute-start | bytes 196616 | tf_op jit(solution)/shard_map/ppermute | solution.py:565
  18.9 2.9 %collective-permute-start.5 = (bf16[80,512]{1,0:T(8,128)(2,1)S(1)}, bf16[80,512]{1,0:T(8,128)(2,1)S(1)}, u32[]{:S(2)}, u32[]{:S(2)}) collective-permute-start(bf16[80,512]{1,0:T(8,128)(2,1)S(1)} %collective-permute-done.4.refs_2_.refs_8_), channel_id=1, source_target_pairs={{0,1},{1,0},{2,3},{3,2},{4,5},{5,4},{6,7},{7,6},{8,9},{9,8},{10,11... | collective-permute-start | bytes 245768 | tf_op jit(solution)/shard_map/ppermute | solution.py:558
  21.3 1.5 %collective-permute-start.7 = (bf16[64,512]{1,0:T(8,128)(2,1)S(1)}, bf16[64,512]{1,0:T(8,128)(2,1)S(1)}, u32[]{:S(2)}, u32[]{:S(2)}) collective-permute-start(bf16[64,512]{1,0:T(8,128)(2,1)S(1)} %collective-permute-done.6.refs_3_), channel_id=1, source_target_pairs={{0,1},{1,0},{2,3},{3,2},{4,5},{5,4},{6,7},{7,6},{8,9},{9,8},{10,11... | collective-permute-start | bytes 196616 | tf_op jit(solution)/shard_map/ppermute | solution.py:558
  21.3 1.5 %collective-permute-start.9 = (bf16[64,512]{1,0:T(8,128)(2,1)S(1)}, bf16[64,512]{1,0:T(8,128)(2,1)S(1)}, u32[]{:S(2)}, u32[]{:S(2)}) collective-permute-start(bf16[64,512]{1,0:T(8,128)(2,1)S(1)} %collective-permute-done.8.refs_4_), channel_id=1, source_target_pairs={{0,1},{1,0},{2,3},{3,2},{4,5},{5,4},{6,7},{7,6},{8,9},{9,8},{10,11... | collective-permute-start | bytes 196616 | tf_op jit(solution)/shard_map/ppermute | solution.py:558
